TPU v7x, 32 devices: a whole 2x2x4 slice. The times are simulated.
32 devices in a mesh: pool: 1, fsdp: 32 (over z, y, x, core).
Axes of the slice: x: 2, y: 2, z: 4, core: 2. Of those that a mesh axis runs over, the one named last changes fastest.
Arguments:
- noisy: bfloat16 [2048, 2560], P(('pool', 'fsdp')), may hold values from -6 to 6
- clean: bfloat16 [2048, 2560], P(('pool', 'fsdp')), may hold values from -6 to 6
- seg_ids: int32 [32], P('pool'), may hold values from 0 to 3, never falling along the last dimension, each value on 1 to 12 neighbouring positions
- lag_mask: int32 [32, 2], P(('pool', 'fsdp')), may hold values 0 or 1
- plan: int32 [32, 2], P(('pool', 'fsdp')), may hold values from 1 to 999, as said below
- w_query: bfloat16 [2560, 2560], P('fsdp'), may hold values from -0.125 to 0.125
- w_key: bfloat16 [2560, 2560], P('fsdp'), may hold values from -0.125 to 0.125
- time_proj: bfloat16 [128, 7680], replicated, may hold values from -0.5 to 0.5
- q_gain: float32 [2560], replicated, may hold values from 0.5 to 14
- k_gain: float32 [2560], replicated, may hold values from 0.5 to 14
Outputs:
- denoised: bfloat16 [2048, 2560], P(('pool', 'fsdp'))
Inputs may be any that keep to these rules, and one draw needn't show every extreme that they name: seg_ids never falls along the spans; each rollout is 1 to 12 consecutive spans. `plan`: entry j of a row lies from 1000 * (1 - j) // 2 + 1 to 1000 * (2 - j) // 2 - 1, so each row falls strictly.
All inputs are finite; a program needn't handle non-finite values. No bound on the sum of `lag_mask` on one device may be relied on, other than what follows from the above.
Results may differ from a plain program's by a relative error of at most 0.024.
Values may be sent and summed in bfloat16 or wider, within the bound.
No kernel may reach another device: no remote copies, remote signals or barrier semaphores. Data moves between devices by JAX's collectives and lax.ppermute only.
A program may use at most 128 MiB of HBM per device.

v0:
```python
import math

import jax
import jax.numpy as jnp
from jax import lax
from jax.sharding import PartitionSpec as P

HEADS = 20
HEAD_DIM = 128
STEPS = 2
LAGS = 2
LEVELS = 1000


SIGMA_SHIFT = 5.0
EPSILON = 1e-06
MASKED = -1e30


def passed_along(value, axis, steps):
    count = lax.axis_size(axis)
    leading, last = (max(0, -steps), min(count, count - steps))
    return lax.ppermute(value, axis, [(source, source + steps) for source in range(leading, last)])


def sigma_of(levels):
    fraction = levels.astype(jnp.float32) / LEVELS
    return SIGMA_SHIFT * fraction / (1.0 + (SIGMA_SHIFT - 1.0) * fraction)


def frequencies(half_count):
    return jnp.exp(-math.log(10000.0) * jnp.arange(half_count, dtype=jnp.float32) / half_count)


def modulation(sigmas, time_proj):
    half_count = time_proj.shape[0] // 2
    angles = 1000.0 * sigmas[:, None] * frequencies(half_count)[None, :]
    features = jnp.concatenate([jnp.cos(angles), jnp.sin(angles)], axis=1).astype(jnp.bfloat16)
    return jnp.dot(features, time_proj, preferred_element_type=jnp.float32)[0]


def modulate(latent, mod_row, model_width):
    values = latent.astype(jnp.float32)
    centred = values - jnp.mean(values, axis=-1, keepdims=True)
    variance = jnp.mean(centred * centred, axis=-1, keepdims=True)
    normed = centred * lax.rsqrt(variance + EPSILON)
    return (normed * (1.0 + mod_row[model_width : 2 * model_width]) + mod_row[:model_width]).astype(
        jnp.bfloat16
    )


def normalize(values, gain):
    mean_square = jnp.mean(values * values, axis=-1, keepdims=True)
    return values * lax.rsqrt(mean_square + EPSILON) * gain


def rotate(values, positions):
    half_count = HEAD_DIM // 2
    split_heads = values.reshape(values.shape[:-1] + (HEADS, HEAD_DIM))
    angles = positions[..., None] * frequencies(half_count)
    cosine = jnp.cos(angles)[..., None, :]
    sine = jnp.sin(angles)[..., None, :]
    front = split_heads[..., :half_count]
    back = split_heads[..., half_count:]
    turned = jnp.concatenate([front * cosine - back * sine, front * sine + back * cosine], axis=-1)
    return turned.reshape(values.shape)


def attend(query_rows, key_rows, value_rows, usable):
    row_count = query_rows.shape[0]
    query_heads = query_rows.reshape(row_count, HEADS, HEAD_DIM)
    key_heads = key_rows.reshape(-1, HEADS, HEAD_DIM)
    value_heads = value_rows.reshape(-1, HEADS, HEAD_DIM)
    scores = jnp.einsum(
        "qhd,khd->hqk", query_heads, key_heads, preferred_element_type=jnp.float32
    ) * HEAD_DIM ** (-0.5)
    scores = jnp.where(usable[None, None, :], scores, MASKED)
    highest = jnp.max(scores, axis=-1, keepdims=True)
    expanded = jnp.exp(scores - highest)
    weights = (expanded / jnp.sum(expanded, axis=-1, keepdims=True)).astype(jnp.bfloat16)
    mixed = jnp.einsum("hqk,khd->qhd", weights, value_heads, preferred_element_type=jnp.float32)
    return mixed.reshape(row_count, HEADS * HEAD_DIM).astype(jnp.bfloat16)


def make_absorbers(noisy_hidden, context_hidden):

    def absorb_both(carry, pieces, offset):
        stored = tuple((piece_rows for piece_rows in pieces))
        query_sum = jnp.dot(noisy_hidden, pieces[0], preferred_element_type=jnp.float32)
        key_sum = jnp.dot(noisy_hidden, pieces[1], preferred_element_type=jnp.float32)
        ctxkey_sum = jnp.dot(context_hidden, pieces[1], preferred_element_type=jnp.float32)
        return (stored, (query_sum, key_sum, ctxkey_sum))

    def absorb_key(carry, piece, offset):
        buffer_rows, partials = carry
        stored = lax.dynamic_update_slice_in_dim(buffer_rows, piece, offset, 0)
        key_sum, ctxkey_sum = partials
        key_sum = key_sum + jnp.dot(noisy_hidden, piece, preferred_element_type=jnp.float32)
        ctxkey_sum = ctxkey_sum + jnp.dot(context_hidden, piece, preferred_element_type=jnp.float32)
        return (stored, (key_sum, ctxkey_sum))

    def absorb_query(carry, piece, offset):
        buffer_rows, query_sum = carry
        stored = lax.dynamic_update_slice_in_dim(buffer_rows, piece, offset, 0)
        query_sum = query_sum + jnp.dot(noisy_hidden, piece, preferred_element_type=jnp.float32)
        return (stored, query_sum)

    return (absorb_both, absorb_key, absorb_query)


def local(noisy, clean, seg_ids, lag_mask, plan, w_query, w_key, time_proj, q_gain, k_gain):
    row_count, model_width = noisy.shape
    inner_width = w_query.shape[1]
    span_index = lax.axis_index("fsdp")
    segment_start = jnp.sum((seg_ids < seg_ids[span_index]).astype(jnp.int32))
    span_place = span_index - segment_start
    positions = (span_place * row_count + jnp.arange(row_count, dtype=jnp.int32)).astype(
        jnp.float32
    )
    sigmas = [sigma_of(plan[0, level_index : level_index + 1]) for level_index in range(STEPS)] + [
        jnp.zeros((1,), jnp.float32)
    ]
    rest_mod = modulation(jnp.zeros((1,), jnp.float32), time_proj)
    step_mods = [modulation(sigmas[level_index], time_proj) for level_index in range(STEPS)]
    context_hidden = modulate(clean, rest_mod, model_width)
    noisy_hidden = modulate(noisy, step_mods[0], model_width)
    absorb_both, absorb_key, absorb_query = make_absorbers(noisy_hidden, context_hidden)
    empty_buffer = jnp.zeros((model_width, inner_width), jnp.bfloat16)
    empty_sum = jnp.zeros((row_count, inner_width), jnp.float32)
    buffers, partials = absorb_both(
        ((empty_buffer, empty_buffer), (empty_sum, empty_sum, empty_sum)),
        (
            lax.all_gather(w_query, "fsdp", axis=0, tiled=True),
            lax.all_gather(w_key, "fsdp", axis=0, tiled=True),
        ),
        jnp.int32(0),
    )
    full_query, full_key = buffers
    query_sum, key_sum, ctxkey_sum = partials
    context_key = rotate(normalize(ctxkey_sum, k_gain), positions).astype(jnp.bfloat16)
    context_pair = jnp.stack([context_key, context_hidden])
    received = [passed_along(context_pair, "fsdp", 1)]
    distance = 2
    received.append(passed_along(context_pair, "fsdp", distance))
    usable_parts = [jnp.ones((row_count,), jnp.int32) > 0]
    for distance in range(1, LAGS + 1):
        source = jnp.maximum(span_index - distance, 0)
        allowed = (
            (span_index >= distance)
            & (seg_ids[source] == seg_ids[span_index])
            & (lag_mask[0, distance - 1] == 1)
        )
        usable_parts.append(jnp.broadcast_to(allowed, (row_count,)))
    usable = jnp.concatenate(usable_parts)
    keys_context = jnp.concatenate([pair_rows[0] for pair_rows in received], axis=0)
    values_context = jnp.concatenate([pair_rows[1] for pair_rows in received], axis=0)
    latent = noisy
    for step_index in range(STEPS):
        if step_index == 0:
            hidden = noisy_hidden
            query_raw, key_raw = (query_sum, key_sum)
        else:
            hidden = modulate(latent, step_mods[step_index], model_width)
            query_raw = jnp.dot(hidden, full_query, preferred_element_type=jnp.float32)
            key_raw = jnp.dot(hidden, full_key, preferred_element_type=jnp.float32)
        query_rows = rotate(normalize(query_raw, q_gain), positions).astype(jnp.bfloat16)
        key_rows = rotate(normalize(key_raw, k_gain), positions).astype(jnp.bfloat16)
        mixed = attend(
            query_rows,
            jnp.concatenate([key_rows, keys_context], axis=0),
            jnp.concatenate([hidden, values_context], axis=0),
            usable,
        )
        sigma_change = sigmas[step_index + 1] - sigmas[step_index]
        factor = sigma_change * step_mods[step_index][2 * model_width :]
        latent = (latent.astype(jnp.float32) + factor[None, :] * mixed.astype(jnp.float32)).astype(
            jnp.bfloat16
        )
    return latent


def solution(mesh):
    placed = (
        P(("pool", "fsdp"), None),
        P(("pool", "fsdp"), None),
        P("pool"),
        P(("pool", "fsdp"), None),
        P(("pool", "fsdp"), None),
        P("fsdp", None),
        P("fsdp", None),
        P(),
        P(),
        P(),
    )
    return jax.shard_map(
        local, mesh=mesh, in_specs=placed, out_specs=P(("pool", "fsdp"), None), check_vma=False
    )
```

profile of v0, /device:TPU:0, one launch (start us, length us, event | category | flops | bytes accessed | tf_op | source)
XLA Modules:
  0.0 295.1 jit_solution(1294598367972171601)
XLA Ops:
  6.5 0.7 all-gather.3.cloned.1.call-update
  7.3 0.7 all-gather.5.cloned.1.call-update
  8.0 1.3 fusion.99
  10.8 1.4 fusion.101
  12.2 2.0 fusion.50
  17.5 1.4 fusion.100
  20.3 0.6 pad_add_fusion
  21.0 1.1 convert_reduce_fusion.1
  22.2 1.1 convert_reduce_fusion.2
  23.3 1.2 fusion.30
  24.6 0.3 fusion.34
  24.8 0.4 convolution_reduce_fusion.2
  25.3 0.4 convolution_reduce_fusion.1
  26.0 1.0 fusion.78
  26.9 83.7 %all-gather.3.cloned.1.call-done = bf16[2560,2560]{1,0:T(8,128)(2,1)} async-done(((bf16[80,2560]{1,0:T(8,128)(2,1)}), bf16[2560,2560]{1,0:T(8,128)(2,1)}) %all-gather.3.cloned.1.call-update) | async-done | bytes 13107216 | tf_op jit(solution)/shard_map/all_gather | solution.py:134
  110.7 7.4 %multiply_reduce_fusion.2 = (f32[64]{0:T(128)S(1)}, f32[64,2560]{1,0:T(8,128)S(1)}) fusion(bf16[2560,2560]{1,0:T(8,128)(2,1)} %all-gather.3.cloned.1.call-done, bf16[64,2560]{1,0:T(8,128)(2,1)S(1)} %copy-done.2, f32[2560]{0:T(1024)S(1)} %get-tuple-element.41, f32[2560]{0:T(1024)S(1)} %get-tuple-element.42, f32[64]{0:T(128)S(1)} %add_rsqrt_fusion.7, ...), kind=kOutput, calls=%fused_computation.79 | convolution fusion | flops 840171456 | bytes 14111488 | tf_op jit(solution)/shard_map/dot_general | solution.py:90
  118.1 1.0 copy-done.1
  119.1 2.5 multiply_reduce_fusion.4
  121.7 1.0 multiply_multiply_fusion.2
  122.6 1.0 reshape.305
  123.6 1.2 reshape.303
  124.8 2.8 fusion.95
  127.6 1.4 fusion.96
  129.0 80.8 %all-gather.5.cloned.1.call-done = bf16[2560,2560]{1,0:T(8,128)(2,1)} async-done(((bf16[80,2560]{1,0:T(8,128)(2,1)}), bf16[2560,2560]{1,0:T(8,128)(2,1)}) %all-gather.5.cloned.1.call-update) | async-done | bytes 13107216 | tf_op jit(solution)/shard_map/all_gather | solution.py:133
  209.8 7.3 %multiply_reduce_fusion.3 = (f32[64]{0:T(128)S(1)}, f32[64,2560]{1,0:T(8,128)S(1)}) fusion(bf16[2560,2560]{1,0:T(8,128)(2,1)} %all-gather.5.cloned.1.call-done, bf16[64,2560]{1,0:T(8,128)(2,1)S(1)} %copy-done.2, f32[2560]{0:T(1024)S(1)} %get-tuple-element.41, f32[2560]{0:T(1024)S(1)} %get-tuple-element.42, f32[64]{0:T(128)S(1)} %add_rsqrt_fusion.7, ...), kind=kOutput, calls=%fused_computation.83 | convolution fusion | flops 840171456 | bytes 14111488 | tf_op jit(solution)/shard_map/dot_general | solution.py:89
  217.1 1.0 multiply_multiply_fusion.3
  218.1 1.2 reshape.304
  219.3 0.3 fusion.94
  219.6 0.8 copy-done.4
  220.4 0.2 copy-done.5
  220.6 0.2 copy-done.6
  220.9 0.2 copy-done.7
  221.1 1.8 subtract_convert_fusion.3
  223.1 0.2 copy.23
  223.5 0.3 copy-done.10
  223.9 0.9 pad_maximum_fusion.12
  224.8 2.2 collective-permute-start
  226.9 0.4 convolution_reduce_fusion
  227.4 1.0 copy_bitcast_fusion.1
  228.4 4.1 %collective-permute-start.1 = (bf16[2,64,2560]{2,1,0:T(8,128)(2,1)}, bf16[2,64,2560]{2,1,0:T(8,128)(2,1)}, u32[]{:S(2)}, u32[]{:S(2)}) collective-permute-start(bf16[2,64,2560]{2,1,0:T(8,128)(2,1)} %pad_maximum_fusion.12), channel_id=1, source_target_pairs={{0,2},{1,3},{2,4},{3,5},{4,6},{5,7},{6,8},{7,9},{8,10},{9,11},{10,... | collective-permute-start | bytes 1966088 | tf_op jit(solution)/shard_map/ppermute | solution.py:23
  232.8 0.8 copy.31
  233.6 13.5 %collective-permute-done.1 = bf16[2,64,2560]{2,1,0:T(8,128)(2,1)} collective-permute-done((bf16[2,64,2560]{2,1,0:T(8,128)(2,1)}, bf16[2,64,2560]{2,1,0:T(8,128)(2,1)}, u32[]{:S(2)}, u32[]{:S(2)}) %collective-permute-start.1) | collective-permute-done | bytes 655392 | tf_op jit(solution)/shard_map/ppermute | solution.py:23
  247.1 1.8 fusion.98
  249.0 1.2 concatenate.89
  250.2 0.8 copy.32
  251.2 0.8 copy.25
  252.3 3.5 %fusion.102 = (f32[20,64]{1,0:T(8,128)S(1)}, f32[20,64,192]{2,1,0:T(8,128)}) fusion(bf16[64,20,128]{2,0,1:T(8,128)(2,1)} %copy.32, bf16[64,20,128]{2,0,1:T(8,128)(2,1)} %copy.31, bf16[64,20,64]{2,0,1:T(8,128)(2,1)} %get-tuple-element.33, bf16[64,20,64]{2,0,1:T(8,128)(2,1)} %get-tuple-element.34, pred[192]{0:T(512)(128)(4,1)S(1)} %copy-done.16, ...), kind=kOutput, calls=%fused_computation.168 | convolution fusion | flops 68485312 | bytes 2299072 | tf_op jit(solution)/shard_map/sub | solution.py:79
  255.8 1.9 fusion.11
  257.9 0.3 fusion.26
  258.2 1.0 copy_bitcast_fusion
  259.2 7.3 %multiply_reduce_fusion = (f32[64]{0:T(128)S(1)}, f32[64,2560]{1,0:T(8,128)S(1)}) fusion(bf16[2560,2560]{1,0:T(8,128)(2,1)} %all-gather.3.cloned.1.call-done, bf16[64,2560]{1,0:T(8,128)(2,1)S(1)} %get-tuple-element.6, f32[2560]{0:T(1024)S(1)} %get-tuple-element.38, f32[2560]{0:T(1024)S(1)} %get-tuple-element.39, f32[64]{0:T(128)S(1)} %add_rsqrt_fusion.2, ...), kind=kOutput, calls=%fused_computation.71 | convolution fusion | flops 840171456 | bytes 14111488 | tf_op jit(solution)/shard_map/dot_general | solution.py:165
  266.5 1.0 multiply_multiply_fusion
  267.5 1.2 reshape.307
  268.7 1.4 fusion.93
  270.1 7.3 %multiply_reduce_fusion.1 = (f32[64]{0:T(128)S(1)}, f32[64,2560]{1,0:T(8,128)S(1)}) fusion(bf16[2560,2560]{1,0:T(8,128)(2,1)} %all-gather.5.cloned.1.call-done, bf16[64,2560]{1,0:T(8,128)(2,1)S(1)} %get-tuple-element.6, f32[2560]{0:T(1024)S(1)} %get-tuple-element.38, f32[2560]{0:T(1024)S(1)} %get-tuple-element.39, f32[64]{0:T(128)S(1)} %add_rsqrt_fusion.2, ...), kind=kOutput, calls=%fused_computation.75 | convolution fusion | flops 840171456 | bytes 14111488 | tf_op jit(solution)/shard_map/dot_general | solution.py:164
  277.4 1.0 multiply_multiply_fusion.1
  278.3 1.2 reshape.306
  279.5 0.3 fusion.92
  279.8 0.8 copy-done.8
  280.7 0.2 copy-done.9
  280.9 1.2 subtract_convert_fusion.1
  282.1 3.2 %fusion.105 = (f32[20,64]{1,0:T(8,128)S(1)}, f32[20,64,192]{2,1,0:T(8,128)}) fusion(bf16[64,20,128]{2,0,1:T(8,128)(2,1)} %copy.32, bf16[64,20,128]{2,0,1:T(8,128)(2,1)} %copy.31, bf16[64,20,64]{2,0,1:T(8,128)(2,1)S(1)} %get-tuple-element.31, bf16[64,20,64]{2,0,1:T(8,128)(2,1)} %get-tuple-element.32, pred[192]{0:T(512)(128)(4,1)S(1)} %copy-done.16, ...), kind=kOutput, calls=%fused_computation.169 | convolution fusion | flops 68485312 | bytes 2299072 | tf_op jit(solution)/shard_map/sub | solution.py:79
  285.3 2.1 fusion.9
  287.4 0.8 fusion.39
  (60 shorter events, 1.9 us)
Async XLA Ops:
  6.5 18.3 %copy-start = (bf16[128,7680]{1,0:T(8,128)(2,1)S(1)}, bf16[128,7680]{1,0:T(8,128)(2,1)}, u32[]{:S(2)}) copy-start(bf16[128,7680]{1,0:T(8,128)(2,1)} %param.17) | copy-start | bytes 5898244
  6.5 18.0 %copy-start.3 = (bf16[64,2560]{1,0:T(8,128)(2,1)S(1)}, bf16[64,2560]{1,0:T(8,128)(2,1)}, u32[]{:S(2)}) copy-start(bf16[64,2560]{1,0:T(8,128)(2,1)} %param.11) | copy-start | bytes 983044
  6.5 104.1 %all-gather.3.cloned.1.call-start = ((), (), s32[]{:S(2)}) async-start(), calls=%async_computation | async-start | bytes 13516800 | tf_op jit(solution)/shard_map/all_gather | solution.py:134
  7.3 202.5 %all-gather.5.cloned.1.call-start = ((), (), s32[]{:S(2)}) async-start(), calls=%async_computation.1 | async-start | bytes 13516800 | tf_op jit(solution)/shard_map/all_gather | solution.py:133
  24.8 85.8 %copy-start.2 = (bf16[64,2560]{1,0:T(8,128)(2,1)S(1)}, bf16[64,2560]{1,0:T(8,128)(2,1)}, u32[]{:S(2)}) copy-start(bf16[64,2560]{1,0:T(8,128)(2,1)} %param.10) | copy-start | bytes 983044
  110.7 8.5 %copy-start.1 = (bf16[2560,2560]{1,0:T(8,128)(2,1)S(1)}, bf16[2560,2560]{1,0:T(8,128)(2,1)}, u32[]{:S(2)}) copy-start(bf16[2560,2560]{1,0:T(8,128)(2,1)} %all-gather.3.cloned.1.call-done) | copy-start | bytes 39321604
  119.1 2.6 copy-start.14
  129.0 88.1 %copy-start.15 = (f32[2560]{0:T(1024)S(1)}, f32[2560]{0:T(1024)}, u32[]{:S(2)}) copy-start(f32[2560]{0:T(1024)} %param.18) | copy-start | bytes 30724
  219.3 1.1 copy-start.4
  219.3 1.4 copy-start.5
  219.3 1.6 copy-start.6
  219.3 1.8 copy-start.7
  222.9 1.0 copy-start.10
  224.8 7.8 %collective-permute-start = (bf16[2,64,2560]{2,1,0:T(8,128)(2,1)}, bf16[2,64,2560]{2,1,0:T(8,128)(2,1)S(1)}, u32[]{:S(2)}, u32[]{:S(2)}) collective-permute-start(bf16[2,64,2560]{2,1,0:T(8,128)(2,1)} %pad_maximum_fusion.12), channel_id=1, source_target_pairs={{0,1},{1,2},{2,3},{3,4},{4,5},{5,6},{6,7},{7,8},{8,9},{9,10},{10,1... | collective-permute-start | bytes 1966088 | tf_op jit(solution)/shard_map/ppermute | solution.py:23
  228.4 18.7 %collective-permute-start.1 = (bf16[2,64,2560]{2,1,0:T(8,128)(2,1)}, bf16[2,64,2560]{2,1,0:T(8,128)(2,1)}, u32[]{:S(2)}, u32[]{:S(2)}) collective-permute-start(bf16[2,64,2560]{2,1,0:T(8,128)(2,1)} %pad_maximum_fusion.12), channel_id=1, source_target_pairs={{0,2},{1,3},{2,4},{3,5},{4,6},{5,7},{6,8},{7,9},{8,10},{9,11},{10,... | collective-permute-start | bytes 1966088 | tf_op jit(solution)/shard_map/ppermute | solution.py:23
  250.2 2.1 copy-start.16
  251.2 1.1 copy-start.11
  252.2 3.5 %copy-start.13 = (bf16[64,20,128]{2,0,1:T(8,128)(2,1)}, bf16[64,20,128]{2,0,1:T(8,128)(2,1)S(1)}, u32[]{:S(2)}) copy-start(bf16[64,20,128]{2,0,1:T(8,128)(2,1)S(1)} %copy.26) | copy-start | bytes 983044
  252.3 3.5 %copy-start.12 = (bf16[64,20,128]{2,0,1:T(8,128)(2,1)S(1)}, bf16[64,20,128]{2,0,1:T(8,128)(2,1)}, u32[]{:S(2)}) copy-start(bf16[64,20,128]{2,0,1:T(8,128)(2,1)} %copy.25) | copy-start | bytes 983044
  279.5 1.1 copy-start.8
  279.5 1.4 copy-start.9
Sparse Core Ops, SparseCore 0:
  10.2 100.4 all-gather.2
  113.5 96.2 all-gather.4
where the time goes:
time: 300 us; the launch traced here: 295 us
  waiting for transfers between devices  179 us (60%)
  matrix products  43.8 us (15%)
  local copies, waits for them, and re-layouts  26.6 us (9%)
  between operations  19.9 us (7%)
  other arithmetic  19.1 us (6%)
  starting transfers between devices  6.37 us (2%)
    all_gather x1, waiting for transfers between devices, local(): lax.all_gather(w_key, 'fsdp', axis=0, tiled=True)  83.7 us
    all_gather x1, waiting for transfers between devices, local(): lax.all_gather(w_query, 'fsdp', axis=0, tiled=True)  80.8 us
    ppermute x2, waiting for transfers between devices, passed_along(): lax.ppermute(value, axis, [(source, source + steps) for source in range(l...  13.5 us
    dot_general x1, matrix products, absorb_both(): jnp.dot(noisy_hidden, pieces[1], preferred_element_type=jnp.float32)  7.43 us
    dot_general x1, matrix products, local(): key_raw = jnp.dot(hidden, full_key, preferred_element_type=jnp.float32)  7.28 us
    dot_general x1, matrix products, local(): query_raw = jnp.dot(hidden, full_query, preferred_element_type=jnp.float32)  7.28 us
    dot_general x1, matrix products, absorb_both(): jnp.dot(noisy_hidden, pieces[0], preferred_element_type=jnp.float32)  7.28 us
    sub x2, matrix products, attend(): expanded = jnp.exp(scores - highest)  6.66 us
  transfers between devices with their start and end apart: 4, of which 3 were waited for; matrix products, arithmetic and copies ran while one was open for 11% of the time, Pallas kernels for 0%

commit v1 on v0

v1 whole, which is shorter than its diff:
```python
import functools
import math

import jax
import jax.numpy as jnp
from jax import lax
from jax.experimental import pallas as pl
from jax.experimental.pallas import tpu as pltpu
from jax.sharding import PartitionSpec as P

HEADS = 20
HEAD_DIM = 128
STEPS = 2
LAGS = 2
LEVELS = 1000

SIGMA_SHIFT = 5.0
EPSILON = 1e-06
MASKED = -1e30
AXIS = "fsdp"


def sigma_of(levels):
    fraction = levels.astype(jnp.float32) / LEVELS
    return SIGMA_SHIFT * fraction / (1.0 + (SIGMA_SHIFT - 1.0) * fraction)


def frequencies(half_count):
    return jnp.exp(-math.log(10000.0) * jnp.arange(half_count, dtype=jnp.float32) / half_count)


def modulation(sigmas, time_proj):
    half_count = time_proj.shape[0] // 2
    angles = 1000.0 * sigmas[:, None] * frequencies(half_count)[None, :]
    features = jnp.concatenate([jnp.cos(angles), jnp.sin(angles)], axis=1).astype(jnp.bfloat16)
    return jnp.dot(features, time_proj, preferred_element_type=jnp.float32)


def modulate(latent, shift, scale):
    values = latent.astype(jnp.float32)
    centred = values - jnp.mean(values, axis=-1, keepdims=True)
    variance = jnp.mean(centred * centred, axis=-1, keepdims=True)
    normed = centred * lax.rsqrt(variance + EPSILON)
    return (normed * (1.0 + scale) + shift).astype(jnp.bfloat16)


def permute(value, target_of):
    pairs = [(s, target_of(s)) for s in range(lax.axis_size(AXIS))]
    return lax.ppermute(value, AXIS, [(s, t) for s, t in pairs if t is not None])


def swap_core(value):
    return permute(value, lambda s: s ^ 1)


def swap_x(value):
    return permute(value, lambda s: s ^ 2)


def swap_y(value):
    return permute(value, lambda s: s ^ 4)


def swap_z_pair(value):
    return permute(value, lambda s: s ^ 8)


def swap_z_middle(value):
    return permute(value, lambda s: {1: s + 8, 2: s - 8}.get(s // 8))


def z_outward(value):
    return permute(value, lambda s: {1: s - 8, 2: s + 8}.get(s // 8))


def gather_block(unit, device):
    rows, width = unit.shape
    half = rows // 2
    z = device // 8
    y = (device // 4) % 2
    x = (device // 2) % 2
    middle = (z == 1) | (z == 2)
    pair = swap_z_pair(unit)
    across = swap_z_middle(unit)
    two_mid = swap_z_middle(pair)
    two_end = z_outward(across)
    three_end = z_outward(two_mid)
    slots = [
        unit,
        pair,
        jnp.where(middle, two_mid, two_end),
        jnp.where(middle, across, three_end),
    ]
    planes = []
    for step, own in enumerate(slots):
        from_x = swap_x(own)
        from_y = swap_y(own)
        far_low = swap_y(from_x[:half])
        far_high = swap_x(from_y[half:])
        far = jnp.concatenate([far_low, far_high], axis=0)
        plane = jnp.zeros((4, rows, width), unit.dtype)
        place = y * 2 + x
        for piece, at in ((own, place), (from_x, place ^ 1), (from_y, place ^ 2), (far, place ^ 3)):
            plane = lax.dynamic_update_slice(plane, piece[None], (at, 0, 0))
        planes.append((z ^ step, plane.reshape(4 * rows, width)))
    return planes


def gather_any(unit, device):
    size = lax.axis_size(AXIS)
    groups = [list(range(core, size, 2)) for core in range(2)]
    return [(jnp.int32(0), lax.all_gather(unit, AXIS, axis=0, tiled=True, axis_index_groups=groups))]


def turn(values, cosine, sine):
    return values * cosine + pltpu.roll(values, HEAD_DIM // 2, 1) * sine


def attend_body(first, *refs):
    if first:
        (q_ref, k_ref, c_ref, qs_ref, ks_ref, cs_ref, qg_ref, kg_ref, cos_ref, sin_ref, mask_ref,
         v_ref, cv_ref, lat_ref, fac_ref, out_ref, ck_ref) = refs
    else:
        (q_ref, k_ref, c_ref, qs_ref, ks_ref, qg_ref, kg_ref, cos_ref, sin_ref, mask_ref,
         v_ref, cv_ref, lat_ref, fac_ref, out_ref) = refs
    rows = q_ref.shape[0]
    extra = c_ref.shape[0]
    own_cos, own_sin = cos_ref[extra - rows // 2 :, :], sin_ref[extra - rows // 2 :, :]
    query = turn(q_ref[...] * qs_ref[...] * qg_ref[...], own_cos, own_sin).astype(jnp.bfloat16)
    key = turn(k_ref[...] * ks_ref[...] * kg_ref[...], own_cos, own_sin).astype(jnp.bfloat16)
    if first:
        past = turn(
            c_ref[...] * cs_ref[...] * kg_ref[...], cos_ref[:extra, :], sin_ref[:extra, :]
        ).astype(jnp.bfloat16)
        ck_ref[...] = past
    else:
        past = c_ref[...]
    keys = jnp.concatenate([key, past], axis=0)
    values = jnp.concatenate([v_ref[...], cv_ref[...]], axis=0)
    scores = lax.dot_general(
        query, keys, (((1,), (1,)), ((), ())), preferred_element_type=jnp.float32
    ) * HEAD_DIM ** (-0.5)
    scores = jnp.where(mask_ref[...] > 0.0, scores, MASKED)
    expanded = jnp.exp(scores - jnp.max(scores, axis=-1, keepdims=True))
    weights = (expanded / jnp.sum(expanded, axis=-1, keepdims=True)).astype(jnp.bfloat16)
    mixed = jnp.dot(weights, values, preferred_element_type=jnp.float32).astype(jnp.bfloat16)
    factor = jnp.concatenate(
        [jnp.broadcast_to(fac_ref[i : i + 1, :], (rows // 2, HEAD_DIM)) for i in range(2)], axis=0
    )
    out_ref[...] = (
        lat_ref[...].astype(jnp.float32) + factor * mixed.astype(jnp.float32)
    ).astype(jnp.bfloat16)


def attend(first, raw, past, scales, gains, tables, mask, values, past_values, latent, factor):
    rows, width = latent.shape
    extra = past.shape[0]
    heads = width // HEAD_DIM

    def column(count, shift=0):
        return pl.BlockSpec((count, HEAD_DIM), lambda h: (0, h + shift))

    def whole(array):
        return pl.BlockSpec(array.shape, lambda h: (0, 0))

    operands = [raw, raw, past, *scales, *gains, *tables, mask, values, past_values, latent, factor]
    specs = [column(rows), column(rows, heads), column(extra)]
    specs += [whole(s) for s in scales]
    specs += [column(1), column(1)]
    specs += [whole(t) for t in tables] + [whole(mask)]
    specs += [column(rows), column(extra), column(rows), column(factor.shape[0])]
    shapes = [jax.ShapeDtypeStruct((rows, width), jnp.bfloat16)]
    outs = [column(rows)]
    if first:
        shapes.append(jax.ShapeDtypeStruct((extra, width), jnp.bfloat16))
        outs.append(column(extra))
    return pl.pallas_call(
        functools.partial(attend_body, first),
        grid=(heads,),
        in_specs=specs,
        out_specs=outs,
        out_shape=shapes,
        name="attend",
    )(*operands)


def local(noisy, clean, seg_ids, lag_mask, plan, w_query, w_key, time_proj, q_gain, k_gain):
    rows, width = noisy.shape
    inner = w_query.shape[1]
    half = inner // 2
    shard = w_query.shape[0]
    devices = lax.axis_size(AXIS)
    device = lax.axis_index(AXIS)
    core = device % 2
    first_span = device - core
    is_low = core == 0

    def mine(value, axis):
        return lax.dynamic_slice_in_dim(value, core * half, half, axis)

    def theirs(value, axis):
        return lax.dynamic_slice_in_dim(value, (1 - core) * half, half, axis)

    def in_order(own, other, axis):
        low = jnp.where(is_low, own, other)
        high = jnp.where(is_low, other, own)
        return jnp.concatenate([low, high], axis=axis)

    own_rows = jnp.concatenate([mine(w_query, 1), mine(w_key, 1)], axis=1)
    sent_rows = jnp.concatenate([theirs(w_query, 1), theirs(w_key, 1)], axis=1)
    unit = in_order(own_rows, swap_core(sent_rows), 0)
    planes = (gather_block if devices == 32 else gather_any)(unit, device)
    plane_rows = planes[0][1].shape[0]
    plane_count = width // plane_rows

    noisy_both = in_order(noisy, swap_core(noisy), 0)
    before = permute(clean, lambda s: s + 2 if s + 2 < devices else None)
    before_both = in_order(before, swap_core(before), 0)
    first_clean = jnp.where(is_low, clean, swap_core(clean))
    past_clean = jnp.concatenate([before_both, first_clean], axis=0)
    small = jnp.concatenate([plan, lag_mask], axis=1)
    small_both = in_order(small, swap_core(small), 0)
    plan_both, lags_both = small_both[:, :STEPS], small_both[:, STEPS:]

    sigmas = [sigma_of(plan_both[:, j]) for j in range(STEPS)] + [jnp.zeros((2,), jnp.float32)]
    mods = modulation(jnp.concatenate([jnp.zeros((1,), jnp.float32)] + sigmas[:STEPS]), time_proj)

    def per_row(pair):
        return jnp.repeat(pair, rows, axis=0)

    step_mods = [mods[1 + 2 * j : 3 + 2 * j] for j in range(STEPS)]
    factors = [
        (sigmas[j + 1] - sigmas[j])[:, None] * mine(step_mods[j][:, 2 * width :], 1)
        for j in range(STEPS)
    ]
    past_hidden = modulate(past_clean, mods[:1, :width], mods[:1, width : 2 * width])
    hidden = modulate(
        noisy_both, per_row(step_mods[0][:, :width]), per_row(step_mods[0][:, width : 2 * width])
    )

    spans = jnp.maximum(first_span - 2 + jnp.arange(4, dtype=jnp.int32), 0)
    segments = seg_ids[spans]
    starts = jnp.sum((seg_ids[None, :] < segments[:, None]).astype(jnp.int32), axis=1)
    positions = (
        (spans - starts)[:, None] * rows + jnp.arange(rows, dtype=jnp.int32)[None, :]
    ).astype(jnp.float32).reshape(-1, 1)
    angles = positions * frequencies(HEAD_DIM // 2)[None, :]
    cosine = jnp.concatenate([jnp.cos(angles)] * 2, axis=1)
    sine = jnp.concatenate([-jnp.sin(angles), jnp.sin(angles)], axis=1)
    allowed = []
    for local_span in range(2):
        seen = [jnp.bool_(s == local_span) for s in range(2)]
        for source in range(3):
            lag = local_span + 2 - source
            if 1 <= lag <= LAGS:
                usable = (
                    (first_span + local_span >= lag)
                    & (segments[source] == segments[2 + local_span])
                    & (lags_both[local_span, lag - 1] == 1)
                )
            else:
                usable = jnp.bool_(False)
            seen.append(usable)
        allowed.append(jnp.stack(seen))
    mask = jnp.repeat(jnp.repeat(jnp.stack(allowed).astype(jnp.float32), rows, 0), rows, 1)

    def project(values, columns):
        total = None
        for place, weights in planes:
            part = lax.dynamic_slice_in_dim(values, place * plane_rows, plane_rows, 1)
            part = jnp.dot(part, weights[:, columns], preferred_element_type=jnp.float32)
            total = part if total is None else total + part
        return total

    def squares(values):
        return jnp.sum(values * values, axis=-1)

    def scale_of(total):
        return lax.rsqrt(total / inner + EPSILON)[:, None]

    gains = (mine(q_gain, 0)[None, :], mine(k_gain, 0)[None, :])
    tables = (cosine, sine)
    latent = mine(noisy_both, 1)
    values = mine(hidden, 1)
    past_values = mine(past_hidden, 1)

    raw = project(hidden, slice(0, 2 * half))
    past_raw = project(past_hidden, slice(half, 2 * half))
    sums = jnp.concatenate([squares(raw[:, :half]), squares(raw[:, half:]), squares(past_raw)])
    scale = scale_of(sums + swap_core(sums))
    both = 2 * rows
    latent, past_key = attend(
        True, raw, past_raw, (scale[:both], scale[both : 2 * both], scale[2 * both :]),
        gains, tables, mask, values, past_values, latent, factors[0],
    )

    f32 = latent.astype(jnp.float32)
    half_mean = jnp.mean(f32, axis=-1)
    half_centred = f32 - half_mean[:, None]
    moments = jnp.stack([half_mean, jnp.sum(half_centred * half_centred, axis=-1)])
    others = swap_core(moments)
    mean = 0.5 * (moments[0] + others[0])
    gap = moments[0] - others[0]
    variance = (moments[1] + others[1] + gap * gap * (half / 2)) / inner
    normed = (f32 - mean[:, None]) * lax.rsqrt(variance + EPSILON)[:, None]
    shift = per_row(mine(step_mods[1][:, :width], 1))
    gain = per_row(mine(step_mods[1][:, width : 2 * width], 1))
    values = (normed * (1.0 + gain) + shift).astype(jnp.bfloat16)
    hidden = in_order(values, swap_core(values), 1)

    raw = project(hidden, slice(0, 2 * half))
    sums = jnp.concatenate([squares(raw[:, :half]), squares(raw[:, half:])])
    scale = scale_of(sums + swap_core(sums))
    (latent,) = attend(
        False, raw, past_key, (scale[:both], scale[both:]),
        gains, tables, mask, values, past_values, latent, factors[1],
    )
    kept = lax.dynamic_slice_in_dim(latent, core * rows, rows, 0)
    sent = lax.dynamic_slice_in_dim(latent, (1 - core) * rows, rows, 0)
    return in_order(kept, swap_core(sent), 1)


def solution(mesh):
    placed = (
        P(("pool", "fsdp"), None),
        P(("pool", "fsdp"), None),
        P("pool"),
        P(("pool", "fsdp"), None),
        P(("pool", "fsdp"), None),
        P("fsdp", None),
        P("fsdp", None),
        P(),
        P(),
        P(),
    )
    return jax.shard_map(
        local, mesh=mesh, in_specs=placed, out_specs=P(("pool", "fsdp"), None), check_vma=False
    )
```

time: 300 us -> 201 us (0.67); the launches traced: 295 us -> 199 us
  waiting for transfers between devices: 179 us -> 92.1 us
  matrix products: 43.8 us -> 11.7 us
  starting transfers between devices: 6.37 us -> 32.8 us
  Pallas kernels: 0 us -> 20.4 us
  between operations: 19.9 us -> 8.14 us
  local copies, waits for them, and re-layouts: 26.6 us -> 18.5 us
  other arithmetic: 19.1 us -> 15.6 us
    all_gather x2 -> x0, waiting for transfers between devices: 164 us -> none  [the longest x1 83.7 us: local(): lax.all_gather(w_key, 'fsdp', axis=0, tiled=True)]
    ppermute x2 -> x32, waiting for transfers between devices: 13.5 us -> 92.1 us  [permute(): lax.ppermute(value, AXIS, [(s, t) for s, t in pairs if t is not None])]
    ppermute x2 -> x32, starting transfers between devices: 6.33 us -> 32.8 us  [permute(): lax.ppermute(value, AXIS, [(s, t) for s, t in pairs if t is not None])]
    dot_general x10 -> x13, matrix products: 37.1 us -> 11.7 us  [the longest x12 11.3 us: project(): jnp.dot(part, weights[:, columns], preferred_element_type=jnp.float32)]
    pallas_call x0 -> x2, Pallas kernels: none -> 20.4 us  [attend(): pl.pallas_call(functools.partial(attend_body, first), grid=(heads,), in_s...]
    sub x2 -> x0, matrix products: 6.66 us -> none  [attend(): expanded = jnp.exp(scores - highest)]
    slice x9 -> x18, local copies, waits for them, and re-layouts: 10.7 us -> 5.24 us  [the longest x2 1.48 us: local(): scale[:both]]
    another operation x7 -> x2, other arithmetic: 5.03 us -> 0.13 us
  transfers between devices with their start and end apart: 4 -> 32, of which waited for: 3 -> 13; matrix products, arithmetic and copies ran while one was open for 11% -> 11% of each run, Pallas kernels for 0% -> 0%
where the time goes in v1:
time: 201 us; the launch traced here: 199 us
  waiting for transfers between devices  92.1 us (46%)
  starting transfers between devices  32.8 us (16%)
  Pallas kernels  20.4 us (10%)
  local copies, waits for them, and re-layouts  18.5 us (9%)
  other arithmetic  15.6 us (8%)
  matrix products  11.7 us (6%)
  between operations  8.14 us (4%)
    ppermute x32, waiting for transfers between devices, permute(): lax.ppermute(value, AXIS, [(s, t) for s, t in pairs if t is not None])  92.1 us
    ppermute x32, starting transfers between devices, permute(): lax.ppermute(value, AXIS, [(s, t) for s, t in pairs if t is not None])  32.8 us
    pallas_call x2, Pallas kernels, attend(): pl.pallas_call(functools.partial(attend_body, first), grid=(heads,), in_s...  20.4 us
    dot_general x12, matrix products, project(): jnp.dot(part, weights[:, columns], preferred_element_type=jnp.float32)  11.3 us
    unnamed x34, local copies, waits for them, and re-layouts  5.08 us
  transfers between devices with their start and end apart: 32, of which 13 were waited for; matrix products, arithmetic and copies ran while one was open for 11% of the time, Pallas kernels for 0%

profile of v1, /device:TPU:0, one launch (start us, length us, event | category | flops | bytes accessed | tf_op | source)
XLA Modules:
  0.0 199.3 jit_solution(17988847096322660038)
XLA Ops:
  0.0 5.7 %collective-permute-start.24 = (bf16[64,2560]{1,0:T(8,128)(2,1)}, bf16[64,2560]{1,0:T(8,128)(2,1)}, u32[]{:S(2)}, u32[]{:S(2)}) collective-permute-start(bf16[64,2560]{1,0:T(8,128)(2,1)} %param.11), channel_id=1, source_target_pairs={{0,2},{1,3},{2,4},{3,5},{4,6},{5,7},{6,8},{7,9},{8,10},{9,11},{10,... | collective-permute-start | bytes 983048 | tf_op jit(solution)/shard_map/ppermute | solution.py:49
  5.8 1.3 constant_dynamic-slice_fusion.9
  8.9 0.7 fusion.86
  16.9 0.8 pad_maximum_fusion.6
  18.8 0.6 fusion.85
  22.5 0.8 copy.27.refs_10_.refs_9_
  23.3 0.7 fusion.63.refs_14_
  23.9 1.1 broadcast_select_fusion.8
  26.3 0.9 fusion.31
  27.4 1.0 collective-permute-start.7
  28.4 1.5 collective-permute-start.3
  29.9 1.5 collective-permute-start.4
  31.4 0.7 collective-permute-start.13
  32.4 1.1 broadcast_select_fusion.6
  34.6 14.7 %collective-permute-done.3 = bf16[160,2560]{1,0:T(8,128)(2,1)S(1)} collective-permute-done((bf16[160,2560]{1,0:T(8,128)(2,1)S(1)}, bf16[160,2560]{1,0:T(8,128)(2,1)S(1)}, u32[]{:S(2)}, u32[]{:S(2)}) %collective-permute-start.3) | collective-permute-done | bytes 819232 | tf_op jit(solution)/shard_map/ppermute | solution.py:49
  49.4 1.6 collective-permute-start.5
  51.0 1.6 collective-permute-start.6
  53.1 1.4 collective-permute-start.9
  55.0 0.7 collective-permute-start.12
  55.7 6.1 %collective-permute-done.5 = bf16[80,2560]{1,0:T(8,128)(2,1)S(1)} collective-permute-done((bf16[80,2560]{1,0:T(8,128)(2,1)S(1)}, bf16[80,2560]{1,0:T(8,128)(2,1)S(1)}, u32[]{:S(2)}, u32[]{:S(2)}) %collective-permute-start.5) | collective-permute-done | bytes 409632 | tf_op jit(solution)/shard_map/ppermute | solution.py:49
  61.8 1.3 collective-permute-start.14
  63.5 0.7 fusion.48
  64.2 1.0 copy-done.6
  65.7 16.8 %collective-permute-done.14 = bf16[160,2560]{1,0:T(8,128)(2,1)S(1)} collective-permute-done((bf16[160,2560]{1,0:T(8,128)(2,1)S(1)}, bf16[160,2560]{1,0:T(8,128)(2,1)S(1)}, u32[]{:S(2)}, u32[]{:S(2)}) %collective-permute-start.14) | collective-permute-done | bytes 819232 | tf_op jit(solution)/shard_map/ppermute | solution.py:49
  83.0 1.6 collective-permute-start.15
  84.6 1.5 collective-permute-start.16
  87.3 1.5 collective-permute-start.19
  88.9 22.1 %collective-permute-done.10 = bf16[80,2560]{1,0:T(8,128)(2,1)S(1)} collective-permute-done((bf16[80,2560]{1,0:T(8,128)(2,1)S(1)}, bf16[80,2560]{1,0:T(8,128)(2,1)S(1)}, u32[]{:S(2)}, u32[]{:S(2)}) %collective-permute-start.10) | collective-permute-done | bytes 409632 | tf_op jit(solution)/shard_map/ppermute | solution.py:49
  111.1 0.7 convolution_add_fusion.5
  111.8 1.0 copy-done.7
  114.5 1.5 collective-permute-start.21
  116.7 1.6 collective-permute-start.18
  118.4 21.5 %collective-permute-done.17 = bf16[80,2560]{1,0:T(8,128)(2,1)S(1)} collective-permute-done((bf16[80,2560]{1,0:T(8,128)(2,1)S(1)}, bf16[80,2560]{1,0:T(8,128)(2,1)S(1)}, u32[]{:S(2)}, u32[]{:S(2)}) %collective-permute-start.17) | collective-permute-done | bytes 409632 | tf_op jit(solution)/shard_map/ppermute | solution.py:49
  140.6 0.7 convolution_add_fusion.4
  141.8 1.6 collective-permute-start.22
  143.4 1.5 collective-permute-start.23
  145.1 4.7 %collective-permute-done.22 = bf16[80,2560]{1,0:T(8,128)(2,1)S(1)} collective-permute-done((bf16[80,2560]{1,0:T(8,128)(2,1)S(1)}, bf16[80,2560]{1,0:T(8,128)(2,1)S(1)}, u32[]{:S(2)}, u32[]{:S(2)}) %collective-permute-start.22) | collective-permute-done | bytes 409632 | tf_op jit(solution)/shard_map/ppermute | solution.py:49
  149.8 1.6 collective-permute-done.23
  151.5 2.0 multiply_reduce_fusion
  153.5 0.7 convolution_add_fusion.3.refs_0_.refs_1_
  154.4 1.0 constant_dynamic-slice_fusion.5.refs_12_.refs_11_
  155.6 0.8 copy.26.refs_5_
  156.4 0.7 copy.24.refs_3_
  157.1 0.7 copy.25.refs_4_
  157.9 10.4 %attend.2 = (bf16[128,1280]{1,0:T(8,128)(2,1)}, bf16[192,1280]{1,0:T(8,128)(2,1)}) custom-call(f32[128,2560]{1,0:T(8,128)} %copy-done.10, f32[128,2560]{1,0:T(8,128)} %copy-done.10, f32[192,1280]{1,0:T(8,128)} %get-tuple-element.69.refs_2_, f32[128,1]{1,0:T(8,128)} %copy.24.refs_3_, f32[128,1]{1,0:T(8,128)} %copy.25.refs_4_, f32[192,1]{1,0:T(8,128)} %copy.26.refs_5_, ...), custom_call_target="tpu_custom_call" | custom-call | tf_op jit(solution)/shard_map/attend/pallas_call | solution.py:177
  168.2 1.1 convert_reduce_fusion.2
  169.4 1.2 fusion.22
  170.8 1.0 collective-permute-done.28
  171.8 1.2 fusion.26.refs_10_
  173.3 1.5 collective-permute-done.29
  174.8 2.8 %fusion.39 = f32[128,2560]{1,0:T(8,128)S(1)} fusion(bf16[640,2560]{1,0:T(8,128)(2,1)} %bitcast.121, s32[]{:T(128)S(6)} %select_n.187, bf16[128,1280]{1,0:T(8,128)(2,1)S(1)} %get-tuple-element.26, bf16[128,1280]{1,0:T(8,128)(2,1)S(1)} %get-tuple-element.25), kind=kOutput, calls=%fused_computation.105 | convolution fusion | flops 419758080 | bytes 5242884 | tf_op jit(solution)/shard_map/dot_general | solution.py:271
  177.7 0.7 convolution_add_fusion.2
  178.4 1.2 copy-done.5
  179.7 0.7 convolution_add_fusion.1
  180.4 1.2 copy-done.3
  181.6 0.7 convolution_add_fusion.refs_0_.refs_1_
  182.7 0.7 fusion.65.refs_13_
  183.7 0.7 copy.28.refs_3_
  184.5 0.7 copy.29.refs_4_
  185.2 10.0 %attend.3 = bf16[128,1280]{1,0:T(8,128)(2,1)} custom-call(f32[128,2560]{1,0:T(8,128)} %copy-done.9, f32[128,2560]{1,0:T(8,128)} %copy-done.9, bf16[192,1280]{1,0:T(8,128)(2,1)} %get-tuple-element.8.refs_2_, f32[128,1]{1,0:T(8,128)} %copy.28.refs_3_, f32[128,1]{1,0:T(8,128)} %copy.29.refs_4_, f32[1,1280]{1,0:T(1,128)} %broadcast_in_dim.109.refs_6_.refs_5_, ...), custom_call_target="tpu_custom_call" | custom-call | tf_op jit(solution)/shard_map/attend/pallas_call | solution.py:177
  195.2 0.9 constant_dynamic-slice_fusion
  196.4 1.2 collective-permute-done.31
  197.6 1.0 broadcast_select_fusion.12
  198.6 0.7 pad_maximum_fusion.5
  (156 shorter events, 18.2 us)
Async XLA Ops:
  0.0 18.3 %copy-start = (bf16[128,7680]{1,0:T(8,128)(2,1)S(1)}, bf16[128,7680]{1,0:T(8,128)(2,1)}, u32[]{:S(2)}) copy-start(bf16[128,7680]{1,0:T(8,128)(2,1)} %param.17) | copy-start | bytes 5898244
  0.0 7.7 %copy-start.15 = (s32[1,2]{1,0:T(1,128)S(1)}, s32[1,2]{1,0:T(1,128)}, u32[]{:S(2)}) copy-start(s32[1,2]{1,0:T(1,128)} %param.13) | copy-start | bytes 28
  0.0 7.7 %copy-start.16 = (s32[1,2]{1,0:T(1,128)S(1)}, s32[1,2]{1,0:T(1,128)}, u32[]{:S(2)}) copy-start(s32[1,2]{1,0:T(1,128)} %param.14) | copy-start | bytes 28
  0.0 8.3 %copy-start.1 = (s32[32]{0:T(128)S(1)}, s32[32]{0:T(128)}, u32[]{:S(2)}) copy-start(s32[32]{0:T(128)} %param.12) | copy-start | bytes 388
  0.0 15.0 %copy-start.13 = (f32[2560]{0:T(1024)S(1)}, f32[2560]{0:T(1024)}, u32[]{:S(2)}) copy-start(f32[2560]{0:T(1024)} %param.18) | copy-start | bytes 30724
  0.0 15.7 %copy-start.14 = (f32[2560]{0:T(1024)S(1)}, f32[2560]{0:T(1024)}, u32[]{:S(2)}) copy-start(f32[2560]{0:T(1024)} %param.19) | copy-start | bytes 30724
  0.0 25.2 %collective-permute-start.24 = (bf16[64,2560]{1,0:T(8,128)(2,1)}, bf16[64,2560]{1,0:T(8,128)(2,1)}, u32[]{:S(2)}, u32[]{:S(2)}) collective-permute-start(bf16[64,2560]{1,0:T(8,128)(2,1)} %param.11), channel_id=1, source_target_pairs={{0,2},{1,3},{2,4},{3,5},{4,6},{5,7},{6,8},{7,9},{8,10},{9,11},{10,... | collective-permute-start | bytes 983048 | tf_op jit(solution)/shard_map/ppermute | solution.py:49
  5.8 19.9 %collective-permute-start.26 = (bf16[64,2560]{1,0:T(8,128)(2,1)}, bf16[64,2560]{1,0:T(8,128)(2,1)}, u32[]{:S(2)}, u32[]{:S(2)}) collective-permute-start(bf16[64,2560]{1,0:T(8,128)(2,1)} %param.11), channel_id=1, source_target_pairs={{0,1},{1,0},{2,3},{3,2},{4,5},{5,4},{6,7},{7,6},{8,9},{9,8},{10,11... | collective-permute-start | bytes 983048 | tf_op jit(solution)/shard_map/ppermute | solution.py:49
  7.1 20.1 %collective-permute-start.2 = (bf16[80,2560]{1,0:T(8,128)(2,1)S(1)}, bf16[80,2560]{1,0:T(8,128)(2,1)S(1)}, u32[]{:S(2)}, u32[]{:S(2)}) collective-permute-start(bf16[80,2560]{1,0:T(8,128)(2,1)S(1)} %pad_maximum_fusion.4), channel_id=1, source_target_pairs={{0,1},{1,0},{2,3},{3,2},{4,5},{5,4},{6,7},{7,6},{8,9},{9,8},{10,11... | collective-permute-start | bytes 1228808 | tf_op jit(solution)/shard_map/ppermute | solution.py:49
  7.8 10.0 %collective-permute-start.1 = (s32[1,4]{1,0:T(1,128)S(1)}, s32[1,4]{1,0:T(1,128)S(1)}, u32[]{:S(2)}, u32[]{:S(2)}) collective-permute-start(s32[1,4]{1,0:T(1,128)S(1)} %pad_add_fusion.1), channel_id=1, source_target_pairs={{0,1},{1,0},{2,3},{3,2},{4,5},{5,4},{6,7},{7,6},{8,9},{9,8},{10,11... | collective-permute-start | bytes 56 | tf_op jit(solution)/shard_map/ppermute | solution.py:49
  7.8 16.2 %collective-permute-start = (bf16[64,2560]{1,0:T(8,128)(2,1)}, bf16[64,2560]{1,0:T(8,128)(2,1)}, u32[]{:S(2)}, u32[]{:S(2)}) collective-permute-start(bf16[64,2560]{1,0:T(8,128)(2,1)} %param.10), channel_id=1, source_target_pairs={{0,1},{1,0},{2,3},{3,2},{4,5},{5,4},{6,7},{7,6},{8,9},{9,8},{10,11... | collective-permute-start | bytes 983048 | tf_op jit(solution)/shard_map/ppermute | solution.py:49
  23.3 2.4 %copy-start.12 = (bf16[64,2560]{1,0:T(8,128)(2,1)S(1)}, bf16[64,2560]{1,0:T(8,128)(2,1)}, u32[]{:S(2)}) copy-start(bf16[64,2560]{1,0:T(8,128)(2,1)} %param.11) | copy-start | bytes 983044
  25.2 7.2 %collective-permute-start.25 = (bf16[64,2560]{1,0:T(8,128)(2,1)}, bf16[64,2560]{1,0:T(8,128)(2,1)S(1)}, u32[]{:S(2)}, u32[]{:S(2)}) collective-permute-start(bf16[64,2560]{1,0:T(8,128)(2,1)} %collective-permute-done.24), channel_id=1, source_target_pairs={{0,1},{1,0},{2,3},{3,2},{4,5},{5,4},{6,7},{7,6},{8,9},{9,8},{10,11... | collective-permute-start | bytes 983048 | tf_op jit(solution)/shard_map/ppermute | solution.py:49
  27.4 25.2 %collective-permute-start.7 = (bf16[160,2560]{1,0:T(8,128)(2,1)S(1)}, bf16[160,2560]{1,0:T(8,128)(2,1)S(1)}, u32[]{:S(2)}, u32[]{:S(2)}) collective-permute-start(bf16[160,2560]{1,0:T(8,128)(2,1)S(1)} %pad_maximum_fusion.1), channel_id=1, source_target_pairs={{0,8},{1,9},{2,10},{3,11},{4,12},{5,13},{6,14},{7,15},{8,0},{9,1},... | collective-permute-start | bytes 2457608 | tf_op jit(solution)/shard_map/ppermute | solution.py:49
  28.4 21.0 %collective-permute-start.3 = (bf16[160,2560]{1,0:T(8,128)(2,1)S(1)}, bf16[160,2560]{1,0:T(8,128)(2,1)S(1)}, u32[]{:S(2)}, u32[]{:S(2)}) collective-permute-start(bf16[160,2560]{1,0:T(8,128)(2,1)S(1)} %pad_maximum_fusion.1), channel_id=1, source_target_pairs={{0,2},{1,3},{2,0},{3,1},{4,6},{5,7},{6,4},{7,5},{8,10},{9,11},{10,... | collective-permute-start | bytes 2457608 | tf_op jit(solution)/shard_map/ppermute | solution.py:49
  29.9 21.1 %collective-permute-start.4 = (bf16[160,2560]{1,0:T(8,128)(2,1)S(1)}, bf16[160,2560]{1,0:T(8,128)(2,1)S(1)}, u32[]{:S(2)}, u32[]{:S(2)}) collective-permute-start(bf16[160,2560]{1,0:T(8,128)(2,1)S(1)} %pad_maximum_fusion.1), channel_id=1, source_target_pairs={{0,4},{1,5},{2,6},{3,7},{4,0},{5,1},{6,2},{7,3},{8,12},{9,13},{10,... | collective-permute-start | bytes 2457608 | tf_op jit(solution)/shard_map/ppermute | solution.py:49
  31.4 23.6 %collective-permute-start.13 = (bf16[160,2560]{1,0:T(8,128)(2,1)S(1)}, bf16[160,2560]{1,0:T(8,128)(2,1)S(1)}, u32[]{:S(2)}, u32[]{:S(2)}) collective-permute-start(bf16[160,2560]{1,0:T(8,128)(2,1)S(1)} %pad_maximum_fusion.1), channel_id=1, source_target_pairs={{8,16},{9,17},{10,18},{11,19},{12,20},{13,21},{14,22},{15,23},{16,... | collective-permute-start | bytes 2457608 | tf_op jit(solution)/shard_map/ppermute | solution.py:49
  49.4 12.4 %collective-permute-start.5 = (bf16[80,2560]{1,0:T(8,128)(2,1)S(1)}, bf16[80,2560]{1,0:T(8,128)(2,1)S(1)}, u32[]{:S(2)}, u32[]{:S(2)}) collective-permute-start(bf16[80,2560]{1,0:T(8,128)(2,1)S(1)} %slice.213), channel_id=1, source_target_pairs={{0,4},{1,5},{2,6},{3,7},{4,0},{5,1},{6,2},{7,3},{8,12},{9,13},{10,... | collective-permute-start | bytes 1228808 | tf_op jit(solution)/shard_map/ppermute | solution.py:49
  51.0 12.4 %collective-permute-start.6 = (bf16[80,2560]{1,0:T(8,128)(2,1)S(1)}, bf16[80,2560]{1,0:T(8,128)(2,1)S(1)}, u32[]{:S(2)}, u32[]{:S(2)}) collective-permute-start(bf16[80,2560]{1,0:T(8,128)(2,1)S(1)} %slice.214), channel_id=1, source_target_pairs={{0,2},{1,3},{2,0},{3,1},{4,6},{5,7},{6,4},{7,5},{8,10},{9,11},{10,... | collective-permute-start | bytes 1228808 | tf_op jit(solution)/shard_map/ppermute | solution.py:49
  52.6 33.5 %collective-permute-start.8 = (bf16[160,2560]{1,0:T(8,128)(2,1)S(1)}, bf16[160,2560]{1,0:T(8,128)(2,1)S(1)}, u32[]{:S(2)}, u32[]{:S(2)}) collective-permute-start(bf16[160,2560]{1,0:T(8,128)(2,1)S(1)} %collective-permute-done.7), channel_id=1, source_target_pairs={{0,2},{1,3},{2,0},{3,1},{4,6},{5,7},{6,4},{7,5},{8,10},{9,11},{10,... | collective-permute-start | bytes 2457608 | tf_op jit(solution)/shard_map/ppermute | solution.py:49
  53.1 33.6 %collective-permute-start.9 = (bf16[160,2560]{1,0:T(8,128)(2,1)S(1)}, bf16[160,2560]{1,0:T(8,128)(2,1)S(1)}, u32[]{:S(2)}, u32[]{:S(2)}) collective-permute-start(bf16[160,2560]{1,0:T(8,128)(2,1)S(1)} %collective-permute-done.7), channel_id=1, source_target_pairs={{0,4},{1,5},{2,6},{3,7},{4,0},{5,1},{6,2},{7,3},{8,12},{9,13},{10,... | collective-permute-start | bytes 2457608 | tf_op jit(solution)/shard_map/ppermute | solution.py:49
  55.0 10.7 %collective-permute-start.12 = (bf16[160,2560]{1,0:T(8,128)(2,1)S(1)}, bf16[160,2560]{1,0:T(8,128)(2,1)S(1)}, u32[]{:S(2)}, u32[]{:S(2)}) collective-permute-start(bf16[160,2560]{1,0:T(8,128)(2,1)S(1)} %collective-permute-done.7), channel_id=1, source_target_pairs={{8,16},{9,17},{10,18},{11,19},{12,20},{13,21},{14,22},{15,23},{16,... | collective-permute-start | bytes 2457608 | tf_op jit(solution)/shard_map/ppermute | solution.py:49
  61.8 20.7 %collective-permute-start.14 = (bf16[160,2560]{1,0:T(8,128)(2,1)S(1)}, bf16[160,2560]{1,0:T(8,128)(2,1)S(1)}, u32[]{:S(2)}, u32[]{:S(2)}) collective-permute-start(bf16[160,2560]{1,0:T(8,128)(2,1)S(1)} %collective-permute-done.13), channel_id=1, source_target_pairs={{8,0},{9,1},{10,2},{11,3},{12,4},{13,5},{14,6},{15,7},{16,24},{17,... | collective-permute-start | bytes 2457608 | tf_op jit(solution)/shard_map/ppermute | solution.py:49
  63.5 1.7 copy-start.6
  83.0 33.1 %collective-permute-start.15 = (bf16[160,2560]{1,0:T(8,128)(2,1)S(1)}, bf16[160,2560]{1,0:T(8,128)(2,1)S(1)}, u32[]{:S(2)}, u32[]{:S(2)}) collective-permute-start(bf16[160,2560]{1,0:T(8,128)(2,1)S(1)} %get-tuple-element.22), channel_id=1, source_target_pairs={{0,2},{1,3},{2,0},{3,1},{4,6},{5,7},{6,4},{7,5},{8,10},{9,11},{10,... | collective-permute-start | bytes 2457608 | tf_op jit(solution)/shard_map/ppermute | solution.py:49
  84.6 32.1 %collective-permute-start.16 = (bf16[160,2560]{1,0:T(8,128)(2,1)S(1)}, bf16[160,2560]{1,0:T(8,128)(2,1)S(1)}, u32[]{:S(2)}, u32[]{:S(2)}) collective-permute-start(bf16[160,2560]{1,0:T(8,128)(2,1)S(1)} %get-tuple-element.22), channel_id=1, source_target_pairs={{0,4},{1,5},{2,6},{3,7},{4,0},{5,1},{6,2},{7,3},{8,12},{9,13},{10,... | collective-permute-start | bytes 2457608 | tf_op jit(solution)/shard_map/ppermute | solution.py:49
  86.1 24.9 %collective-permute-start.10 = (bf16[80,2560]{1,0:T(8,128)(2,1)S(1)}, bf16[80,2560]{1,0:T(8,128)(2,1)S(1)}, u32[]{:S(2)}, u32[]{:S(2)}) collective-permute-start(bf16[80,2560]{1,0:T(8,128)(2,1)S(1)} %slice.215), channel_id=1, source_target_pairs={{0,4},{1,5},{2,6},{3,7},{4,0},{5,1},{6,2},{7,3},{8,12},{9,13},{10,... | collective-permute-start | bytes 1228808 | tf_op jit(solution)/shard_map/ppermute | solution.py:49
  86.7 24.3 %collective-permute-start.11 = (bf16[80,2560]{1,0:T(8,128)(2,1)S(1)}, bf16[80,2560]{1,0:T(8,128)(2,1)S(1)}, u32[]{:S(2)}, u32[]{:S(2)}) collective-permute-start(bf16[80,2560]{1,0:T(8,128)(2,1)S(1)} %slice.216), channel_id=1, source_target_pairs={{0,2},{1,3},{2,0},{3,1},{4,6},{5,7},{6,4},{7,5},{8,10},{9,11},{10,... | collective-permute-start | bytes 1228808 | tf_op jit(solution)/shard_map/ppermute | solution.py:49
  87.3 26.1 %collective-permute-start.19 = (bf16[160,2560]{1,0:T(8,128)(2,1)S(1)}, bf16[160,2560]{1,0:T(8,128)(2,1)S(1)}, u32[]{:S(2)}, u32[]{:S(2)}) collective-permute-start(bf16[160,2560]{1,0:T(8,128)(2,1)S(1)} %collective-permute-done.12), channel_id=1, source_target_pairs={{8,0},{9,1},{10,2},{11,3},{12,4},{13,5},{14,6},{15,7},{16,24},{17,... | collective-permute-start | bytes 2457608 | tf_op jit(solution)/shard_map/ppermute | solution.py:49
  111.1 1.7 copy-start.7
  113.9 27.8 %collective-permute-start.20 = (bf16[160,2560]{1,0:T(8,128)(2,1)S(1)}, bf16[160,2560]{1,0:T(8,128)(2,1)S(1)}, u32[]{:S(2)}, u32[]{:S(2)}) collective-permute-start(bf16[160,2560]{1,0:T(8,128)(2,1)S(1)} %get-tuple-element.20), channel_id=1, source_target_pairs={{0,2},{1,3},{2,0},{3,1},{4,6},{5,7},{6,4},{7,5},{8,10},{9,11},{10,... | collective-permute-start | bytes 2457608 | tf_op jit(solution)/shard_map/ppermute | solution.py:49
  114.5 28.8 %collective-permute-start.21 = (bf16[160,2560]{1,0:T(8,128)(2,1)S(1)}, bf16[160,2560]{1,0:T(8,128)(2,1)S(1)}, u32[]{:S(2)}, u32[]{:S(2)}) collective-permute-start(bf16[160,2560]{1,0:T(8,128)(2,1)S(1)} %get-tuple-element.20), channel_id=1, source_target_pairs={{0,4},{1,5},{2,6},{3,7},{4,0},{5,1},{6,2},{7,3},{8,12},{9,13},{10,... | collective-permute-start | bytes 2457608 | tf_op jit(solution)/shard_map/ppermute | solution.py:49
  116.1 23.8 %collective-permute-start.17 = (bf16[80,2560]{1,0:T(8,128)(2,1)S(1)}, bf16[80,2560]{1,0:T(8,128)(2,1)S(1)}, u32[]{:S(2)}, u32[]{:S(2)}) collective-permute-start(bf16[80,2560]{1,0:T(8,128)(2,1)S(1)} %slice.217), channel_id=1, source_target_pairs={{0,4},{1,5},{2,6},{3,7},{4,0},{5,1},{6,2},{7,3},{8,12},{9,13},{10,... | collective-permute-start | bytes 1228808 | tf_op jit(solution)/shard_map/ppermute | solution.py:49
  116.7 23.2 %collective-permute-start.18 = (bf16[80,2560]{1,0:T(8,128)(2,1)S(1)}, bf16[80,2560]{1,0:T(8,128)(2,1)S(1)}, u32[]{:S(2)}, u32[]{:S(2)}) collective-permute-start(bf16[80,2560]{1,0:T(8,128)(2,1)S(1)} %slice.218), channel_id=1, source_target_pairs={{0,2},{1,3},{2,0},{3,1},{4,6},{5,7},{6,4},{7,5},{8,10},{9,11},{10,... | collective-permute-start | bytes 1228808 | tf_op jit(solution)/shard_map/ppermute | solution.py:49
  140.0 1.7 copy-start.4
  141.8 8.0 %collective-permute-start.22 = (bf16[80,2560]{1,0:T(8,128)(2,1)S(1)}, bf16[80,2560]{1,0:T(8,128)(2,1)S(1)}, u32[]{:S(2)}, u32[]{:S(2)}) collective-permute-start(bf16[80,2560]{1,0:T(8,128)(2,1)S(1)} %slice.219), channel_id=1, source_target_pairs={{0,4},{1,5},{2,6},{3,7},{4,0},{5,1},{6,2},{7,3},{8,12},{9,13},{10,... | collective-permute-start | bytes 1228808 | tf_op jit(solution)/shard_map/ppermute | solution.py:49
  143.4 8.0 %collective-permute-start.23 = (bf16[80,2560]{1,0:T(8,128)(2,1)S(1)}, bf16[80,2560]{1,0:T(8,128)(2,1)S(1)}, u32[]{:S(2)}, u32[]{:S(2)}) collective-permute-start(bf16[80,2560]{1,0:T(8,128)(2,1)S(1)} %slice.220), channel_id=1, source_target_pairs={{0,2},{1,3},{2,0},{3,1},{4,6},{5,7},{6,4},{7,5},{8,10},{9,11},{10,... | collective-permute-start | bytes 1228808 | tf_op jit(solution)/shard_map/ppermute | solution.py:49
  151.5 2.7 %copy-start.2 = (bf16[4,160,2560]{2,1,0:T(8,128)(2,1)}, bf16[4,160,2560]{2,1,0:T(8,128)(2,1)S(1)}, u32[]{:S(2)}) copy-start(bf16[4,160,2560]{2,1,0:T(8,128)(2,1)S(1)} %fusion.20) | copy-start | bytes 9830404
  154.2 3.7 %copy-start.10 = (f32[128,2560]{1,0:T(8,128)}, f32[128,2560]{1,0:T(8,128)S(1)}, u32[]{:S(2)}) copy-start(f32[128,2560]{1,0:T(8,128)S(1)} %convolution_add_fusion.3.refs_0_.refs_1_) | copy-start | bytes 3932164
  154.4 1.2 collective-permute-start.27
  170.6 1.2 collective-permute-start.28
  173.1 4.5 %copy-start.11 = (bf16[128,1280]{1,0:T(8,128)(2,1)}, bf16[128,1280]{1,0:T(8,128)(2,1)S(1)}, u32[]{:S(2)}) copy-start(bf16[128,1280]{1,0:T(8,128)(2,1)S(1)} %fusion.26.refs_10_) | copy-start | bytes 983044
  173.1 1.7 collective-permute-start.29
  174.8 2.9 %copy-start.8 = (bf16[4,160,2560]{2,1,0:T(8,128)(2,1)S(1)}, bf16[4,160,2560]{2,1,0:T(8,128)(2,1)}, u32[]{:S(2)}) copy-start(bf16[4,160,2560]{2,1,0:T(8,128)(2,1)} %copy-done.7) | copy-start | bytes 9830404
  177.7 1.9 copy-start.5
  179.7 1.9 copy-start.3
  182.3 2.9 %copy-start.9 = (f32[128,2560]{1,0:T(8,128)}, f32[128,2560]{1,0:T(8,128)S(1)}, u32[]{:S(2)}) copy-start(f32[128,2560]{1,0:T(8,128)S(1)} %convolution_add_fusion.refs_0_.refs_1_) | copy-start | bytes 3932164
  182.5 1.2 collective-permute-start.30
  196.2 1.5 collective-permute-start.31

commit v2 on v1

v2 whole, which is shorter than its diff:
```python
import functools
import math

import jax
import jax.numpy as jnp
from jax import lax
from jax.experimental import pallas as pl
from jax.experimental.pallas import tpu as pltpu
from jax.sharding import PartitionSpec as P


HEAD_DIM = 128
STEPS = 2
LAGS = 2
LEVELS = 1000

SIGMA_SHIFT = 5.0
EPSILON = 1e-06
MASKED = -1e30
AXIS = "fsdp"


def sigma_of(levels):
    fraction = levels.astype(jnp.float32) / LEVELS
    return SIGMA_SHIFT * fraction / (1.0 + (SIGMA_SHIFT - 1.0) * fraction)


def frequencies(half_count):
    return jnp.exp(-math.log(10000.0) * jnp.arange(half_count, dtype=jnp.float32) / half_count)


def modulation(sigmas, time_proj):
    half_count = time_proj.shape[0] // 2
    angles = 1000.0 * sigmas[:, None] * frequencies(half_count)[None, :]
    features = jnp.concatenate([jnp.cos(angles), jnp.sin(angles)], axis=1).astype(jnp.bfloat16)
    return jnp.dot(features, time_proj, preferred_element_type=jnp.float32)


def modulate(latent, shift, scale):
    parts = shift.shape[0]
    values = latent.astype(jnp.float32).reshape(parts, -1, latent.shape[1])
    centred = values - jnp.mean(values, axis=-1, keepdims=True)
    variance = jnp.mean(centred * centred, axis=-1, keepdims=True)
    normed = centred * lax.rsqrt(variance + EPSILON)
    result = normed * (1.0 + scale[:, None, :]) + shift[:, None, :]
    return result.astype(jnp.bfloat16).reshape(latent.shape)


def permute(value, target_of):
    pairs = [(s, target_of(s)) for s in range(lax.axis_size(AXIS))]
    return lax.ppermute(value, AXIS, [(s, t) for s, t in pairs if t is not None])


def swap_core(value):
    return permute(value, lambda s: s ^ 1)


def swap_x(value):
    return permute(value, lambda s: s ^ 2)


def swap_y(value):
    return permute(value, lambda s: s ^ 4)


def swap_z_pair(value):
    return permute(value, lambda s: s ^ 8)


def swap_z_middle(value):
    return permute(value, lambda s: {1: s + 8, 2: s - 8}.get(s // 8))


def z_outward(value):
    return permute(value, lambda s: {1: s - 8, 2: s + 8}.get(s // 8))


def across_plane(value):
    half = value.shape[0] // 2
    from_x = swap_x(value)
    from_y = swap_y(value)
    low, high = from_x[:half], from_y[half:]
    return [value, from_x, from_y, swap_y(low), swap_x(high)]


def across_plane_in_halves(value):
    half = value.shape[0] // 2
    low, high = value[:half], value[half:]
    low_x = swap_x(low)
    high_y = swap_y(high)
    high_x = swap_x(high)
    low_y = swap_y(low)
    return [value, low_x, high_x, low_y, high_y, swap_y(low_x), swap_x(high_y)]


def gather_block(unit, device):
    z = device // 8
    place = (device // 2) % 4
    middle = (z == 1) | (z == 2)
    pair = swap_z_pair(unit)
    across = swap_z_middle(unit)
    two_mid = swap_z_middle(pair)
    two_end = z_outward(across)
    second = jnp.where(middle, two_mid, two_end)
    three_end = z_outward(second)
    third = jnp.where(middle, across, three_end)
    slots = [unit, pair, second, third]
    pieces = [across_plane(slot) for slot in slots[:3]]
    pieces.append(across_plane_in_halves(third))
    rows = unit.shape[0]
    halves = [[(i, 0, rows // 2), (i, rows // 2, rows // 2)] for i in range(4)]
    spots = [[(0, 0, rows), (1, 0, rows), (2, 0, rows)] + halves[3]] * 3
    spots.append([(0, 0, rows)] + halves[1] + halves[2] + halves[3])
    return [z ^ step for step in range(4)], place, pieces, spots


def gather_any(unit, device):
    size = lax.axis_size(AXIS)
    groups = [list(range(core, size, 2)) for core in range(2)]
    whole = lax.all_gather(unit, AXIS, axis=0, tiled=True, axis_index_groups=groups)
    none = jnp.int32(0)
    return [none], none, [[whole]], [[(0, 0, whole.shape[0])]]


def absorb_body(spots, step, has_sum, last, places_ref, hidden_ref, *refs):
    count = len(spots)
    piece_refs, refs = refs[:count], refs[count:]
    if has_sum:
        raw_in_ref, past_in_ref, *refs = refs
    plane_out_ref, raw_ref, past_ref, *refs = refs
    if last:
        sum_ref, *refs = refs
    plane_ref, sems, out_sem = refs
    place = places_ref[places_ref.shape[0] - 2]
    copies = []
    for i, (other, start, size) in enumerate(spots):
        target = plane_ref.at[jnp.bitwise_xor(place, other), pl.ds(start, size), :]
        copies.append(pltpu.make_async_copy(piece_refs[i], target, sems.at[i]))
    for copy in copies:
        copy.start()
    for copy in copies:
        copy.wait()
    out = pltpu.make_async_copy(plane_ref, plane_out_ref, out_sem)
    out.start()
    weights = plane_ref[...].reshape(-1, plane_ref.shape[2])
    hidden = hidden_ref[places_ref[step]]
    rows, split = raw_ref.shape[0], weights.shape[1] // 2
    raw = jnp.dot(hidden[:rows], weights, preferred_element_type=jnp.float32)
    past = jnp.dot(hidden[rows:], weights[:, split:], preferred_element_type=jnp.float32)
    if has_sum:
        raw = raw + raw_in_ref[...]
        past = past + past_in_ref[...]
    raw_ref[...] = raw
    past_ref[...] = past
    if last:
        at = 0
        for side in (raw[:, :split], raw[:, split:], past):
            count = side.shape[0]
            total = jnp.sum(side * side, -1, keepdims=True)
            sum_ref[at : at + count] = jnp.broadcast_to(total, (count, HEAD_DIM))
            at += count
    out.wait()


def absorb(step, last, places, hidden, pieces, spots, chips, rows, sums):
    hbm = pl.BlockSpec(memory_space=pltpu.HBM)
    vmem = pl.BlockSpec(memory_space=pltpu.VMEM)
    width = pieces[0].shape[1]
    chip_rows = hidden.shape[2] // chips
    past_rows = hidden.shape[1] - rows
    operands = [places, hidden, *pieces, *sums]
    specs = [pl.BlockSpec(memory_space=pltpu.SMEM), vmem] + [hbm] * len(pieces)
    specs += [vmem] * len(sums)
    shapes = [
        pltpu.HBM((chips, chip_rows, width), jnp.bfloat16),
        jax.ShapeDtypeStruct((rows, width), jnp.float32),
        jax.ShapeDtypeStruct((past_rows, width // 2), jnp.float32),
    ]
    outs = [hbm, vmem, vmem]
    if last:
        shapes.append(jax.ShapeDtypeStruct((2 * rows + past_rows, HEAD_DIM), jnp.float32))
        outs.append(vmem)
    return pl.pallas_call(
        functools.partial(absorb_body, spots, step, bool(sums), last),
        in_specs=specs,
        out_specs=outs,
        out_shape=shapes,
        scratch_shapes=[
            pltpu.VMEM((chips, chip_rows, width), jnp.bfloat16),
            pltpu.SemaphoreType.DMA((len(pieces),)),
            pltpu.SemaphoreType.DMA,
        ],
        compiler_params=pltpu.CompilerParams(vmem_limit_bytes=16 << 20),
        name="absorb",
    )(*operands)


def turn(values, cosine, sine):
    return values * cosine + pltpu.roll(values, HEAD_DIM // 2, 1) * sine


def attend_body(first, inner, *refs):
    (raw_ref, own_sum_ref, other_sum_ref, q_gain_ref, k_gain_ref, cos_ref, sin_ref,
     usable_ref, v_ref, past_v_ref, latent_ref, factor_ref, *refs) = refs
    if first:
        past_ref, out_ref, past_key_ref = refs
    else:
        past_key_ref, out_ref = refs
    rows, width = latent_ref.shape
    extra = past_v_ref.shape[0]
    heads = width // HEAD_DIM
    scale = lax.rsqrt((own_sum_ref[...] + other_sum_ref[...]) / inner + EPSILON)
    q_scale, k_scale = scale[:rows], scale[rows : 2 * rows]
    turned = slice(extra - rows // 2, extra + rows // 2)
    own_cos, own_sin = cos_ref[turned, :], sin_ref[turned, :]

    def per_row(pair):
        rows_of = [jnp.broadcast_to(pair[i : i + 1], (rows // 2, pair.shape[1])) for i in range(2)]
        return jnp.concatenate(rows_of, axis=0)

    allowed = per_row(usable_ref[...]) > 0.0
    for head in range(heads):
        at = slice(head * HEAD_DIM, (head + 1) * HEAD_DIM)
        key_at = slice(width + at.start, width + at.stop)
        query = raw_ref[:, at] * q_scale * q_gain_ref[:, at]
        query = turn(query, own_cos, own_sin).astype(jnp.bfloat16)
        key = raw_ref[:, key_at] * k_scale * k_gain_ref[:, at]
        key = turn(key, own_cos, own_sin).astype(jnp.bfloat16)
        if first:
            past = past_ref[:, at] * scale[2 * rows :] * k_gain_ref[:, at]
            past = turn(past, cos_ref[:extra, :], sin_ref[:extra, :]).astype(jnp.bfloat16)
            past_key_ref[:, at] = past
        else:
            past = past_key_ref[:, at]
        keys = jnp.concatenate([key, past], axis=0)
        values = jnp.concatenate([v_ref[:, at], past_v_ref[:, at]], axis=0)
        scores = lax.dot_general(
            query, keys, (((1,), (1,)), ((), ())), preferred_element_type=jnp.float32
        ) * HEAD_DIM ** (-0.5)
        scores = jnp.where(allowed, scores, MASKED)
        expanded = jnp.exp(scores - jnp.max(scores, axis=-1, keepdims=True))
        weights = (expanded / jnp.sum(expanded, axis=-1, keepdims=True)).astype(jnp.bfloat16)
        mixed = jnp.dot(weights, values, preferred_element_type=jnp.float32).astype(jnp.bfloat16)
        step = per_row(factor_ref[:, at]) * mixed.astype(jnp.float32)
        out_ref[:, at] = (latent_ref[:, at].astype(jnp.float32) + step).astype(jnp.bfloat16)


def attend(first, inner, raw, sums, others, gains, tables, fixed, latent, factor, past):
    shapes = [jax.ShapeDtypeStruct(latent.shape, jnp.bfloat16)]
    if first:
        shapes.append(jax.ShapeDtypeStruct(past.shape, jnp.bfloat16))
    return pl.pallas_call(
        functools.partial(attend_body, first, inner),
        out_shape=shapes,
        compiler_params=pltpu.CompilerParams(vmem_limit_bytes=16 << 20),
        name="attend",
    )(raw, sums, others, *gains, *tables, *fixed, latent, factor, past)


def project_body(places_ref, own_ref, other_ref, mod_ref, *refs):
    count = len(refs) - 6
    plane_refs = refs[:count]
    raw_ref, sum_ref, value_ref, hidden_ref, weight_ref, sems = refs[count:]
    rows, half = own_ref.shape
    parts, _, part_width = hidden_ref.shape
    copies = [
        pltpu.make_async_copy(ref, weight_ref.at[i], sems.at[i])
        for i, ref in enumerate(plane_refs)
    ]
    for copy in copies:
        copy.start()
    is_low = places_ref[count + 1] == 0
    own, other = own_ref[...].astype(jnp.float32), other_ref[...].astype(jnp.float32)
    low, high = jnp.where(is_low, own, other), jnp.where(is_low, other, own)
    width = 2 * half
    mean = (jnp.sum(low, -1, keepdims=True) + jnp.sum(high, -1, keepdims=True)) / width
    low, high = low - mean, high - mean
    variance = (
        jnp.sum(low * low, -1, keepdims=True) + jnp.sum(high * high, -1, keepdims=True)
    ) / width
    scale = lax.rsqrt(variance + EPSILON)
    sides = []
    for side, centred in enumerate((low, high)):
        normed = centred * scale
        at = slice(side * half, (side + 1) * half)
        gain_at = slice(width + side * half, width + (side + 1) * half)
        pieces = []
        for span in range(2):
            piece = normed[span * (rows // 2) : (span + 1) * (rows // 2)]
            row = slice(3 + span, 4 + span)
            pieces.append(piece * (1.0 + mod_ref[row, gain_at]) + mod_ref[row, at])
        sides.append(jnp.concatenate(pieces, axis=0).astype(jnp.bfloat16))
    value_ref[...] = jnp.where(is_low, sides[0], sides[1])
    for i in range(parts):
        for side in range(2):
            if parts == 1:
                hidden_ref[0, :, side * half : (side + 1) * half] = sides[side]
            elif i * part_width // half == side:
                at = i * part_width - side * half
                hidden_ref[i] = sides[side][:, at : at + part_width]
    total = None
    for i, copy in enumerate(copies):
        copy.wait()
        weights = weight_ref[i].reshape(-1, weight_ref.shape[-1])
        part = jnp.dot(hidden_ref[places_ref[i]], weights, preferred_element_type=jnp.float32)
        total = part if total is None else total + part
    raw_ref[...] = total
    for i in range(2):
        side = total[:, i * half : (i + 1) * half]
        square = jnp.sum(side * side, -1, keepdims=True)
        sum_ref[i * rows : (i + 1) * rows] = jnp.broadcast_to(square, (rows, HEAD_DIM))


def project_latent(places, own, other, mods, planes):
    rows, half = own.shape
    count = len(planes)
    planes = [pltpu.with_memory_space_constraint(plane, pltpu.HBM) for plane in planes]
    vmem = pl.BlockSpec(memory_space=pltpu.VMEM)
    hbm = pl.BlockSpec(memory_space=pltpu.HBM)
    return pl.pallas_call(
        project_body,
        in_specs=[pl.BlockSpec(memory_space=pltpu.SMEM)] + [vmem] * 3 + [hbm] * count,
        out_shape=[
            jax.ShapeDtypeStruct((rows, planes[0].shape[-1]), jnp.float32),
            jax.ShapeDtypeStruct((2 * rows, HEAD_DIM), jnp.float32),
            jax.ShapeDtypeStruct((rows, half), jnp.bfloat16),
        ],
        scratch_shapes=[
            pltpu.VMEM((count, rows, 2 * half // count), jnp.bfloat16),
            pltpu.VMEM((count,) + planes[0].shape, jnp.bfloat16),
            pltpu.SemaphoreType.DMA((count,)),
        ],
        compiler_params=pltpu.CompilerParams(vmem_limit_bytes=24 << 20),
        name="project",
    )(places, own, other, mods, *planes)


def denoise(noisy, clean, seg_ids, lag_mask, plan, w_query, w_key, time_proj, q_gain, k_gain):
    rows, width = noisy.shape
    inner = w_query.shape[1]
    half = inner // 2
    devices = lax.axis_size(AXIS)
    device = lax.axis_index(AXIS)
    core = device % 2
    first_span = device - core
    is_low = core == 0

    def mine(value, axis):
        return lax.dynamic_slice_in_dim(value, core * half, half, axis)

    def theirs(value, axis):
        return lax.dynamic_slice_in_dim(value, (1 - core) * half, half, axis)

    def in_order(own, other, axis):
        low = jnp.where(is_low, own, other)
        high = jnp.where(is_low, other, own)
        return jnp.concatenate([low, high], axis=axis)

    before = permute(clean, lambda s: s + 2 if s + 2 < devices else None)
    others = swap_core(clean)

    own_rows = jnp.concatenate([mine(w_query, 1), mine(w_key, 1)], axis=1)
    sent_rows = jnp.concatenate([theirs(w_query, 1), theirs(w_key, 1)], axis=1)
    unit = in_order(own_rows, swap_core(sent_rows), 0)
    unit, noisy, seg_ids, plan, lag_mask, time_proj = lax.optimization_barrier(
        (unit, noisy, seg_ids, plan, lag_mask, time_proj)
    )
    gather = gather_block if devices == 32 else gather_any
    plane_ids, place, pieces, spots = gather(unit, device)
    noisy_both = in_order(noisy, swap_core(noisy), 0)
    small = jnp.concatenate([plan, lag_mask], axis=1)
    small_both = in_order(small, swap_core(small), 0)
    plan_both, lags_both = small_both[:, :STEPS], small_both[:, STEPS:]
    sigmas = [sigma_of(plan_both[:, j]) for j in range(STEPS)] + [jnp.zeros((2,), jnp.float32)]
    mods = modulation(jnp.concatenate([jnp.zeros((1,), jnp.float32)] + sigmas[:STEPS]), time_proj)
    step_mods = [mods[1 + 2 * j : 3 + 2 * j] for j in range(STEPS)]
    hidden = modulate(noisy_both, step_mods[0][:, :width], step_mods[0][:, width : 2 * width])
    latent = mine(noisy_both, 1)
    values = mine(hidden, 1)

    before_both = in_order(before, swap_core(before), 0)
    past_clean = jnp.concatenate([before_both, jnp.where(is_low, clean, others)], axis=0)
    past_hidden = modulate(past_clean, mods[:1, :width], mods[:1, width : 2 * width])
    past_values = mine(past_hidden, 1)
    stack = jnp.concatenate([hidden, past_hidden], axis=0)
    stack = stack.reshape(stack.shape[0], len(plane_ids), -1).swapaxes(0, 1)
    places = jnp.stack(plane_ids + [place, core]).astype(jnp.int32)

    factors = [
        (sigmas[j + 1] - sigmas[j])[:, None] * mine(step_mods[j][:, 2 * width :], 1)
        for j in range(STEPS)
    ]
    gains = (mine(q_gain, 0)[None, :], mine(k_gain, 0)[None, :])
    spans = jnp.maximum(first_span - 2 + jnp.arange(4, dtype=jnp.int32), 0)
    segments = seg_ids[spans]
    starts = jnp.sum((seg_ids[None, :] < segments[:, None]).astype(jnp.int32), axis=1)
    positions = (
        (spans - starts)[:, None] * rows + jnp.arange(rows, dtype=jnp.int32)[None, :]
    ).astype(jnp.float32).reshape(-1, 1)
    angles = positions * frequencies(HEAD_DIM // 2)[None, :]
    cosine = jnp.concatenate([jnp.cos(angles)] * 2, axis=1)
    sine = jnp.concatenate([-jnp.sin(angles), jnp.sin(angles)], axis=1)
    tables = (cosine, sine)
    block = jnp.arange(5 * rows, dtype=jnp.int32)[None, :] // rows
    here = jnp.arange(2, dtype=jnp.int32)[:, None]
    usable = block == here
    for lag in range(1, LAGS + 1):
        allowed = (
            (first_span + here >= lag)
            & (segments[2 - lag : 4 - lag] == segments[2:])[:, None]
            & (lags_both[:, lag - 1 : lag] == 1)
        )
        usable = usable | (allowed & (block == here + 4 - lag))
    usable = usable.astype(jnp.float32)

    chips = 4 if len(pieces) == 4 else 1
    sums, planes = [], []
    for step, parts in enumerate(pieces):
        last = step + 1 == len(pieces)
        plane, *sums = absorb(step, last, places, stack, parts, spots[step], chips, 2 * rows, sums)
        planes.append(plane)
    raw, past_raw, sums = sums
    latent, past_key = attend(
        True, inner, raw, sums, swap_core(sums), gains, tables, (usable, values, past_values),
        latent, factors[0], past_raw,
    )
    raw, sums, values = project_latent(places, latent, swap_core(latent), mods, planes)
    (latent,) = attend(
        False, inner, raw, sums, swap_core(sums), gains, tables, (usable, values, past_values),
        latent, factors[1], past_key,
    )
    kept = lax.dynamic_slice_in_dim(latent, core * rows, rows, 0)
    sent = lax.dynamic_slice_in_dim(latent, (1 - core) * rows, rows, 0)
    return in_order(kept, swap_core(sent), 1)


def solution(mesh):
    placed = (
        P(("pool", "fsdp"), None),
        P(("pool", "fsdp"), None),
        P("pool"),
        P(("pool", "fsdp"), None),
        P(("pool", "fsdp"), None),
        P("fsdp", None),
        P("fsdp", None),
        P(),
        P(),
        P(),
    )
    return jax.shard_map(
        denoise, mesh=mesh, in_specs=placed, out_specs=P(("pool", "fsdp"), None), check_vma=False
    )
```

time: 201 us -> 182 us (0.905)
  matrix products: 11.7 us -> 0.41 us
  Pallas kernels: 20.4 us -> 28.3 us
  between operations: 8.14 us -> 0.55 us
  local copies, waits for them, and re-layouts: 18.5 us -> 11.4 us
  starting transfers between devices: 32.8 us -> 37.5 us
  other arithmetic: 15.6 us -> 11.3 us
    dot_general x12 -> x0, matrix products: 11.3 us -> none  [project(): jnp.dot(part, weights[:, columns], preferred_element_type=jnp.float32)]
    pallas_call x2 -> x7, Pallas kernels: 20.4 us -> 28.3 us  [the longest x4 14.3 us: absorb(): pl.pallas_call(functools.partial(absorb_body, spots, step, bool(sums), la...]
    ppermute x32 -> x33, starting transfers between devices: 32.8 us -> 37.5 us  [permute(): lax.ppermute(value, AXIS, [(s, t) for s, t in pairs if t is not None])]
    unnamed x34 -> x40, local copies, waits for them, and re-layouts: 5.08 us -> 0.86 us
    add x0 -> x4, local copies, waits for them, and re-layouts: none -> 3.95 us  [modulate(): result = normed * (1.0 + scale[:, None, :]) + shift[:, None, :]]
    reduce_sum x7 -> x1, other arithmetic: 3.56 us -> 0.18 us  [denoise(): jnp.sum((seg_ids[None, :] < segments[:, None]).astype(jnp.int32), axis=1)]
    slice x18 -> x7, local copies, waits for them, and re-layouts: 5.24 us -> 2.23 us  [the longest x6 2.17 us: across_plane(): low, high = (from_x[:half], from_y[half:])]
    ppermute x32 -> x33, waiting for transfers between devices: 92.1 us -> 92.3 us  [permute(): lax.ppermute(value, AXIS, [(s, t) for s, t in pairs if t is not None])]
  transfers between devices with their start and end apart: 32 -> 33, of which waited for: 13 -> 16; matrix products, arithmetic and copies ran while one was open for 11% -> 12% of each run, Pallas kernels for 0% -> 6%
where the time goes in v2:
time: 182 us
  waiting for transfers between devices  92.3 us (51%)
  starting transfers between devices  37.5 us (21%)
  Pallas kernels  28.3 us (16%)
  local copies, waits for them, and re-layouts  11.4 us (6%)
  other arithmetic  11.3 us (6%)
    ppermute x33, waiting for transfers between devices, permute(): lax.ppermute(value, AXIS, [(s, t) for s, t in pairs if t is not None])  92.3 us
    ppermute x33, starting transfers between devices, permute(): lax.ppermute(value, AXIS, [(s, t) for s, t in pairs if t is not None])  37.5 us
    pallas_call x4, Pallas kernels, absorb(): pl.pallas_call(functools.partial(absorb_body, spots, step, bool(sums), la...  14.3 us
    pallas_call x2, Pallas kernels, attend(): pl.pallas_call(functools.partial(attend_body, first, inner), out_shape=sh...  7.81 us
    pallas_call x1, Pallas kernels, project_latent(): pl.pallas_call(project_body, in_specs=[pl.BlockSpec(memory_space=pltpu.SM...  6.13 us
    add x4, local copies, waits for them, and re-layouts, modulate(): result = normed * (1.0 + scale[:, None, :]) + shift[:, None, :]  3.95 us
  transfers between devices with their start and end apart: 33, of which 16 were waited for; matrix products, arithmetic and copies ran while one was open for 12% of the time, Pallas kernels for 6%

profile of v2, /device:TPU:0, one launch (start us, length us, event | category | flops | bytes accessed | tf_op | source)
XLA Modules:
  0.0 181.8 jit_solution(6796232579997411887)
XLA Ops:
  0.0 5.8 %collective-permute-start.3 = (bf16[64,2560]{1,0:T(8,128)(2,1)}, bf16[64,2560]{1,0:T(8,128)(2,1)}, u32[]{:S(2)}, u32[]{:S(2)}) collective-permute-start(bf16[64,2560]{1,0:T(8,128)(2,1)} %param.11), channel_id=1, source_target_pairs={{0,2},{1,3},{2,4},{3,5},{4,6},{5,7},{6,8},{7,9},{8,10},{9,11},{10,... | collective-permute-start | bytes 983048 | tf_op jit(solution)/shard_map/ppermute | solution.py:51
  5.8 1.3 constant_dynamic-slice_fusion.3
  7.1 0.6 collective-permute-start
  7.7 0.6 multiply_exponential_fusion
  8.2 0.6 iota_add_fusion
  9.1 3.2 %collective-permute-done.3 = bf16[64,2560]{1,0:T(8,128)(2,1)} collective-permute-done((bf16[64,2560]{1,0:T(8,128)(2,1)}, bf16[64,2560]{1,0:T(8,128)(2,1)}, u32[]{:S(2)}, u32[]{:S(2)}) %collective-permute-start.3) | collective-permute-done | bytes 327712 | tf_op jit(solution)/shard_map/ppermute | solution.py:51
  12.3 1.0 broadcast_select_fusion.4
  13.6 3.5 %collective-permute-start.26 = (bf16[160,2560]{1,0:T(8,128)(2,1)S(1)}, bf16[160,2560]{1,0:T(8,128)(2,1)}, u32[]{:S(2)}, u32[]{:S(2)}) collective-permute-start(bf16[160,2560]{1,0:T(8,128)(2,1)S(1)} %pad_maximum_fusion.1.refs_0_), channel_id=1, source_target_pairs={{0,4},{1,5},{2,6},{3,7},{4,0},{5,1},{6,2},{7,3},{8,12},{9,13},{10,... | collective-permute-start | bytes 2457608 | tf_op jit(solution)/shard_map/ppermute | solution.py:51
  17.1 0.6 collective-permute-start.25
  17.6 1.6 collective-permute-start.7
  19.2 0.6 gather_fusion
  21.0 0.8 pad_maximum_fusion.6.refs_5_
  21.7 0.7 pad_maximum_fusion.7.refs_6_
  22.5 1.6 collective-permute-start.6
  25.4 1.6 mul.217
  26.9 1.2 add.216
  28.1 2.7 %add.217 = f32[128,4,640]{2,1,0:T(4,128)} reshape(f32[2,64,2560]{2,1,0:T(8,128)} %add.216) | data formatting | bytes 2621440 | tf_op jit(solution)/shard_map/add | solution.py:45
  30.9 0.6 collective-permute-start.1
  31.5 1.1 broadcast_select_fusion.6
  33.4 4.5 %collective-permute-done.7.refs_0_ = bf16[160,2560]{1,0:T(8,128)(2,1)} collective-permute-done((bf16[160,2560]{1,0:T(8,128)(2,1)S(1)}, bf16[160,2560]{1,0:T(8,128)(2,1)}, u32[]{:S(2)}, u32[]{:S(2)}) %collective-permute-start.7) | collective-permute-done | bytes 819232 | tf_op jit(solution)/shard_map/ppermute | solution.py:51
  37.8 0.7 collective-permute-start.8
  38.6 1.3 collective-permute-start.9
  40.6 1.0 collective-permute-start.22
  41.6 24.8 %collective-permute-done.9 = bf16[160,2560]{1,0:T(8,128)(2,1)S(1)} collective-permute-done((bf16[160,2560]{1,0:T(8,128)(2,1)}, bf16[160,2560]{1,0:T(8,128)(2,1)S(1)}, u32[]{:S(2)}, u32[]{:S(2)}) %collective-permute-start.9) | collective-permute-done | bytes 819232 | tf_op jit(solution)/shard_map/ppermute | solution.py:51
  66.3 1.4 collective-permute-start.21
  67.9 1.3 collective-permute-start.10
  69.2 1.1 broadcast_select_fusion.8
  70.8 1.5 collective-permute-start.18
  72.3 1.0 slice.110
  73.4 1.0 slice.109
  74.5 1.3 collective-permute-start.27
  75.8 11.9 %collective-permute-done.21.refs_1_ = bf16[160,2560]{1,0:T(8,128)(2,1)S(1)} collective-permute-done((bf16[160,2560]{1,0:T(8,128)(2,1)}, bf16[160,2560]{1,0:T(8,128)(2,1)S(1)}, u32[]{:S(2)}, u32[]{:S(2)}) %collective-permute-start.21) | collective-permute-done | bytes 819232 | tf_op jit(solution)/shard_map/ppermute | solution.py:51
  87.7 1.4 collective-permute-start.17
  89.1 0.7 collective-permute-start.24
  89.9 2.0 %collective-permute-done.18.refs_2_ = bf16[160,2560]{1,0:T(8,128)(2,1)S(1)} collective-permute-done((bf16[160,2560]{1,0:T(8,128)(2,1)S(1)}, bf16[160,2560]{1,0:T(8,128)(2,1)S(1)}, u32[]{:S(2)}, u32[]{:S(2)}) %collective-permute-start.18) | collective-permute-done | bytes 819232 | tf_op jit(solution)/shard_map/ppermute | solution.py:51
  91.9 1.4 collective-permute-start.23
  93.4 3.0 %collective-permute-done.28.refs_4_ = bf16[80,2560]{1,0:T(8,128)(2,1)S(1)} collective-permute-done((bf16[80,2560]{1,0:T(8,128)(2,1)S(1)}, bf16[80,2560]{1,0:T(8,128)(2,1)S(1)}, u32[]{:S(2)}, u32[]{:S(2)}) %collective-permute-start.28) | collective-permute-done | bytes 409632 | tf_op jit(solution)/shard_map/ppermute | solution.py:51
  96.4 1.4 collective-permute-start.20
  97.9 2.8 %collective-permute-done.27.refs_3_ = bf16[80,2560]{1,0:T(8,128)(2,1)S(1)} collective-permute-done((bf16[80,2560]{1,0:T(8,128)(2,1)S(1)}, bf16[80,2560]{1,0:T(8,128)(2,1)S(1)}, u32[]{:S(2)}, u32[]{:S(2)}) %collective-permute-start.27) | collective-permute-done | bytes 409632 | tf_op jit(solution)/shard_map/ppermute | solution.py:51
  100.7 1.4 collective-permute-start.14
  102.1 11.9 %collective-permute-done.17.refs_1_ = bf16[160,2560]{1,0:T(8,128)(2,1)S(1)} collective-permute-done((bf16[160,2560]{1,0:T(8,128)(2,1)S(1)}, bf16[160,2560]{1,0:T(8,128)(2,1)S(1)}, u32[]{:S(2)}, u32[]{:S(2)}) %collective-permute-start.17) | collective-permute-done | bytes 819232 | tf_op jit(solution)/shard_map/ppermute | solution.py:51
  114.0 1.4 collective-permute-start.11
  116.2 6.6 %collective-permute-done.24.refs_4_ = bf16[80,2560]{1,0:T(8,128)(2,1)S(1)} collective-permute-done((bf16[80,2560]{1,0:T(8,128)(2,1)S(1)}, bf16[80,2560]{1,0:T(8,128)(2,1)S(1)}, u32[]{:S(2)}, u32[]{:S(2)}) %collective-permute-start.24) | collective-permute-done | bytes 409632 | tf_op jit(solution)/shard_map/ppermute | solution.py:51
  122.8 1.4 collective-permute-start.12
  124.2 1.4 collective-permute-start.13
  125.6 5.9 %collective-permute-done.20.refs_4_ = bf16[80,2560]{1,0:T(8,128)(2,1)S(1)} collective-permute-done((bf16[80,2560]{1,0:T(8,128)(2,1)S(1)}, bf16[80,2560]{1,0:T(8,128)(2,1)S(1)}, u32[]{:S(2)}, u32[]{:S(2)}) %collective-permute-start.20) | collective-permute-done | bytes 409632 | tf_op jit(solution)/shard_map/ppermute | solution.py:51
  131.6 0.8 collective-permute-start.19
  132.4 2.0 %collective-permute-start.16 = (bf16[80,2560]{1,0:T(8,128)(2,1)S(1)}, bf16[80,2560]{1,0:T(8,128)(2,1)S(1)}, u32[]{:S(2)}, u32[]{:S(2)}) collective-permute-start(bf16[80,2560]{1,0:T(8,128)(2,1)S(1)} %collective-permute-done.14.refs_4_), channel_id=1, source_target_pairs={{0,2},{1,3},{2,0},{3,1},{4,6},{5,7},{6,4},{7,5},{8,10},{9,11},{10,... | collective-permute-start | bytes 1228808 | tf_op jit(solution)/shard_map/ppermute | solution.py:51
  134.4 5.9 %collective-permute-done.11.refs_1_ = bf16[80,2560]{1,0:T(8,128)(2,1)S(1)} collective-permute-done((bf16[80,2560]{1,0:T(8,128)(2,1)S(1)}, bf16[80,2560]{1,0:T(8,128)(2,1)S(1)}, u32[]{:S(2)}, u32[]{:S(2)}) %collective-permute-start.11) | collective-permute-done | bytes 409632 | tf_op jit(solution)/shard_map/ppermute | solution.py:51
  140.3 0.8 collective-permute-start.15
  141.3 3.8 %absorb.4 = (bf16[4,160,2560]{2,1,0:T(8,128)(2,1)}, f32[128,2560]{1,0:T(8,128)S(1)}, f32[192,1280]{1,0:T(8,128)S(1)}) custom-call(s32[6]{0:T(128)S(1)} %stack.27.places_ref, bf16[4,320,640]{2,1,0:T(8,128)(2,1)S(1)} %maximum_bitcast_fusion.hidden_ref, bf16[160,2560]{1,0:T(8,128)(2,1)S(1)} %pad_maximum_fusion.1.refs_0_, ...), custom_call_target="tpu_custom_call" | custom-call | tf_op jit(solution)/shard_map/absorb/pallas_call | solution.py:183
  145.1 3.5 %absorb.5 = (bf16[4,160,2560]{2,1,0:T(8,128)(2,1)}, f32[128,2560]{1,0:T(8,128)S(1)}, f32[192,1280]{1,0:T(8,128)S(1)}) custom-call(s32[6]{0:T(128)S(1)} %stack.27.places_ref, bf16[4,320,640]{2,1,0:T(8,128)(2,1)S(1)} %maximum_bitcast_fusion.hidden_ref, bf16[160,2560]{1,0:T(8,128)(2,1)} %collective-permute-done.7.refs_0_, ...), custom_call_target="tpu_custom_call" | custom-call | tf_op jit(solution)/shard_map/absorb/pallas_call | solution.py:183
  148.6 3.1 %absorb.6 = (bf16[4,160,2560]{2,1,0:T(8,128)(2,1)}, f32[128,2560]{1,0:T(8,128)S(1)}, f32[192,1280]{1,0:T(8,128)S(1)}) custom-call(s32[6]{0:T(128)S(1)} %stack.27.places_ref, bf16[4,320,640]{2,1,0:T(8,128)(2,1)S(1)} %maximum_bitcast_fusion.hidden_ref, bf16[160,2560]{1,0:T(8,128)(2,1)S(1)} %broadcast_select_fusion.1.refs_0_, ...), custom_call_target="tpu_custom_call" | custom-call | tf_op jit(solution)/shard_map/absorb/pallas_call | solution.py:183
  151.7 4.4 %collective-permute-done.16.refs_6_ = bf16[80,2560]{1,0:T(8,128)(2,1)S(1)} collective-permute-done((bf16[80,2560]{1,0:T(8,128)(2,1)S(1)}, bf16[80,2560]{1,0:T(8,128)(2,1)S(1)}, u32[]{:S(2)}, u32[]{:S(2)}) %collective-permute-start.16) | collective-permute-done | bytes 409632 | tf_op jit(solution)/shard_map/ppermute | solution.py:51
  156.1 4.0 %absorb.7 = (bf16[4,160,2560]{2,1,0:T(8,128)(2,1)}, f32[128,2560]{1,0:T(8,128)S(1)}, f32[192,1280]{1,0:T(8,128)S(1)}, f32[448,128]{1,0:T(8,128)S(1)}) custom-call(s32[6]{0:T(128)S(1)} %stack.27.places_ref, bf16[4,320,640]{2,1,0:T(8,128)(2,1)S(1)} %maximum_bitcast_fusion.hidden_ref, bf16[160,2560]{1,0:T(8,128)(2,1)S(1)} %broadcast_select_fusion.refs_0_, ...), custom_call_target="tpu_custom_call" | custom-call | tf_op jit(solution)/shard_map/absorb/pallas_call | solution.py:183
  160.2 1.4 collective-permute-done.29.refs_2_
  161.7 4.0 %attend.2 = (bf16[128,1280]{1,0:T(8,128)(2,1)S(1)}, bf16[192,1280]{1,0:T(8,128)(2,1)S(1)}) custom-call(f32[128,2560]{1,0:T(8,128)S(1)} %get-tuple-element.40.refs_0_, f32[448,128]{1,0:T(8,128)S(1)} %get-tuple-element.41.refs_1_, f32[448,128]{1,0:T(8,128)S(1)} %collective-permute-done.29.refs_2_, f32[1,1280]{1,0:T(1,128)S(1)} %broadcast_in_dim.4.refs_3_, ...), custom_call_target="tpu_custom_call" | custom-call | tf_op jit(solution)/shard_map/attend/pallas_call | solution.py:252
  165.7 0.8 copy-done.5
  166.6 1.5 collective-permute-done.30.other_ref
  168.1 6.1 %project.1 = (f32[128,2560]{1,0:T(8,128)S(1)}, f32[256,128]{1,0:T(8,128)S(1)}, bf16[128,1280]{1,0:T(8,128)(2,1)S(1)}) custom-call(s32[6]{0:T(128)S(1)} %stack.27.places_ref, bf16[128,1280]{1,0:T(8,128)(2,1)S(1)} %get-tuple-element.44.own_ref.refs_10_, bf16[128,1280]{1,0:T(8,128)(2,1)S(1)} %collective-permute-done.30.other_ref, ...), custom_call_target="tpu_custom_call" | custom-call | tf_op jit(solution)/shard_map/project/pallas_call | solution.py:320
  174.5 1.1 collective-permute-done.31.refs_2_
  175.6 3.9 %attend.3 = bf16[128,1280]{1,0:T(8,128)(2,1)S(1)} custom-call(f32[128,2560]{1,0:T(8,128)S(1)} %get-tuple-element.49.refs_0_, f32[256,128]{1,0:T(8,128)S(1)} %get-tuple-element.50.refs_1_, f32[256,128]{1,0:T(8,128)S(1)} %collective-permute-done.31.refs_2_, f32[1,1280]{1,0:T(1,128)S(1)} %broadcast_in_dim.4.refs_3_, f32[1,1280]{1,0:T(1,128)S(1)} %broadcast_in_dim.5.refs_4_, ...), custom_call_target="tpu_custom_call" | custom-call | tf_op jit(solution)/shard_map/attend/pallas_call | solution.py:252
  179.7 1.2 collective-permute-done.32
  181.0 0.7 pad_maximum_fusion.5
  (127 shorter events, 7.1 us)
Async XLA Ops:
  0.0 24.4 %copy-start = (bf16[128,7680]{1,0:T(8,128)(2,1)S(1)}, bf16[128,7680]{1,0:T(8,128)(2,1)}, u32[]{:S(2)}) copy-start(bf16[128,7680]{1,0:T(8,128)(2,1)} %param.17) | copy-start | bytes 5898244
  0.0 8.8 %copy-start.13 = (f32[2560]{0:T(1024)S(1)}, f32[2560]{0:T(1024)}, u32[]{:S(2)}) copy-start(f32[2560]{0:T(1024)} %param.18) | copy-start | bytes 30724
  0.0 8.9 %copy-start.14 = (f32[2560]{0:T(1024)S(1)}, f32[2560]{0:T(1024)}, u32[]{:S(2)}) copy-start(f32[2560]{0:T(1024)} %param.19) | copy-start | bytes 30724
  0.0 12.3 %collective-permute-start.3 = (bf16[64,2560]{1,0:T(8,128)(2,1)}, bf16[64,2560]{1,0:T(8,128)(2,1)}, u32[]{:S(2)}, u32[]{:S(2)}) collective-permute-start(bf16[64,2560]{1,0:T(8,128)(2,1)} %param.11), channel_id=1, source_target_pairs={{0,2},{1,3},{2,4},{3,5},{4,6},{5,7},{6,8},{7,9},{8,10},{9,11},{10,... | collective-permute-start | bytes 983048 | tf_op jit(solution)/shard_map/ppermute | solution.py:51
  5.8 6.5 %collective-permute-start.5 = (bf16[64,2560]{1,0:T(8,128)(2,1)}, bf16[64,2560]{1,0:T(8,128)(2,1)}, u32[]{:S(2)}, u32[]{:S(2)}) collective-permute-start(bf16[64,2560]{1,0:T(8,128)(2,1)} %param.11), channel_id=1, source_target_pairs={{0,1},{1,0},{2,3},{3,2},{4,5},{5,4},{6,7},{7,6},{8,9},{9,8},{10,11... | collective-permute-start | bytes 983048 | tf_op jit(solution)/shard_map/ppermute | solution.py:51
  7.1 6.2 %collective-permute-start = (bf16[80,2560]{1,0:T(8,128)(2,1)S(1)}, bf16[80,2560]{1,0:T(8,128)(2,1)S(1)}, u32[]{:S(2)}, u32[]{:S(2)}) collective-permute-start(bf16[80,2560]{1,0:T(8,128)(2,1)S(1)} %pad_maximum_fusion.4), channel_id=1, source_target_pairs={{0,1},{1,0},{2,3},{3,2},{4,5},{5,4},{6,7},{7,6},{8,9},{9,8},{10,11... | collective-permute-start | bytes 1228808 | tf_op jit(solution)/shard_map/ppermute | solution.py:51
  12.3 18.6 %collective-permute-start.4 = (bf16[64,2560]{1,0:T(8,128)(2,1)}, bf16[64,2560]{1,0:T(8,128)(2,1)}, u32[]{:S(2)}, u32[]{:S(2)}) collective-permute-start(bf16[64,2560]{1,0:T(8,128)(2,1)} %collective-permute-done.3), channel_id=1, source_target_pairs={{0,1},{1,0},{2,3},{3,2},{4,5},{5,4},{6,7},{7,6},{8,9},{9,8},{10,11... | collective-permute-start | bytes 983048 | tf_op jit(solution)/shard_map/ppermute | solution.py:51
  13.3 5.9 %copy-start.7 = (s32[32]{0:T(128)S(1)}, s32[32]{0:T(128)}, u32[]{:S(2)}) copy-start(s32[32]{0:T(128)} %param.12) | copy-start | bytes 388
  13.3 6.7 %copy-start.18 = (s32[1,2]{1,0:T(1,128)S(1)}, s32[1,2]{1,0:T(1,128)}, u32[]{:S(2)}) copy-start(s32[1,2]{1,0:T(1,128)} %param.13) | copy-start | bytes 28
  13.3 6.7 %copy-start.19 = (s32[1,2]{1,0:T(1,128)S(1)}, s32[1,2]{1,0:T(1,128)}, u32[]{:S(2)}) copy-start(s32[1,2]{1,0:T(1,128)} %param.14) | copy-start | bytes 28
  13.4 7.1 %copy-start.15 = (f32[64]{0:T(128)S(1)}, f32[64]{0:T(128)}, u32[]{:S(2)}) copy-start(f32[64]{0:T(128)} %multiply_exponential_fusion) | copy-start | bytes 772
  13.6 57.2 %collective-permute-start.26 = (bf16[160,2560]{1,0:T(8,128)(2,1)S(1)}, bf16[160,2560]{1,0:T(8,128)(2,1)}, u32[]{:S(2)}, u32[]{:S(2)}) collective-permute-start(bf16[160,2560]{1,0:T(8,128)(2,1)S(1)} %pad_maximum_fusion.1.refs_0_), channel_id=1, source_target_pairs={{0,4},{1,5},{2,6},{3,7},{4,0},{5,1},{6,2},{7,3},{8,12},{9,13},{10,... | collective-permute-start | bytes 2457608 | tf_op jit(solution)/shard_map/ppermute | solution.py:51
  17.1 56.3 %collective-permute-start.25 = (bf16[160,2560]{1,0:T(8,128)(2,1)S(1)}, bf16[160,2560]{1,0:T(8,128)(2,1)}, u32[]{:S(2)}, u32[]{:S(2)}) collective-permute-start(bf16[160,2560]{1,0:T(8,128)(2,1)S(1)} %pad_maximum_fusion.1.refs_0_), channel_id=1, source_target_pairs={{0,2},{1,3},{2,0},{3,1},{4,6},{5,7},{6,4},{7,5},{8,10},{9,11},{10,... | collective-permute-start | bytes 2457608 | tf_op jit(solution)/shard_map/ppermute | solution.py:51
  17.6 20.2 %collective-permute-start.7 = (bf16[160,2560]{1,0:T(8,128)(2,1)S(1)}, bf16[160,2560]{1,0:T(8,128)(2,1)}, u32[]{:S(2)}, u32[]{:S(2)}) collective-permute-start(bf16[160,2560]{1,0:T(8,128)(2,1)S(1)} %pad_maximum_fusion.1.refs_0_), channel_id=1, source_target_pairs={{0,8},{1,9},{2,10},{3,11},{4,12},{5,13},{6,14},{7,15},{8,0},{9,1},... | collective-permute-start | bytes 2457608 | tf_op jit(solution)/shard_map/ppermute | solution.py:51
  20.4 2.1 %collective-permute-start.2 = (s32[1,4]{0,1:T(4,128)S(1)}, s32[1,4]{0,1:T(4,128)S(1)}, u32[]{:S(2)}, u32[]{:S(2)}) collective-permute-start(s32[1,4]{0,1:T(4,128)S(1)} %copy.40), channel_id=1, source_target_pairs={{0,1},{1,0},{2,3},{3,2},{4,5},{5,4},{6,7},{7,6},{8,9},{9,8},{10,11... | collective-permute-start | bytes 56 | tf_op jit(solution)/shard_map/ppermute | solution.py:51
  22.5 16.1 %collective-permute-start.6 = (bf16[160,2560]{1,0:T(8,128)(2,1)S(1)}, bf16[160,2560]{1,0:T(8,128)(2,1)}, u32[]{:S(2)}, u32[]{:S(2)}) collective-permute-start(bf16[160,2560]{1,0:T(8,128)(2,1)S(1)} %pad_maximum_fusion.1.refs_0_), channel_id=1, source_target_pairs={{8,16},{9,17},{10,18},{11,19},{12,20},{13,21},{14,22},{15,23},{16,... | collective-permute-start | bytes 2457608 | tf_op jit(solution)/shard_map/ppermute | solution.py:51
  25.4 2.8 %copy-start.8 = (f32[2,64,2560]{2,1,0:T(8,128)}, f32[2,64,2560]{2,1,0:T(8,128)S(1)}, u32[]{:S(2)}) copy-start(f32[2,64,2560]{2,1,0:T(8,128)S(1)} %mul.216) | copy-start | bytes 3932164
  28.1 2.7 %copy-start.16 = (s32[2]{0:T(128)S(1)}, s32[2]{0:T(128)}, u32[]{:S(2)}) copy-start(s32[2]{0:T(128)} %get-tuple-element.94) | copy-start | bytes 28
  28.1 2.7 %copy-start.17 = (s32[2]{0:T(128)S(1)}, s32[2]{0:T(128)}, u32[]{:S(2)}) copy-start(s32[2]{0:T(128)} %get-tuple-element.95) | copy-start | bytes 28
  30.9 36.9 %collective-permute-start.1 = (bf16[64,2560]{1,0:T(8,128)(2,1)}, bf16[64,2560]{1,0:T(8,128)(2,1)S(1)}, u32[]{:S(2)}, u32[]{:S(2)}) collective-permute-start(bf16[64,2560]{1,0:T(8,128)(2,1)} %param.10), channel_id=1, source_target_pairs={{0,1},{1,0},{2,3},{3,2},{4,5},{5,4},{6,7},{7,6},{8,9},{9,8},{10,11... | collective-permute-start | bytes 983048 | tf_op jit(solution)/shard_map/ppermute | solution.py:51
  37.8 2.7 %collective-permute-start.8 = (bf16[160,2560]{1,0:T(8,128)(2,1)}, bf16[160,2560]{1,0:T(8,128)(2,1)S(1)}, u32[]{:S(2)}, u32[]{:S(2)}) collective-permute-start(bf16[160,2560]{1,0:T(8,128)(2,1)} %collective-permute-done.7.refs_0_), channel_id=1, source_target_pairs={{8,16},{9,17},{10,18},{11,19},{12,20},{13,21},{14,22},{15,23},{16,... | collective-permute-start | bytes 2457608 | tf_op jit(solution)/shard_map/ppermute | solution.py:51
  38.6 27.8 %collective-permute-start.9 = (bf16[160,2560]{1,0:T(8,128)(2,1)}, bf16[160,2560]{1,0:T(8,128)(2,1)S(1)}, u32[]{:S(2)}, u32[]{:S(2)}) collective-permute-start(bf16[160,2560]{1,0:T(8,128)(2,1)} %collective-permute-done.6), channel_id=1, source_target_pairs={{8,0},{9,1},{10,2},{11,3},{12,4},{13,5},{14,6},{15,7},{16,24},{17,... | collective-permute-start | bytes 2457608 | tf_op jit(solution)/shard_map/ppermute | solution.py:51
  40.6 33.9 %collective-permute-start.22 = (bf16[160,2560]{1,0:T(8,128)(2,1)}, bf16[160,2560]{1,0:T(8,128)(2,1)S(1)}, u32[]{:S(2)}, u32[]{:S(2)}) collective-permute-start(bf16[160,2560]{1,0:T(8,128)(2,1)} %collective-permute-done.7.refs_0_), channel_id=1, source_target_pairs={{0,4},{1,5},{2,6},{3,7},{4,0},{5,1},{6,2},{7,3},{8,12},{9,13},{10,... | collective-permute-start | bytes 2457608 | tf_op jit(solution)/shard_map/ppermute | solution.py:51
  66.3 21.3 %collective-permute-start.21 = (bf16[160,2560]{1,0:T(8,128)(2,1)}, bf16[160,2560]{1,0:T(8,128)(2,1)S(1)}, u32[]{:S(2)}, u32[]{:S(2)}) collective-permute-start(bf16[160,2560]{1,0:T(8,128)(2,1)} %collective-permute-done.7.refs_0_), channel_id=1, source_target_pairs={{0,2},{1,3},{2,0},{3,1},{4,6},{5,7},{6,4},{7,5},{8,10},{9,11},{10,... | collective-permute-start | bytes 2457608 | tf_op jit(solution)/shard_map/ppermute | solution.py:51
  67.9 21.3 %collective-permute-start.10 = (bf16[160,2560]{1,0:T(8,128)(2,1)S(1)}, bf16[160,2560]{1,0:T(8,128)(2,1)S(1)}, u32[]{:S(2)}, u32[]{:S(2)}) collective-permute-start(bf16[160,2560]{1,0:T(8,128)(2,1)S(1)} %broadcast_select_fusion.1.refs_0_), channel_id=1, source_target_pairs={{8,0},{9,1},{10,2},{11,3},{12,4},{13,5},{14,6},{15,7},{16,24},{17,... | collective-permute-start | bytes 2457608 | tf_op jit(solution)/shard_map/ppermute | solution.py:51
  70.8 21.2 %collective-permute-start.18 = (bf16[160,2560]{1,0:T(8,128)(2,1)S(1)}, bf16[160,2560]{1,0:T(8,128)(2,1)S(1)}, u32[]{:S(2)}, u32[]{:S(2)}) collective-permute-start(bf16[160,2560]{1,0:T(8,128)(2,1)S(1)} %broadcast_select_fusion.1.refs_0_), channel_id=1, source_target_pairs={{0,4},{1,5},{2,6},{3,7},{4,0},{5,1},{6,2},{7,3},{8,12},{9,13},{10,... | collective-permute-start | bytes 2457608 | tf_op jit(solution)/shard_map/ppermute | solution.py:51
  73.3 23.1 %collective-permute-start.28 = (bf16[80,2560]{1,0:T(8,128)(2,1)S(1)}, bf16[80,2560]{1,0:T(8,128)(2,1)S(1)}, u32[]{:S(2)}, u32[]{:S(2)}) collective-permute-start(bf16[80,2560]{1,0:T(8,128)(2,1)S(1)} %slice.110), channel_id=1, source_target_pairs={{0,2},{1,3},{2,0},{3,1},{4,6},{5,7},{6,4},{7,5},{8,10},{9,11},{10,... | collective-permute-start | bytes 1228808 | tf_op jit(solution)/shard_map/ppermute | solution.py:51
  74.5 26.2 %collective-permute-start.27 = (bf16[80,2560]{1,0:T(8,128)(2,1)S(1)}, bf16[80,2560]{1,0:T(8,128)(2,1)S(1)}, u32[]{:S(2)}, u32[]{:S(2)}) collective-permute-start(bf16[80,2560]{1,0:T(8,128)(2,1)S(1)} %slice.109), channel_id=1, source_target_pairs={{0,4},{1,5},{2,6},{3,7},{4,0},{5,1},{6,2},{7,3},{8,12},{9,13},{10,... | collective-permute-start | bytes 1228808 | tf_op jit(solution)/shard_map/ppermute | solution.py:51
  87.7 26.3 %collective-permute-start.17 = (bf16[160,2560]{1,0:T(8,128)(2,1)S(1)}, bf16[160,2560]{1,0:T(8,128)(2,1)S(1)}, u32[]{:S(2)}, u32[]{:S(2)}) collective-permute-start(bf16[160,2560]{1,0:T(8,128)(2,1)S(1)} %broadcast_select_fusion.1.refs_0_), channel_id=1, source_target_pairs={{0,2},{1,3},{2,0},{3,1},{4,6},{5,7},{6,4},{7,5},{8,10},{9,11},{10,... | collective-permute-start | bytes 2457608 | tf_op jit(solution)/shard_map/ppermute | solution.py:51
  89.1 33.6 %collective-permute-start.24 = (bf16[80,2560]{1,0:T(8,128)(2,1)S(1)}, bf16[80,2560]{1,0:T(8,128)(2,1)S(1)}, u32[]{:S(2)}, u32[]{:S(2)}) collective-permute-start(bf16[80,2560]{1,0:T(8,128)(2,1)S(1)} %slice.108), channel_id=1, source_target_pairs={{0,2},{1,3},{2,0},{3,1},{4,6},{5,7},{6,4},{7,5},{8,10},{9,11},{10,... | collective-permute-start | bytes 1228808 | tf_op jit(solution)/shard_map/ppermute | solution.py:51
  89.8 25.6 %copy-start.12 = (f32[128,4,640]{2,1,0:T(4,128)S(1)}, f32[128,4,640]{2,1,0:T(4,128)}, u32[]{:S(2)}) copy-start(f32[128,4,640]{2,1,0:T(4,128)} %add.217) | copy-start | bytes 3932164
  89.9 25.5 %copy-start.11 = (f32[128,4,640]{2,1,0:T(4,128)S(1)}, f32[128,4,640]{2,1,0:T(4,128)}, u32[]{:S(2)}) copy-start(f32[128,4,640]{2,1,0:T(4,128)} %mul.217) | copy-start | bytes 3932164
  91.9 32.3 %collective-permute-start.23 = (bf16[80,2560]{1,0:T(8,128)(2,1)S(1)}, bf16[80,2560]{1,0:T(8,128)(2,1)S(1)}, u32[]{:S(2)}, u32[]{:S(2)}) collective-permute-start(bf16[80,2560]{1,0:T(8,128)(2,1)S(1)} %slice.107), channel_id=1, source_target_pairs={{0,4},{1,5},{2,6},{3,7},{4,0},{5,1},{6,2},{7,3},{8,12},{9,13},{10,... | collective-permute-start | bytes 1228808 | tf_op jit(solution)/shard_map/ppermute | solution.py:51
  96.4 35.1 %collective-permute-start.20 = (bf16[80,2560]{1,0:T(8,128)(2,1)S(1)}, bf16[80,2560]{1,0:T(8,128)(2,1)S(1)}, u32[]{:S(2)}, u32[]{:S(2)}) collective-permute-start(bf16[80,2560]{1,0:T(8,128)(2,1)S(1)} %slice.106), channel_id=1, source_target_pairs={{0,2},{1,3},{2,0},{3,1},{4,6},{5,7},{6,4},{7,5},{8,10},{9,11},{10,... | collective-permute-start | bytes 1228808 | tf_op jit(solution)/shard_map/ppermute | solution.py:51
  100.7 31.7 %collective-permute-start.14 = (bf16[80,2560]{1,0:T(8,128)(2,1)S(1)}, bf16[80,2560]{1,0:T(8,128)(2,1)S(1)}, u32[]{:S(2)}, u32[]{:S(2)}) collective-permute-start(bf16[80,2560]{1,0:T(8,128)(2,1)S(1)} %get-tuple-element.61), channel_id=1, source_target_pairs={{0,4},{1,5},{2,6},{3,7},{4,0},{5,1},{6,2},{7,3},{8,12},{9,13},{10,... | collective-permute-start | bytes 1228808 | tf_op jit(solution)/shard_map/ppermute | solution.py:51
  114.0 26.3 %collective-permute-start.11 = (bf16[80,2560]{1,0:T(8,128)(2,1)S(1)}, bf16[80,2560]{1,0:T(8,128)(2,1)S(1)}, u32[]{:S(2)}, u32[]{:S(2)}) collective-permute-start(bf16[80,2560]{1,0:T(8,128)(2,1)S(1)} %get-tuple-element.62), channel_id=1, source_target_pairs={{0,2},{1,3},{2,0},{3,1},{4,6},{5,7},{6,4},{7,5},{8,10},{9,11},{10,... | collective-permute-start | bytes 1228808 | tf_op jit(solution)/shard_map/ppermute | solution.py:51
  116.0 25.2 %copy-start.9 = (f32[2,64,2560]{2,1,0:T(8,128)S(1)}, f32[2,64,2560]{2,1,0:T(8,128)}, u32[]{:S(2)}) copy-start(f32[2,64,2560]{2,1,0:T(8,128)} %copy-done.8) | copy-start | bytes 3932164
  116.0 25.2 %copy-start.10 = (f32[2,64,2560]{2,1,0:T(8,128)S(1)}, f32[2,64,2560]{2,1,0:T(8,128)}, u32[]{:S(2)}) copy-start(f32[2,64,2560]{2,1,0:T(8,128)} %add.216) | copy-start | bytes 3932164
  122.8 28.9 %collective-permute-start.12 = (bf16[80,2560]{1,0:T(8,128)(2,1)S(1)}, bf16[80,2560]{1,0:T(8,128)(2,1)S(1)}, u32[]{:S(2)}, u32[]{:S(2)}) collective-permute-start(bf16[80,2560]{1,0:T(8,128)(2,1)S(1)} %get-tuple-element.61), channel_id=1, source_target_pairs={{0,2},{1,3},{2,0},{3,1},{4,6},{5,7},{6,4},{7,5},{8,10},{9,11},{10,... | collective-permute-start | bytes 1228808 | tf_op jit(solution)/shard_map/ppermute | solution.py:51
  124.2 27.5 %collective-permute-start.13 = (bf16[80,2560]{1,0:T(8,128)(2,1)S(1)}, bf16[80,2560]{1,0:T(8,128)(2,1)S(1)}, u32[]{:S(2)}, u32[]{:S(2)}) collective-permute-start(bf16[80,2560]{1,0:T(8,128)(2,1)S(1)} %get-tuple-element.62), channel_id=1, source_target_pairs={{0,4},{1,5},{2,6},{3,7},{4,0},{5,1},{6,2},{7,3},{8,12},{9,13},{10,... | collective-permute-start | bytes 1228808 | tf_op jit(solution)/shard_map/ppermute | solution.py:51
  131.6 17.0 %collective-permute-start.19 = (bf16[80,2560]{1,0:T(8,128)(2,1)S(1)}, bf16[80,2560]{1,0:T(8,128)(2,1)S(1)}, u32[]{:S(2)}, u32[]{:S(2)}) collective-permute-start(bf16[80,2560]{1,0:T(8,128)(2,1)S(1)} %slice.105), channel_id=1, source_target_pairs={{0,4},{1,5},{2,6},{3,7},{4,0},{5,1},{6,2},{7,3},{8,12},{9,13},{10,... | collective-permute-start | bytes 1228808 | tf_op jit(solution)/shard_map/ppermute | solution.py:51
  132.4 23.7 %collective-permute-start.16 = (bf16[80,2560]{1,0:T(8,128)(2,1)S(1)}, bf16[80,2560]{1,0:T(8,128)(2,1)S(1)}, u32[]{:S(2)}, u32[]{:S(2)}) collective-permute-start(bf16[80,2560]{1,0:T(8,128)(2,1)S(1)} %collective-permute-done.14.refs_4_), channel_id=1, source_target_pairs={{0,2},{1,3},{2,0},{3,1},{4,6},{5,7},{6,4},{7,5},{8,10},{9,11},{10,... | collective-permute-start | bytes 1228808 | tf_op jit(solution)/shard_map/ppermute | solution.py:51
  140.3 15.8 %collective-permute-start.15 = (bf16[80,2560]{1,0:T(8,128)(2,1)S(1)}, bf16[80,2560]{1,0:T(8,128)(2,1)S(1)}, u32[]{:S(2)}, u32[]{:S(2)}) collective-permute-start(bf16[80,2560]{1,0:T(8,128)(2,1)S(1)} %collective-permute-done.11.refs_1_), channel_id=1, source_target_pairs={{0,4},{1,5},{2,6},{3,7},{4,0},{5,1},{6,2},{7,3},{8,12},{9,13},{10,... | collective-permute-start | bytes 1228808 | tf_op jit(solution)/shard_map/ppermute | solution.py:51
  156.1 5.6 %copy-start.2 = (f32[256,128]{1,0:T(8,128)S(1)}, f32[256,128]{1,0:T(8,128)}, u32[]{:S(2)}) copy-start(f32[256,128]{1,0:T(8,128)} %pad_maximum_fusion.7.refs_6_) | copy-start | bytes 393220
  156.1 5.6 %copy-start.3 = (f32[256,128]{1,0:T(8,128)S(1)}, f32[256,128]{1,0:T(8,128)}, u32[]{:S(2)}) copy-start(f32[256,128]{1,0:T(8,128)} %pad_maximum_fusion.6.refs_5_) | copy-start | bytes 393220
  160.1 1.6 collective-permute-start.29
  165.6 0.8 copy-start.5
  166.4 1.6 collective-permute-start.30
  168.1 7.6 %copy-start.4 = (f32[256,128]{1,0:T(8,128)S(1)}, f32[256,128]{1,0:T(8,128)}, u32[]{:S(2)}) copy-start(f32[256,128]{1,0:T(8,128)} %pad_maximum_fusion.6.refs_5_) | copy-start | bytes 393220
  168.1 7.6 %copy-start.6 = (bf16[192,1280]{1,0:T(8,128)(2,1)S(1)}, bf16[192,1280]{1,0:T(8,128)(2,1)}, u32[]{:S(2)}) copy-start(bf16[192,1280]{1,0:T(8,128)(2,1)} %copy-done.5) | copy-start | bytes 1474564
  174.2 1.4 collective-permute-start.31
  175.6 6.2 %copy-start.1 = (bf16[128,7680]{1,0:T(8,128)(2,1)S(1)}, bf16[128,7680]{1,0:T(8,128)(2,1)}, u32[]{:S(2)}) copy-start(bf16[128,7680]{1,0:T(8,128)(2,1)} %param.17) | copy-start | bytes 5898244
  179.5 1.5 collective-permute-start.32

commit v3 on v2

--- a/solution.py
+++ b/solution.py
@@ -114,6 +114,29 @@
     return [z ^ step for step in range(4)], place, pieces, spots
 
 
+def gather_rest(unit, device):
+    z = device // 8
+    place = (device // 2) % 4
+    middle = (z == 1) | (z == 2)
+    half = unit.shape[0] // 2
+    from_x = swap_x(unit)
+    from_y = swap_y(unit)
+    low, high = from_x[:half], from_y[half:]
+    low, high = swap_y(low), swap_x(high)
+    plane = jnp.zeros((4,) + unit.shape, unit.dtype)
+    far = jnp.concatenate([low, high], axis=0)
+    for piece, at in ((unit, place), (from_x, place ^ 1), (from_y, place ^ 2), (far, place ^ 3)):
+        plane = lax.dynamic_update_slice(plane, piece[None], (at, 0, 0))
+    plane = plane.reshape(-1, unit.shape[1])
+    pair = swap_z_pair(plane)
+    across = swap_z_middle(plane)
+    two_mid = swap_z_middle(pair)
+    two_end = z_outward(across)
+    second = jnp.where(middle, two_mid, two_end)
+    three_end = z_outward(second)
+    return [plane, pair, second, jnp.where(middle, across, three_end)]
+
+
 def gather_any(unit, device):
     size = lax.axis_size(AXIS)
     groups = [list(range(core, size, 2)) for core in range(2)]
@@ -122,11 +145,17 @@
     return [none], none, [[whole]], [[(0, 0, whole.shape[0])]]
 
 
+def gather_rest_any(unit, device):
+    return gather_any(unit, device)[2][0]
+
+
 def absorb_body(spots, step, has_sum, last, places_ref, hidden_ref, *refs):
     count = len(spots)
     piece_refs, refs = refs[:count], refs[count:]
     if has_sum:
         raw_in_ref, past_in_ref, *refs = refs
+    if last:
+        rest_ref, past_rest_ref, *refs = refs
     plane_out_ref, raw_ref, past_ref, *refs = refs
     if last:
         sum_ref, *refs = refs
@@ -144,37 +173,51 @@
     out.start()
     weights = plane_ref[...].reshape(-1, plane_ref.shape[2])
     hidden = hidden_ref[places_ref[step]]
-    rows, split = raw_ref.shape[0], weights.shape[1] // 2
+    split = weights.shape[1] // 2
+    rows = raw_ref.shape[0]
     raw = jnp.dot(hidden[:rows], weights, preferred_element_type=jnp.float32)
     past = jnp.dot(hidden[rows:], weights[:, split:], preferred_element_type=jnp.float32)
     if has_sum:
         raw = raw + raw_in_ref[...]
         past = past + past_in_ref[...]
-    raw_ref[...] = raw
-    past_ref[...] = past
-    if last:
+    if not last:
+        raw_ref[...] = raw
+        past_ref[...] = past
+    else:
+        rest, past_rest = rest_ref[...], past_rest_ref[...]
+        more = past_rest.shape[1]
+        half = split + more
         at = 0
-        for side in (raw[:, :split], raw[:, split:], past):
-            count = side.shape[0]
-            total = jnp.sum(side * side, -1, keepdims=True)
+        for target, start, main, other in (
+            (raw_ref, 0, raw[:, :split], rest[:, :more]),
+            (raw_ref, half, raw[:, split:], rest[:, more:]),
+            (past_ref, 0, past, past_rest),
+        ):
+            target[:, start : start + split] = main
+            target[:, start + split : start + half] = other
+            count = main.shape[0]
+            total = jnp.sum(main * main, -1, keepdims=True)
+            total = total + jnp.sum(other * other, -1, keepdims=True)
             sum_ref[at : at + count] = jnp.broadcast_to(total, (count, HEAD_DIM))
             at += count
     out.wait()
 
 
-def absorb(step, last, places, hidden, pieces, spots, chips, rows, sums):
+def absorb(step, places, hidden, pieces, spots, chips, rows, sums, rests):
+    last = bool(rests)
     hbm = pl.BlockSpec(memory_space=pltpu.HBM)
     vmem = pl.BlockSpec(memory_space=pltpu.VMEM)
     width = pieces[0].shape[1]
     chip_rows = hidden.shape[2] // chips
     past_rows = hidden.shape[1] - rows
-    operands = [places, hidden, *pieces, *sums]
+    more = rests[1].shape[1] if last else 0
+    operands = [places, hidden, *pieces, *sums, *rests]
     specs = [pl.BlockSpec(memory_space=pltpu.SMEM), vmem] + [hbm] * len(pieces)
-    specs += [vmem] * len(sums)
+    specs += [vmem] * (len(sums) + len(rests))
     shapes = [
         pltpu.HBM((chips, chip_rows, width), jnp.bfloat16),
-        jax.ShapeDtypeStruct((rows, width), jnp.float32),
-        jax.ShapeDtypeStruct((past_rows, width // 2), jnp.float32),
+        jax.ShapeDtypeStruct((rows, width + 2 * more), jnp.float32),
+        jax.ShapeDtypeStruct((past_rows, width // 2 + more), jnp.float32),
     ]
     outs = [hbm, vmem, vmem]
     if last:
@@ -193,6 +236,48 @@
         compiler_params=pltpu.CompilerParams(vmem_limit_bytes=16 << 20),
         name="absorb",
     )(*operands)
+
+
+def absorb_rest_body(places_ref, hidden_ref, *refs):
+    count = len(refs) - 4
+    plane_refs = refs[:count]
+    raw_ref, past_ref, weight_ref, sems = refs[count:]
+    copies = [
+        pltpu.make_async_copy(ref, weight_ref.at[i], sems.at[i]) for i, ref in enumerate(plane_refs)
+    ]
+    for copy in copies:
+        copy.start()
+    rows, split = raw_ref.shape[0], past_ref.shape[1]
+    raw = past = None
+    for i, copy in enumerate(copies):
+        copy.wait()
+        hidden, weights = hidden_ref[places_ref[i]], weight_ref[i]
+        part = jnp.dot(hidden[:rows], weights, preferred_element_type=jnp.float32)
+        raw = part if raw is None else raw + part
+        part = jnp.dot(hidden[rows:], weights[:, split:], preferred_element_type=jnp.float32)
+        past = part if past is None else past + part
+    raw_ref[...] = raw
+    past_ref[...] = past
+
+
+def absorb_rest(places, hidden, planes, rows):
+    hbm = pl.BlockSpec(memory_space=pltpu.HBM)
+    vmem = pl.BlockSpec(memory_space=pltpu.VMEM)
+    count, width = len(planes), planes[0].shape[1]
+    return pl.pallas_call(
+        absorb_rest_body,
+        in_specs=[pl.BlockSpec(memory_space=pltpu.SMEM), vmem] + [hbm] * count,
+        out_shape=[
+            jax.ShapeDtypeStruct((rows, width), jnp.float32),
+            jax.ShapeDtypeStruct((hidden.shape[1] - rows, width // 2), jnp.float32),
+        ],
+        scratch_shapes=[
+            pltpu.VMEM((count,) + planes[0].shape, jnp.bfloat16),
+            pltpu.SemaphoreType.DMA((count,)),
+        ],
+        compiler_params=pltpu.CompilerParams(vmem_limit_bytes=12 << 20),
+        name="absorb_rest",
+    )(places, hidden, *planes)
 
 
 def turn(values, cosine, sine):
@@ -248,7 +333,14 @@
 def attend(first, inner, raw, sums, others, gains, tables, fixed, latent, factor, past):
     shapes = [jax.ShapeDtypeStruct(latent.shape, jnp.bfloat16)]
     if first:
-        shapes.append(jax.ShapeDtypeStruct(past.shape, jnp.bfloat16))
+        shapes.append(pltpu.HBM(past.shape, jnp.bfloat16))
+    else:
+        own_values, past_values = fixed[1:]
+        raw, past, own_values, sums, others = (
+            pltpu.with_memory_space_constraint(x, pltpu.HBM)
+            for x in (raw, past, own_values, sums, others)
+        )
+        fixed = (fixed[0], own_values, past_values)
     return pl.pallas_call(
         functools.partial(attend_body, first, inner),
         out_shape=shapes,
@@ -258,14 +350,14 @@
 
 
 def project_body(places_ref, own_ref, other_ref, mod_ref, *refs):
-    count = len(refs) - 6
-    plane_refs = refs[:count]
-    raw_ref, sum_ref, value_ref, hidden_ref, weight_ref, sems = refs[count:]
+    count = (len(refs) - 7) // 2
+    raw_ref, sum_ref, value_ref, hidden_ref, main_ref, rest_ref, sems = refs[2 * count :]
+    targets = [main_ref.at[i] for i in range(count)] + [rest_ref.at[i] for i in range(count)]
     rows, half = own_ref.shape
     parts, _, part_width = hidden_ref.shape
     copies = [
-        pltpu.make_async_copy(ref, weight_ref.at[i], sems.at[i])
-        for i, ref in enumerate(plane_refs)
+        pltpu.make_async_copy(ref, target, sems.at[i])
+        for i, (ref, target) in enumerate(zip(refs, targets))
     ]
     for copy in copies:
         copy.start()
@@ -298,41 +390,52 @@
             elif i * part_width // half == side:
                 at = i * part_width - side * half
                 hidden_ref[i] = sides[side][:, at : at + part_width]
-    total = None
-    for i, copy in enumerate(copies):
-        copy.wait()
-        weights = weight_ref[i].reshape(-1, weight_ref.shape[-1])
-        part = jnp.dot(hidden_ref[places_ref[i]], weights, preferred_element_type=jnp.float32)
-        total = part if total is None else total + part
-    raw_ref[...] = total
+    squares = [None, None]
+    start = 0
+    for weight_ref, waits in ((main_ref, copies[:count]), (rest_ref, copies[count:])):
+        total = None
+        for i, copy in enumerate(waits):
+            copy.wait()
+            weights = weight_ref[i].reshape(-1, weight_ref.shape[-1])
+            part = jnp.dot(hidden_ref[places_ref[i]], weights, preferred_element_type=jnp.float32)
+            total = part if total is None else total + part
+        split = total.shape[1] // 2
+        for i in range(2):
+            side = total[:, i * split : (i + 1) * split]
+            raw_ref[:, i * half + start : i * half + start + split] = side
+            square = jnp.sum(side * side, -1, keepdims=True)
+            squares[i] = square if squares[i] is None else squares[i] + square
+        start += split
     for i in range(2):
-        side = total[:, i * half : (i + 1) * half]
-        square = jnp.sum(side * side, -1, keepdims=True)
-        sum_ref[i * rows : (i + 1) * rows] = jnp.broadcast_to(square, (rows, HEAD_DIM))
-
-
-def project_latent(places, own, other, mods, planes):
+        sum_ref[i * rows : (i + 1) * rows] = jnp.broadcast_to(squares[i], (rows, HEAD_DIM))
+
+
+def project_latent(places, own, other, mods, planes, rests):
     rows, half = own.shape
     count = len(planes)
-    planes = [pltpu.with_memory_space_constraint(plane, pltpu.HBM) for plane in planes]
+    planes, rests = (
+        [pltpu.with_memory_space_constraint(plane, pltpu.HBM) for plane in group]
+        for group in (planes, rests)
+    )
     vmem = pl.BlockSpec(memory_space=pltpu.VMEM)
     hbm = pl.BlockSpec(memory_space=pltpu.HBM)
     return pl.pallas_call(
         project_body,
-        in_specs=[pl.BlockSpec(memory_space=pltpu.SMEM)] + [vmem] * 3 + [hbm] * count,
+        in_specs=[pl.BlockSpec(memory_space=pltpu.SMEM)] + [vmem] * 3 + [hbm] * (2 * count),
         out_shape=[
-            jax.ShapeDtypeStruct((rows, planes[0].shape[-1]), jnp.float32),
-            jax.ShapeDtypeStruct((2 * rows, HEAD_DIM), jnp.float32),
-            jax.ShapeDtypeStruct((rows, half), jnp.bfloat16),
+            pltpu.HBM((rows, 2 * half), jnp.float32),
+            pltpu.HBM((2 * rows, HEAD_DIM), jnp.float32),
+            pltpu.HBM((rows, half), jnp.bfloat16),
         ],
         scratch_shapes=[
             pltpu.VMEM((count, rows, 2 * half // count), jnp.bfloat16),
             pltpu.VMEM((count,) + planes[0].shape, jnp.bfloat16),
-            pltpu.SemaphoreType.DMA((count,)),
+            pltpu.VMEM((count,) + rests[0].shape, jnp.bfloat16),
+            pltpu.SemaphoreType.DMA((2 * count,)),
         ],
         compiler_params=pltpu.CompilerParams(vmem_limit_bytes=24 << 20),
         name="project",
-    )(places, own, other, mods, *planes)
+    )(places, own, other, mods, *planes, *rests)
 
 
 def denoise(noisy, clean, seg_ids, lag_mask, plan, w_query, w_key, time_proj, q_gain, k_gain):
@@ -348,9 +451,6 @@
     def mine(value, axis):
         return lax.dynamic_slice_in_dim(value, core * half, half, axis)
 
-    def theirs(value, axis):
-        return lax.dynamic_slice_in_dim(value, (1 - core) * half, half, axis)
-
     def in_order(own, other, axis):
         low = jnp.where(is_low, own, other)
         high = jnp.where(is_low, other, own)
@@ -359,14 +459,26 @@
     before = permute(clean, lambda s: s + 2 if s + 2 < devices else None)
     others = swap_core(clean)
 
-    own_rows = jnp.concatenate([mine(w_query, 1), mine(w_key, 1)], axis=1)
-    sent_rows = jnp.concatenate([theirs(w_query, 1), theirs(w_key, 1)], axis=1)
-    unit = in_order(own_rows, swap_core(sent_rows), 0)
+    split = (half // HEAD_DIM) * 4 // 5 * HEAD_DIM
+
+    def columns(start, low, high):
+        return jnp.concatenate(
+            [lax.dynamic_slice_in_dim(w, start + low, high - low, 1) for w in (w_query, w_key)],
+            axis=1,
+        )
+
+    own_start, other_start = core * half, (1 - core) * half
+    unit = in_order(
+        columns(own_start, 0, split), swap_core(columns(other_start, 0, split)), 0
+    )
+    sent_rest = swap_core(columns(other_start, split, half))
+    rest_unit = in_order(columns(own_start, split, half), sent_rest, 0)
     unit, noisy, seg_ids, plan, lag_mask, time_proj = lax.optimization_barrier(
         (unit, noisy, seg_ids, plan, lag_mask, time_proj)
     )
-    gather = gather_block if devices == 32 else gather_any
-    plane_ids, place, pieces, spots = gather(unit, device)
+    on_block = devices == 32
+    plane_ids, place, pieces, spots = (gather_block if on_block else gather_any)(unit, device)
+    rests = (gather_rest if on_block else gather_rest_any)(rest_unit, device)
     noisy_both = in_order(noisy, swap_core(noisy), 0)
     small = jnp.concatenate([plan, lag_mask], axis=1)
     small_both = in_order(small, swap_core(small), 0)
@@ -414,17 +526,18 @@
     usable = usable.astype(jnp.float32)
 
     chips = 4 if len(pieces) == 4 else 1
+    more = absorb_rest(places, stack, rests, 2 * rows)
     sums, planes = [], []
     for step, parts in enumerate(pieces):
-        last = step + 1 == len(pieces)
-        plane, *sums = absorb(step, last, places, stack, parts, spots[step], chips, 2 * rows, sums)
+        final = more if step + 1 == len(pieces) else []
+        plane, *sums = absorb(step, places, stack, parts, spots[step], chips, 2 * rows, sums, final)
         planes.append(plane)
     raw, past_raw, sums = sums
     latent, past_key = attend(
         True, inner, raw, sums, swap_core(sums), gains, tables, (usable, values, past_values),
         latent, factors[0], past_raw,
     )
-    raw, sums, values = project_latent(places, latent, swap_core(latent), mods, planes)
+    raw, sums, values = project_latent(places, latent, swap_core(latent), mods, planes, rests)
     (latent,) = attend(
         False, inner, raw, sums, swap_core(sums), gains, tables, (usable, values, past_values),
         latent, factors[1], past_key,

time: 182 us -> 189 us (1.038)
  the two profiles are of different devices: /device:TPU:0 before, /device:TPU:9 now
where the time goes in v3:
time: 189 us
  waiting for transfers between devices  69.1 us (37%)
  starting transfers between devices  59.7 us (32%)
  Pallas kernels  34.5 us (18%)
  other arithmetic  13.1 us (7%)
  local copies, waits for them, and re-layouts  11.1 us (6%)
    ppermute x43, waiting for transfers between devices, permute(): lax.ppermute(value, AXIS, [(s, t) for s, t in pairs if t is not None])  69.1 us
    ppermute x43, starting transfers between devices, permute(): lax.ppermute(value, AXIS, [(s, t) for s, t in pairs if t is not None])  59.7 us
    pallas_call x4, Pallas kernels, absorb(): pl.pallas_call(functools.partial(absorb_body, spots, step, bool(sums), la...  13.8 us
    pallas_call x2, Pallas kernels, attend(): pl.pallas_call(functools.partial(attend_body, first, inner), out_shape=sh...  10.1 us
    pallas_call x1, Pallas kernels, project_latent(): pl.pallas_call(project_body, in_specs=[pl.BlockSpec(memory_space=pltpu.SM...  7.31 us
    add x4, local copies, waits for them, and re-layouts, modulate(): result = normed * (1.0 + scale[:, None, :]) + shift[:, None, :]  3.93 us
  transfers between devices with their start and end apart: 43, of which 20 were waited for; matrix products, arithmetic and copies ran while one was open for 12% of the time, Pallas kernels for 7%

profile of v3, /device:TPU:9, one launch (start us, length us, event | category | flops | bytes accessed | tf_op | source)
XLA Modules:
  0.0 188.7 jit_solution(9815012197279567487)
XLA Ops:
  0.0 3.3 %collective-permute-start.3 = (bf16[64,2560]{1,0:T(8,128)(2,1)}, bf16[64,2560]{1,0:T(8,128)(2,1)}, u32[]{:S(2)}, u32[]{:S(2)}) collective-permute-start(bf16[64,2560]{1,0:T(8,128)(2,1)} %param.11), channel_id=1, source_target_pairs={{0,2},{1,3},{2,4},{3,5},{4,6},{5,7},{6,8},{7,9},{8,10},{9,11},{10,... | collective-permute-start | bytes 983048 | tf_op jit(solution)/shard_map/ppermute | solution.py:51
  3.3 1.0 collective-permute-start.5
  4.3 0.9 constant_dynamic-slice_fusion.3
  5.3 1.2 constant_dynamic-slice_fusion.7
  6.5 0.7 pad_maximum_fusion.4
  8.4 1.2 collective-permute-start.30
  9.7 1.2 collective-permute-start.31
  11.3 4.0 %collective-permute-done.30 = bf16[160,512]{1,0:T(8,128)(2,1)S(1)} collective-permute-done((bf16[160,512]{1,0:T(8,128)(2,1)}, bf16[160,512]{1,0:T(8,128)(2,1)S(1)}, u32[]{:S(2)}, u32[]{:S(2)}) %collective-permute-start.30) | collective-permute-done | bytes 163872 | tf_op jit(solution)/shard_map/ppermute | solution.py:51
  15.3 2.2 %collective-permute-start.32 = (bf16[80,512]{1,0:T(8,128)(2,1)S(1)}, bf16[80,512]{1,0:T(8,128)(2,1)S(1)}, u32[]{:S(2)}, u32[]{:S(2)}) collective-permute-start(bf16[80,512]{1,0:T(8,128)(2,1)S(1)} %slice.119), channel_id=1, source_target_pairs={{0,4},{1,5},{2,6},{3,7},{4,0},{5,1},{6,2},{7,3},{8,12},{9,13},{10,... | collective-permute-start | bytes 245768 | tf_op jit(solution)/shard_map/ppermute | solution.py:51
  17.7 1.7 collective-permute-done.32
  19.4 1.5 collective-permute-done.33
  20.9 3.2 %collective-permute-start.36 = (bf16[640,512]{1,0:T(8,128)(2,1)S(1)}, bf16[640,512]{1,0:T(8,128)(2,1)}, u32[]{:S(2)}, u32[]{:S(2)}) collective-permute-start(bf16[640,512]{1,0:T(8,128)(2,1)S(1)} %bitcast.65), channel_id=1, source_target_pairs={{8,16},{9,17},{10,18},{11,19},{12,20},{13,21},{14,22},{15,23},{16,... | collective-permute-start | bytes 1966088 | tf_op jit(solution)/shard_map/ppermute | solution.py:51
  24.3 1.1 broadcast_select_fusion.5
  25.4 0.9 pad_maximum_fusion.2.refs_0_
  28.2 1.5 collective-permute-start.7
  29.7 1.0 broadcast_select_fusion.6
  30.9 0.8 pad_maximum_fusion.7.refs_5_
  31.8 3.0 %collective-permute-start.2 = (s32[1,4]{0,1:T(4,128)S(1)}, s32[1,4]{0,1:T(4,128)S(1)}, u32[]{:S(2)}, u32[]{:S(2)}) collective-permute-start(s32[1,4]{0,1:T(4,128)S(1)} %copy.40), channel_id=1, source_target_pairs={{0,1},{1,0},{2,3},{3,2},{4,5},{5,4},{6,7},{7,6},{8,9},{9,8},{10,11... | collective-permute-start | bytes 56 | tf_op jit(solution)/shard_map/ppermute | solution.py:51
  34.9 0.8 collective-permute-done.2
  37.3 1.6 mul.215
  38.9 1.2 add.249
  40.1 2.7 %add.250 = f32[128,4,640]{2,1,0:T(4,128)} reshape(f32[2,64,2560]{2,1,0:T(8,128)} %add.249) | data formatting | bytes 2621440 | tf_op jit(solution)/shard_map/add | solution.py:45
  43.1 1.1 broadcast_select_fusion.8
  44.6 2.1 %collective-permute-start.6 = (bf16[160,2048]{1,0:T(8,128)(2,1)}, bf16[160,2048]{1,0:T(8,128)(2,1)S(1)}, u32[]{:S(2)}, u32[]{:S(2)}) collective-permute-start(bf16[160,2048]{1,0:T(8,128)(2,1)} %pad_maximum_fusion.2.refs_0_), channel_id=1, source_target_pairs={{8,16},{9,17},{10,18},{11,19},{12,20},{13,21},{14,22},{15,23},{16,... | collective-permute-start | bytes 1966088 | tf_op jit(solution)/shard_map/ppermute | solution.py:51
  48.0 4.5 %collective-permute-done.7.refs_0_ = bf16[160,2048]{1,0:T(8,128)(2,1)} collective-permute-done((bf16[160,2048]{1,0:T(8,128)(2,1)}, bf16[160,2048]{1,0:T(8,128)(2,1)}, u32[]{:S(2)}, u32[]{:S(2)}) %collective-permute-start.7) | collective-permute-done | bytes 655392 | tf_op jit(solution)/shard_map/ppermute | solution.py:51
  52.5 2.1 %collective-permute-start.8 = (bf16[160,2048]{1,0:T(8,128)(2,1)}, bf16[160,2048]{1,0:T(8,128)(2,1)S(1)}, u32[]{:S(2)}, u32[]{:S(2)}) collective-permute-start(bf16[160,2048]{1,0:T(8,128)(2,1)} %collective-permute-done.7.refs_0_), channel_id=1, source_target_pairs={{8,16},{9,17},{10,18},{11,19},{12,20},{13,21},{14,22},{15,23},{16,... | collective-permute-start | bytes 1966088 | tf_op jit(solution)/shard_map/ppermute | solution.py:51
  54.6 8.2 %collective-permute-done.6 = bf16[160,2048]{1,0:T(8,128)(2,1)S(1)} collective-permute-done((bf16[160,2048]{1,0:T(8,128)(2,1)}, bf16[160,2048]{1,0:T(8,128)(2,1)S(1)}, u32[]{:S(2)}, u32[]{:S(2)}) %collective-permute-start.6) | collective-permute-done | bytes 655392 | tf_op jit(solution)/shard_map/ppermute | solution.py:51
  62.8 1.3 collective-permute-start.9
  64.7 1.2 collective-permute-start.22
  65.9 1.1 collective-permute-start.21
  67.0 9.8 %collective-permute-done.8 = bf16[160,2048]{1,0:T(8,128)(2,1)S(1)} collective-permute-done((bf16[160,2048]{1,0:T(8,128)(2,1)}, bf16[160,2048]{1,0:T(8,128)(2,1)S(1)}, u32[]{:S(2)}, u32[]{:S(2)}) %collective-permute-start.8) | collective-permute-done | bytes 655392 | tf_op jit(solution)/shard_map/ppermute | solution.py:51
  76.8 1.3 collective-permute-start.37
  78.2 2.1 %collective-permute-start.35 = (bf16[640,512]{1,0:T(8,128)(2,1)}, bf16[640,512]{1,0:T(8,128)(2,1)S(1)}, u32[]{:S(2)}, u32[]{:S(2)}) collective-permute-start(bf16[640,512]{1,0:T(8,128)(2,1)} %collective-permute-done.34.refs_1_.refs_5_), channel_id=1, source_target_pairs={{8,16},{9,17},{10,18},{11,19},{12,20},{13,21},{14,22},{15,23},{16,... | collective-permute-start | bytes 1966088 | tf_op jit(solution)/shard_map/ppermute | solution.py:51
  80.4 1.4 collective-permute-start.10
  82.0 1.0 slice.118
  83.3 9.9 %collective-permute-done.21.refs_1_ = bf16[160,2048]{1,0:T(8,128)(2,1)S(1)} collective-permute-done((bf16[160,2048]{1,0:T(8,128)(2,1)}, bf16[160,2048]{1,0:T(8,128)(2,1)S(1)}, u32[]{:S(2)}, u32[]{:S(2)}) %collective-permute-start.21) | collective-permute-done | bytes 655392 | tf_op jit(solution)/shard_map/ppermute | solution.py:51
  93.3 1.1 collective-permute-start.27
  95.9 9.8 %collective-permute-done.10 = bf16[160,2048]{1,0:T(8,128)(2,1)S(1)} collective-permute-done((bf16[160,2048]{1,0:T(8,128)(2,1)S(1)}, bf16[160,2048]{1,0:T(8,128)(2,1)S(1)}, u32[]{:S(2)}, u32[]{:S(2)}) %collective-permute-start.10) | collective-permute-done | bytes 655392 | tf_op jit(solution)/shard_map/ppermute | solution.py:51
  105.7 4.3 %collective-permute-start.38 = (bf16[640,512]{1,0:T(8,128)(2,1)S(1)}, bf16[640,512]{1,0:T(8,128)(2,1)S(1)}, u32[]{:S(2)}, u32[]{:S(2)}) collective-permute-start(bf16[640,512]{1,0:T(8,128)(2,1)S(1)} %broadcast_select_fusion.1.refs_2_.refs_6_), channel_id=1, source_target_pairs={{8,0},{9,1},{10,2},{11,3},{12,4},{13,5},{14,6},{15,7},{16,24},{17,... | collective-permute-start | bytes 1966088 | tf_op jit(solution)/shard_map/ppermute | solution.py:51
  110.1 1.9 collective-permute-done.18.refs_2_
  112.4 1.3 collective-permute-start.23
  113.7 1.1 collective-permute-start.20
  114.8 4.9 %collective-permute-done.24.refs_4_ = bf16[80,2048]{1,0:T(8,128)(2,1)S(1)} collective-permute-done((bf16[80,2048]{1,0:T(8,128)(2,1)S(1)}, bf16[80,2048]{1,0:T(8,128)(2,1)S(1)}, u32[]{:S(2)}, u32[]{:S(2)}) %collective-permute-start.24) | collective-permute-done | bytes 327712 | tf_op jit(solution)/shard_map/ppermute | solution.py:51
  119.7 1.1 collective-permute-start.14
  122.3 1.2 collective-permute-start.12
  124.4 1.2 collective-permute-start.19
  125.7 3.4 %collective-permute-done.14.refs_4_ = bf16[80,2048]{1,0:T(8,128)(2,1)S(1)} collective-permute-done((bf16[80,2048]{1,0:T(8,128)(2,1)S(1)}, bf16[80,2048]{1,0:T(8,128)(2,1)S(1)}, u32[]{:S(2)}, u32[]{:S(2)}) %collective-permute-start.14) | collective-permute-done | bytes 327712 | tf_op jit(solution)/shard_map/ppermute | solution.py:51
  129.1 2.4 %collective-permute-done.11.refs_1_ = bf16[80,2048]{1,0:T(8,128)(2,1)S(1)} collective-permute-done((bf16[80,2048]{1,0:T(8,128)(2,1)S(1)}, bf16[80,2048]{1,0:T(8,128)(2,1)S(1)}, u32[]{:S(2)}, u32[]{:S(2)}) %collective-permute-start.11) | collective-permute-done | bytes 327712 | tf_op jit(solution)/shard_map/ppermute | solution.py:51
  131.4 1.2 collective-permute-start.15
  132.8 3.4 %absorb.4 = (bf16[4,160,2048]{2,1,0:T(8,128)(2,1)}, f32[128,2048]{1,0:T(8,128)S(1)}, f32[192,1024]{1,0:T(8,128)S(1)}) custom-call(s32[6]{0:T(128)S(1)} %stack.27.places_ref, bf16[4,320,640]{2,1,0:T(8,128)(2,1)S(1)} %maximum_bitcast_fusion.hidden_ref, bf16[160,2048]{1,0:T(8,128)(2,1)} %pad_maximum_fusion.2.refs_0_, ...), custom_call_target="tpu_custom_call" | custom-call | tf_op jit(solution)/shard_map/absorb/pallas_call | solution.py:226
  136.3 3.2 %absorb.5 = (bf16[4,160,2048]{2,1,0:T(8,128)(2,1)}, f32[128,2048]{1,0:T(8,128)S(1)}, f32[192,1024]{1,0:T(8,128)S(1)}) custom-call(s32[6]{0:T(128)S(1)} %stack.27.places_ref, bf16[4,320,640]{2,1,0:T(8,128)(2,1)S(1)} %maximum_bitcast_fusion.hidden_ref, bf16[160,2048]{1,0:T(8,128)(2,1)} %collective-permute-done.7.refs_0_, ...), custom_call_target="tpu_custom_call" | custom-call | tf_op jit(solution)/shard_map/absorb/pallas_call | solution.py:226
  139.4 1.2 broadcast_select_fusion.refs_3_.refs_7_
  140.6 3.2 %absorb_rest.1 = (f32[128,512]{1,0:T(8,128)S(1)}, f32[192,256]{1,0:T(8,128)S(1)}) custom-call(s32[6]{0:T(128)S(1)} %stack.27.places_ref, bf16[4,320,640]{2,1,0:T(8,128)(2,1)S(1)} %maximum_bitcast_fusion.hidden_ref, bf16[640,512]{1,0:T(8,128)(2,1)S(1)} %bitcast.67, bf16[640,512]{1,0:T(8,128)(2,1)} %collective-permute-done.34.refs_1_.refs_5_, ...), custom_call_target="tpu_custom_call" | custom-call | tf_op jit(solution)/shard_map/absorb_rest/pallas_call | solution.py:267
  143.9 3.0 %absorb.6 = (bf16[4,160,2048]{2,1,0:T(8,128)(2,1)}, f32[128,2048]{1,0:T(8,128)S(1)}, f32[192,1024]{1,0:T(8,128)S(1)}) custom-call(s32[6]{0:T(128)S(1)} %stack.27.places_ref, bf16[4,320,640]{2,1,0:T(8,128)(2,1)S(1)} %maximum_bitcast_fusion.hidden_ref, bf16[160,2048]{1,0:T(8,128)(2,1)S(1)} %broadcast_select_fusion.3.refs_0_, ...), custom_call_target="tpu_custom_call" | custom-call | tf_op jit(solution)/shard_map/absorb/pallas_call | solution.py:226
  147.0 4.2 %absorb.7 = (bf16[4,160,2048]{2,1,0:T(8,128)(2,1)}, f32[128,2560]{1,0:T(8,128)S(1)}, f32[192,1280]{1,0:T(8,128)S(1)}, f32[448,128]{1,0:T(8,128)S(1)}) custom-call(s32[6]{0:T(128)S(1)} %stack.27.places_ref, bf16[4,320,640]{2,1,0:T(8,128)(2,1)S(1)} %maximum_bitcast_fusion.hidden_ref, bf16[160,2048]{1,0:T(8,128)(2,1)S(1)} %broadcast_select_fusion.2.refs_0_, ...), custom_call_target="tpu_custom_call" | custom-call | tf_op jit(solution)/shard_map/absorb/pallas_call | solution.py:226
  151.2 12.7 %collective-permute-start.39 = (f32[448,128]{1,0:T(8,128)S(1)}, f32[448,128]{1,0:T(8,128)S(1)}, u32[]{:S(2)}, u32[]{:S(2)}) collective-permute-start(f32[448,128]{1,0:T(8,128)S(1)} %get-tuple-element.45.refs_1_), channel_id=1, source_target_pairs={{0,1},{1,0},{2,3},{3,2},{4,5},{5,4},{6,7},{7,6},{8,9},{9,8},{10,11... | collective-permute-start | bytes 688136 | tf_op jit(solution)/shard_map/ppermute | solution.py:51
  163.9 1.1 collective-permute-done.39.refs_2_
  164.9 4.7 %attend.2 = (bf16[128,1280]{1,0:T(8,128)(2,1)S(1)}, bf16[192,1280]{1,0:T(8,128)(2,1)}) custom-call(f32[128,2560]{1,0:T(8,128)S(1)} %get-tuple-element.44.refs_0_, f32[448,128]{1,0:T(8,128)S(1)} %get-tuple-element.45.refs_1_, f32[448,128]{1,0:T(8,128)S(1)} %collective-permute-done.39.refs_2_, f32[1,1280]{1,0:T(1,128)S(1)} %broadcast_in_dim.19.refs_3_, ...), custom_call_target="tpu_custom_call" | custom-call | tf_op jit(solution)/shard_map/attend/pallas_call | solution.py:344
  170.0 1.3 collective-permute-done.40.other_ref
  171.2 7.3 %project.1 = (f32[128,2560]{1,0:T(8,128)}, f32[256,128]{1,0:T(8,128)}, bf16[128,1280]{1,0:T(8,128)(2,1)}) custom-call(s32[6]{0:T(128)S(1)} %stack.27.places_ref, bf16[128,1280]{1,0:T(8,128)(2,1)S(1)} %get-tuple-element.48.own_ref.refs_10_, bf16[128,1280]{1,0:T(8,128)(2,1)S(1)} %collective-permute-done.40.other_ref, f32[5,7680]{1,0:T(8,128)S(1)} %fusion.14.mod_ref, ...), custom_call_target="tpu_custom_call" | custom-call | tf_op jit(solution)/shard_map/project/pallas_call | solution.py:422
  179.1 1.1 collective-permute-done.41.refs_2_
  180.9 5.5 %attend.3 = bf16[128,1280]{1,0:T(8,128)(2,1)S(1)} custom-call(f32[128,2560]{1,0:T(8,128)} %get-tuple-element.53.refs_0_, f32[256,128]{1,0:T(8,128)} %get-tuple-element.54.refs_1_, f32[256,128]{1,0:T(8,128)} %copy-done.14, f32[1,1280]{1,0:T(1,128)S(1)} %broadcast_in_dim.19.refs_3_, f32[1,1280]{1,0:T(1,128)S(1)} %broadcast_in_dim.20.refs_4_, ...), custom_call_target="tpu_custom_call" | custom-call | tf_op jit(solution)/shard_map/attend/pallas_call | solution.py:344
  186.8 1.0 collective-permute-done.42
  187.9 0.7 pad_maximum_fusion.5
  (159 shorter events, 15.3 us)
Async XLA Ops:
  0.0 36.4 %copy-start = (bf16[128,7680]{1,0:T(8,128)(2,1)S(1)}, bf16[128,7680]{1,0:T(8,128)(2,1)}, u32[]{:S(2)}) copy-start(bf16[128,7680]{1,0:T(8,128)(2,1)} %param.17) | copy-start | bytes 5898244
  0.0 10.9 %copy-start.15 = (f32[2560]{0:T(1024)S(1)}, f32[2560]{0:T(1024)}, u32[]{:S(2)}) copy-start(f32[2560]{0:T(1024)} %param.18) | copy-start | bytes 30724
  0.0 11.0 %copy-start.16 = (f32[2560]{0:T(1024)S(1)}, f32[2560]{0:T(1024)}, u32[]{:S(2)}) copy-start(f32[2560]{0:T(1024)} %param.19) | copy-start | bytes 30724
  0.0 31.8 %collective-permute-start.3 = (bf16[64,2560]{1,0:T(8,128)(2,1)}, bf16[64,2560]{1,0:T(8,128)(2,1)}, u32[]{:S(2)}, u32[]{:S(2)}) collective-permute-start(bf16[64,2560]{1,0:T(8,128)(2,1)} %param.11), channel_id=1, source_target_pairs={{0,2},{1,3},{2,4},{3,5},{4,6},{5,7},{6,8},{7,9},{8,10},{9,11},{10,... | collective-permute-start | bytes 983048 | tf_op jit(solution)/shard_map/ppermute | solution.py:51
  3.3 25.0 %collective-permute-start.5 = (bf16[64,2560]{1,0:T(8,128)(2,1)}, bf16[64,2560]{1,0:T(8,128)(2,1)}, u32[]{:S(2)}, u32[]{:S(2)}) collective-permute-start(bf16[64,2560]{1,0:T(8,128)(2,1)} %param.11), channel_id=1, source_target_pairs={{0,1},{1,0},{2,3},{3,2},{4,5},{5,4},{6,7},{7,6},{8,9},{9,8},{10,11... | collective-permute-start | bytes 983048 | tf_op jit(solution)/shard_map/ppermute | solution.py:51
  5.2 2.6 %collective-permute-start.29 = (bf16[80,512]{1,0:T(8,128)(2,1)S(1)}, bf16[80,512]{1,0:T(8,128)(2,1)S(1)}, u32[]{:S(2)}, u32[]{:S(2)}) collective-permute-start(bf16[80,512]{1,0:T(8,128)(2,1)S(1)} %pad_maximum_fusion.10), channel_id=1, source_target_pairs={{0,1},{1,0},{2,3},{3,2},{4,5},{5,4},{6,7},{7,6},{8,9},{9,8},{10,11... | collective-permute-start | bytes 245768 | tf_op jit(solution)/shard_map/ppermute | solution.py:51
  7.2 17.0 %collective-permute-start = (bf16[80,2048]{1,0:T(8,128)(2,1)}, bf16[80,2048]{1,0:T(8,128)(2,1)}, u32[]{:S(2)}, u32[]{:S(2)}) collective-permute-start(bf16[80,2048]{1,0:T(8,128)(2,1)} %pad_maximum_fusion.4), channel_id=1, source_target_pairs={{0,1},{1,0},{2,3},{3,2},{4,5},{5,4},{6,7},{7,6},{8,9},{9,8},{10,11... | collective-permute-start | bytes 983048 | tf_op jit(solution)/shard_map/ppermute | solution.py:51
  8.4 6.9 %collective-permute-start.30 = (bf16[160,512]{1,0:T(8,128)(2,1)}, bf16[160,512]{1,0:T(8,128)(2,1)S(1)}, u32[]{:S(2)}, u32[]{:S(2)}) collective-permute-start(bf16[160,512]{1,0:T(8,128)(2,1)} %pad_maximum_fusion.6), channel_id=1, source_target_pairs={{0,2},{1,3},{2,0},{3,1},{4,6},{5,7},{6,4},{7,5},{8,10},{9,11},{10,... | collective-permute-start | bytes 491528 | tf_op jit(solution)/shard_map/ppermute | solution.py:51
  9.7 7.9 %collective-permute-start.31 = (bf16[160,512]{1,0:T(8,128)(2,1)}, bf16[160,512]{1,0:T(8,128)(2,1)S(1)}, u32[]{:S(2)}, u32[]{:S(2)}) collective-permute-start(bf16[160,512]{1,0:T(8,128)(2,1)} %pad_maximum_fusion.6), channel_id=1, source_target_pairs={{0,4},{1,5},{2,6},{3,7},{4,0},{5,1},{6,2},{7,3},{8,12},{9,13},{10,... | collective-permute-start | bytes 491528 | tf_op jit(solution)/shard_map/ppermute | solution.py:51
  11.2 15.1 %copy-start.7 = (s32[32]{0:T(128)S(1)}, s32[32]{0:T(128)}, u32[]{:S(2)}) copy-start(s32[32]{0:T(128)} %param.12) | copy-start | bytes 388
  15.3 4.0 %collective-permute-start.32 = (bf16[80,512]{1,0:T(8,128)(2,1)S(1)}, bf16[80,512]{1,0:T(8,128)(2,1)S(1)}, u32[]{:S(2)}, u32[]{:S(2)}) collective-permute-start(bf16[80,512]{1,0:T(8,128)(2,1)S(1)} %slice.119), channel_id=1, source_target_pairs={{0,4},{1,5},{2,6},{3,7},{4,0},{5,1},{6,2},{7,3},{8,12},{9,13},{10,... | collective-permute-start | bytes 245768 | tf_op jit(solution)/shard_map/ppermute | solution.py:51
  17.5 3.4 %collective-permute-start.33 = (bf16[80,512]{1,0:T(8,128)(2,1)S(1)}, bf16[80,512]{1,0:T(8,128)(2,1)S(1)}, u32[]{:S(2)}, u32[]{:S(2)}) collective-permute-start(bf16[80,512]{1,0:T(8,128)(2,1)S(1)} %slice.120), channel_id=1, source_target_pairs={{0,2},{1,3},{2,0},{3,1},{4,6},{5,7},{6,4},{7,5},{8,10},{9,11},{10,... | collective-permute-start | bytes 245768 | tf_op jit(solution)/shard_map/ppermute | solution.py:51
  20.9 119.7 %copy-start.4 = (bf16[4,160,512]{2,1,0:T(8,128)(2,1)}, bf16[4,160,512]{2,1,0:T(8,128)(2,1)S(1)}, u32[]{:S(2)}) copy-start(bf16[4,160,512]{2,1,0:T(8,128)(2,1)S(1)} %fusion.7) | copy-start | bytes 1966084
  20.9 43.4 %collective-permute-start.36 = (bf16[640,512]{1,0:T(8,128)(2,1)S(1)}, bf16[640,512]{1,0:T(8,128)(2,1)}, u32[]{:S(2)}, u32[]{:S(2)}) collective-permute-start(bf16[640,512]{1,0:T(8,128)(2,1)S(1)} %bitcast.65), channel_id=1, source_target_pairs={{8,16},{9,17},{10,18},{11,19},{12,20},{13,21},{14,22},{15,23},{16,... | collective-permute-start | bytes 1966088 | tf_op jit(solution)/shard_map/ppermute | solution.py:51
  24.1 40.5 %collective-permute-start.34 = (bf16[640,512]{1,0:T(8,128)(2,1)S(1)}, bf16[640,512]{1,0:T(8,128)(2,1)}, u32[]{:S(2)}, u32[]{:S(2)}) collective-permute-start(bf16[640,512]{1,0:T(8,128)(2,1)S(1)} %bitcast.66), channel_id=1, source_target_pairs={{0,8},{1,9},{2,10},{3,11},{4,12},{5,13},{6,14},{7,15},{8,0},{9,1},... | collective-permute-start | bytes 1966088 | tf_op jit(solution)/shard_map/ppermute | solution.py:51
  24.2 6.5 %copy-start.17 = (s32[1,2]{1,0:T(1,128)S(1)}, s32[1,2]{1,0:T(1,128)}, u32[]{:S(2)}) copy-start(s32[1,2]{1,0:T(1,128)} %param.13) | copy-start | bytes 28
  24.2 6.5 %copy-start.18 = (s32[1,2]{1,0:T(1,128)S(1)}, s32[1,2]{1,0:T(1,128)}, u32[]{:S(2)}) copy-start(s32[1,2]{1,0:T(1,128)} %param.14) | copy-start | bytes 28
  27.3 38.6 %collective-permute-start.26 = (bf16[160,2048]{1,0:T(8,128)(2,1)}, bf16[160,2048]{1,0:T(8,128)(2,1)}, u32[]{:S(2)}, u32[]{:S(2)}) collective-permute-start(bf16[160,2048]{1,0:T(8,128)(2,1)} %pad_maximum_fusion.2.refs_0_), channel_id=1, source_target_pairs={{0,4},{1,5},{2,6},{3,7},{4,0},{5,1},{6,2},{7,3},{8,12},{9,13},{10,... | collective-permute-start | bytes 1966088 | tf_op jit(solution)/shard_map/ppermute | solution.py:51
  28.2 24.3 %collective-permute-start.7 = (bf16[160,2048]{1,0:T(8,128)(2,1)}, bf16[160,2048]{1,0:T(8,128)(2,1)}, u32[]{:S(2)}, u32[]{:S(2)}) collective-permute-start(bf16[160,2048]{1,0:T(8,128)(2,1)} %pad_maximum_fusion.2.refs_0_), channel_id=1, source_target_pairs={{0,8},{1,9},{2,10},{3,11},{4,12},{5,13},{6,14},{7,15},{8,0},{9,1},... | collective-permute-start | bytes 1966088 | tf_op jit(solution)/shard_map/ppermute | solution.py:51
  31.8 3.8 %collective-permute-start.2 = (s32[1,4]{0,1:T(4,128)S(1)}, s32[1,4]{0,1:T(4,128)S(1)}, u32[]{:S(2)}, u32[]{:S(2)}) collective-permute-start(s32[1,4]{0,1:T(4,128)S(1)} %copy.40), channel_id=1, source_target_pairs={{0,1},{1,0},{2,3},{3,2},{4,5},{5,4},{6,7},{7,6},{8,9},{9,8},{10,11... | collective-permute-start | bytes 56 | tf_op jit(solution)/shard_map/ppermute | solution.py:51
  35.7 7.2 %collective-permute-start.4 = (bf16[64,2560]{1,0:T(8,128)(2,1)}, bf16[64,2560]{1,0:T(8,128)(2,1)}, u32[]{:S(2)}, u32[]{:S(2)}) collective-permute-start(bf16[64,2560]{1,0:T(8,128)(2,1)} %collective-permute-done.3), channel_id=1, source_target_pairs={{0,1},{1,0},{2,3},{3,2},{4,5},{5,4},{6,7},{7,6},{8,9},{9,8},{10,11... | collective-permute-start | bytes 983048 | tf_op jit(solution)/shard_map/ppermute | solution.py:51
  37.3 2.8 %copy-start.8 = (f32[2,64,2560]{2,1,0:T(8,128)}, f32[2,64,2560]{2,1,0:T(8,128)S(1)}, u32[]{:S(2)}) copy-start(f32[2,64,2560]{2,1,0:T(8,128)S(1)} %mul.214) | copy-start | bytes 3932164
  38.9 4.0 %copy-start.13 = (bf16[64,2560]{1,0:T(8,128)(2,1)S(1)}, bf16[64,2560]{1,0:T(8,128)(2,1)}, u32[]{:S(2)}) copy-start(bf16[64,2560]{1,0:T(8,128)(2,1)} %param.10) | copy-start | bytes 983044
  42.9 1.7 collective-permute-start.1
  44.6 18.2 %collective-permute-start.6 = (bf16[160,2048]{1,0:T(8,128)(2,1)}, bf16[160,2048]{1,0:T(8,128)(2,1)S(1)}, u32[]{:S(2)}, u32[]{:S(2)}) collective-permute-start(bf16[160,2048]{1,0:T(8,128)(2,1)} %pad_maximum_fusion.2.refs_0_), channel_id=1, source_target_pairs={{8,16},{9,17},{10,18},{11,19},{12,20},{13,21},{14,22},{15,23},{16,... | collective-permute-start | bytes 1966088 | tf_op jit(solution)/shard_map/ppermute | solution.py:51
  48.0 33.7 %copy-start.9 = (f32[2,64,2560]{2,1,0:T(8,128)S(1)}, f32[2,64,2560]{2,1,0:T(8,128)}, u32[]{:S(2)}) copy-start(f32[2,64,2560]{2,1,0:T(8,128)} %copy-done.8) | copy-start | bytes 3932164
  48.0 33.8 %copy-start.10 = (f32[2,64,2560]{2,1,0:T(8,128)S(1)}, f32[2,64,2560]{2,1,0:T(8,128)}, u32[]{:S(2)}) copy-start(f32[2,64,2560]{2,1,0:T(8,128)} %add.249) | copy-start | bytes 3932164
  52.5 24.3 %collective-permute-start.8 = (bf16[160,2048]{1,0:T(8,128)(2,1)}, bf16[160,2048]{1,0:T(8,128)(2,1)S(1)}, u32[]{:S(2)}, u32[]{:S(2)}) collective-permute-start(bf16[160,2048]{1,0:T(8,128)(2,1)} %collective-permute-done.7.refs_0_), channel_id=1, source_target_pairs={{8,16},{9,17},{10,18},{11,19},{12,20},{13,21},{14,22},{15,23},{16,... | collective-permute-start | bytes 1966088 | tf_op jit(solution)/shard_map/ppermute | solution.py:51
  62.8 15.4 %collective-permute-start.9 = (bf16[160,2048]{1,0:T(8,128)(2,1)S(1)}, bf16[160,2048]{1,0:T(8,128)(2,1)S(1)}, u32[]{:S(2)}, u32[]{:S(2)}) collective-permute-start(bf16[160,2048]{1,0:T(8,128)(2,1)S(1)} %collective-permute-done.6), channel_id=1, source_target_pairs={{8,0},{9,1},{10,2},{11,3},{12,4},{13,5},{14,6},{15,7},{16,24},{17,... | collective-permute-start | bytes 1966088 | tf_op jit(solution)/shard_map/ppermute | solution.py:51
  64.3 16.0 %collective-permute-start.25 = (bf16[160,2048]{1,0:T(8,128)(2,1)}, bf16[160,2048]{1,0:T(8,128)(2,1)S(1)}, u32[]{:S(2)}, u32[]{:S(2)}) collective-permute-start(bf16[160,2048]{1,0:T(8,128)(2,1)} %pad_maximum_fusion.2.refs_0_), channel_id=1, source_target_pairs={{0,2},{1,3},{2,0},{3,1},{4,6},{5,7},{6,4},{7,5},{8,10},{9,11},{10,... | collective-permute-start | bytes 1966088 | tf_op jit(solution)/shard_map/ppermute | solution.py:51
  64.7 18.3 %collective-permute-start.22 = (bf16[160,2048]{1,0:T(8,128)(2,1)}, bf16[160,2048]{1,0:T(8,128)(2,1)S(1)}, u32[]{:S(2)}, u32[]{:S(2)}) collective-permute-start(bf16[160,2048]{1,0:T(8,128)(2,1)} %collective-permute-done.7.refs_0_), channel_id=1, source_target_pairs={{0,4},{1,5},{2,6},{3,7},{4,0},{5,1},{6,2},{7,3},{8,12},{9,13},{10,... | collective-permute-start | bytes 1966088 | tf_op jit(solution)/shard_map/ppermute | solution.py:51
  65.9 27.4 %collective-permute-start.21 = (bf16[160,2048]{1,0:T(8,128)(2,1)}, bf16[160,2048]{1,0:T(8,128)(2,1)S(1)}, u32[]{:S(2)}, u32[]{:S(2)}) collective-permute-start(bf16[160,2048]{1,0:T(8,128)(2,1)} %collective-permute-done.7.refs_0_), channel_id=1, source_target_pairs={{0,2},{1,3},{2,0},{3,1},{4,6},{5,7},{6,4},{7,5},{8,10},{9,11},{10,... | collective-permute-start | bytes 1966088 | tf_op jit(solution)/shard_map/ppermute | solution.py:51
  76.8 17.6 %collective-permute-start.37 = (bf16[640,512]{1,0:T(8,128)(2,1)}, bf16[640,512]{1,0:T(8,128)(2,1)S(1)}, u32[]{:S(2)}, u32[]{:S(2)}) collective-permute-start(bf16[640,512]{1,0:T(8,128)(2,1)} %collective-permute-done.36), channel_id=1, source_target_pairs={{8,0},{9,1},{10,2},{11,3},{12,4},{13,5},{14,6},{15,7},{16,24},{17,... | collective-permute-start | bytes 1966088 | tf_op jit(solution)/shard_map/ppermute | solution.py:51
  78.2 17.4 %collective-permute-start.35 = (bf16[640,512]{1,0:T(8,128)(2,1)}, bf16[640,512]{1,0:T(8,128)(2,1)S(1)}, u32[]{:S(2)}, u32[]{:S(2)}) collective-permute-start(bf16[640,512]{1,0:T(8,128)(2,1)} %collective-permute-done.34.refs_1_.refs_5_), channel_id=1, source_target_pairs={{8,16},{9,17},{10,18},{11,19},{12,20},{13,21},{14,22},{15,23},{16,... | collective-permute-start | bytes 1966088 | tf_op jit(solution)/shard_map/ppermute | solution.py:51
  80.4 25.4 %collective-permute-start.10 = (bf16[160,2048]{1,0:T(8,128)(2,1)S(1)}, bf16[160,2048]{1,0:T(8,128)(2,1)S(1)}, u32[]{:S(2)}, u32[]{:S(2)}) collective-permute-start(bf16[160,2048]{1,0:T(8,128)(2,1)S(1)} %broadcast_select_fusion.3.refs_0_), channel_id=1, source_target_pairs={{8,0},{9,1},{10,2},{11,3},{12,4},{13,5},{14,6},{15,7},{16,24},{17,... | collective-permute-start | bytes 1966088 | tf_op jit(solution)/shard_map/ppermute | solution.py:51
  83.0 29.4 %collective-permute-start.28 = (bf16[80,2048]{1,0:T(8,128)(2,1)S(1)}, bf16[80,2048]{1,0:T(8,128)(2,1)S(1)}, u32[]{:S(2)}, u32[]{:S(2)}) collective-permute-start(bf16[80,2048]{1,0:T(8,128)(2,1)S(1)} %slice.118), channel_id=1, source_target_pairs={{0,2},{1,3},{2,0},{3,1},{4,6},{5,7},{6,4},{7,5},{8,10},{9,11},{10,... | collective-permute-start | bytes 983048 | tf_op jit(solution)/shard_map/ppermute | solution.py:51
  93.3 20.4 %collective-permute-start.27 = (bf16[80,2048]{1,0:T(8,128)(2,1)S(1)}, bf16[80,2048]{1,0:T(8,128)(2,1)S(1)}, u32[]{:S(2)}, u32[]{:S(2)}) collective-permute-start(bf16[80,2048]{1,0:T(8,128)(2,1)S(1)} %slice.117), channel_id=1, source_target_pairs={{0,4},{1,5},{2,6},{3,7},{4,0},{5,1},{6,2},{7,3},{8,12},{9,13},{10,... | collective-permute-start | bytes 983048 | tf_op jit(solution)/shard_map/ppermute | solution.py:51
  94.5 17.5 %collective-permute-start.18 = (bf16[160,2048]{1,0:T(8,128)(2,1)S(1)}, bf16[160,2048]{1,0:T(8,128)(2,1)S(1)}, u32[]{:S(2)}, u32[]{:S(2)}) collective-permute-start(bf16[160,2048]{1,0:T(8,128)(2,1)S(1)} %broadcast_select_fusion.3.refs_0_), channel_id=1, source_target_pairs={{0,4},{1,5},{2,6},{3,7},{4,0},{5,1},{6,2},{7,3},{8,12},{9,13},{10,... | collective-permute-start | bytes 1966088 | tf_op jit(solution)/shard_map/ppermute | solution.py:51
  95.5 25.3 %collective-permute-start.17 = (bf16[160,2048]{1,0:T(8,128)(2,1)S(1)}, bf16[160,2048]{1,0:T(8,128)(2,1)S(1)}, u32[]{:S(2)}, u32[]{:S(2)}) collective-permute-start(bf16[160,2048]{1,0:T(8,128)(2,1)S(1)} %broadcast_select_fusion.3.refs_0_), channel_id=1, source_target_pairs={{0,2},{1,3},{2,0},{3,1},{4,6},{5,7},{6,4},{7,5},{8,10},{9,11},{10,... | collective-permute-start | bytes 1966088 | tf_op jit(solution)/shard_map/ppermute | solution.py:51
  95.9 44.7 %copy-start.2 = (bf16[640,512]{1,0:T(8,128)(2,1)}, bf16[640,512]{1,0:T(8,128)(2,1)S(1)}, u32[]{:S(2)}) copy-start(bf16[640,512]{1,0:T(8,128)(2,1)S(1)} %broadcast_select_fusion.1.refs_2_.refs_6_) | copy-start | bytes 1966084
  105.7 17.8 %collective-permute-start.38 = (bf16[640,512]{1,0:T(8,128)(2,1)S(1)}, bf16[640,512]{1,0:T(8,128)(2,1)S(1)}, u32[]{:S(2)}, u32[]{:S(2)}) collective-permute-start(bf16[640,512]{1,0:T(8,128)(2,1)S(1)} %broadcast_select_fusion.1.refs_2_.refs_6_), channel_id=1, source_target_pairs={{8,0},{9,1},{10,2},{11,3},{12,4},{13,5},{14,6},{15,7},{16,24},{17,... | collective-permute-start | bytes 1966088 | tf_op jit(solution)/shard_map/ppermute | solution.py:51
  112.0 7.7 %collective-permute-start.24 = (bf16[80,2048]{1,0:T(8,128)(2,1)S(1)}, bf16[80,2048]{1,0:T(8,128)(2,1)S(1)}, u32[]{:S(2)}, u32[]{:S(2)}) collective-permute-start(bf16[80,2048]{1,0:T(8,128)(2,1)S(1)} %slice.116), channel_id=1, source_target_pairs={{0,2},{1,3},{2,0},{3,1},{4,6},{5,7},{6,4},{7,5},{8,10},{9,11},{10,... | collective-permute-start | bytes 983048 | tf_op jit(solution)/shard_map/ppermute | solution.py:51
  112.3 9.4 %copy-start.11 = (f32[128,4,640]{2,1,0:T(4,128)S(1)}, f32[128,4,640]{2,1,0:T(4,128)}, u32[]{:S(2)}) copy-start(f32[128,4,640]{2,1,0:T(4,128)} %mul.215) | copy-start | bytes 3932164
  112.3 9.4 %copy-start.12 = (f32[128,4,640]{2,1,0:T(4,128)S(1)}, f32[128,4,640]{2,1,0:T(4,128)}, u32[]{:S(2)}) copy-start(f32[128,4,640]{2,1,0:T(4,128)} %add.250) | copy-start | bytes 3932164
  112.4 9.9 %collective-permute-start.23 = (bf16[80,2048]{1,0:T(8,128)(2,1)S(1)}, bf16[80,2048]{1,0:T(8,128)(2,1)S(1)}, u32[]{:S(2)}, u32[]{:S(2)}) collective-permute-start(bf16[80,2048]{1,0:T(8,128)(2,1)S(1)} %slice.115), channel_id=1, source_target_pairs={{0,4},{1,5},{2,6},{3,7},{4,0},{5,1},{6,2},{7,3},{8,12},{9,13},{10,... | collective-permute-start | bytes 983048 | tf_op jit(solution)/shard_map/ppermute | solution.py:51
  113.7 10.8 %collective-permute-start.20 = (bf16[80,2048]{1,0:T(8,128)(2,1)S(1)}, bf16[80,2048]{1,0:T(8,128)(2,1)S(1)}, u32[]{:S(2)}, u32[]{:S(2)}) collective-permute-start(bf16[80,2048]{1,0:T(8,128)(2,1)S(1)} %slice.114), channel_id=1, source_target_pairs={{0,2},{1,3},{2,0},{3,1},{4,6},{5,7},{6,4},{7,5},{8,10},{9,11},{10,... | collective-permute-start | bytes 983048 | tf_op jit(solution)/shard_map/ppermute | solution.py:51
  119.7 9.4 %collective-permute-start.14 = (bf16[80,2048]{1,0:T(8,128)(2,1)S(1)}, bf16[80,2048]{1,0:T(8,128)(2,1)S(1)}, u32[]{:S(2)}, u32[]{:S(2)}) collective-permute-start(bf16[80,2048]{1,0:T(8,128)(2,1)S(1)} %get-tuple-element.67), channel_id=1, source_target_pairs={{0,4},{1,5},{2,6},{3,7},{4,0},{5,1},{6,2},{7,3},{8,12},{9,13},{10,... | collective-permute-start | bytes 983048 | tf_op jit(solution)/shard_map/ppermute | solution.py:51
  120.8 10.6 %collective-permute-start.11 = (bf16[80,2048]{1,0:T(8,128)(2,1)S(1)}, bf16[80,2048]{1,0:T(8,128)(2,1)S(1)}, u32[]{:S(2)}, u32[]{:S(2)}) collective-permute-start(bf16[80,2048]{1,0:T(8,128)(2,1)S(1)} %get-tuple-element.68), channel_id=1, source_target_pairs={{0,2},{1,3},{2,0},{3,1},{4,6},{5,7},{6,4},{7,5},{8,10},{9,11},{10,... | collective-permute-start | bytes 983048 | tf_op jit(solution)/shard_map/ppermute | solution.py:51
  122.3 24.6 %collective-permute-start.12 = (bf16[80,2048]{1,0:T(8,128)(2,1)S(1)}, bf16[80,2048]{1,0:T(8,128)(2,1)S(1)}, u32[]{:S(2)}, u32[]{:S(2)}) collective-permute-start(bf16[80,2048]{1,0:T(8,128)(2,1)S(1)} %get-tuple-element.67), channel_id=1, source_target_pairs={{0,2},{1,3},{2,0},{3,1},{4,6},{5,7},{6,4},{7,5},{8,10},{9,11},{10,... | collective-permute-start | bytes 983048 | tf_op jit(solution)/shard_map/ppermute | solution.py:51
  123.5 23.4 %collective-permute-start.13 = (bf16[80,2048]{1,0:T(8,128)(2,1)S(1)}, bf16[80,2048]{1,0:T(8,128)(2,1)S(1)}, u32[]{:S(2)}, u32[]{:S(2)}) collective-permute-start(bf16[80,2048]{1,0:T(8,128)(2,1)S(1)} %get-tuple-element.68), channel_id=1, source_target_pairs={{0,4},{1,5},{2,6},{3,7},{4,0},{5,1},{6,2},{7,3},{8,12},{9,13},{10,... | collective-permute-start | bytes 983048 | tf_op jit(solution)/shard_map/ppermute | solution.py:51
  124.4 19.5 %collective-permute-start.19 = (bf16[80,2048]{1,0:T(8,128)(2,1)S(1)}, bf16[80,2048]{1,0:T(8,128)(2,1)S(1)}, u32[]{:S(2)}, u32[]{:S(2)}) collective-permute-start(bf16[80,2048]{1,0:T(8,128)(2,1)S(1)} %slice.113), channel_id=1, source_target_pairs={{0,4},{1,5},{2,6},{3,7},{4,0},{5,1},{6,2},{7,3},{8,12},{9,13},{10,... | collective-permute-start | bytes 983048 | tf_op jit(solution)/shard_map/ppermute | solution.py:51
  129.1 17.9 %collective-permute-start.16 = (bf16[80,2048]{1,0:T(8,128)(2,1)S(1)}, bf16[80,2048]{1,0:T(8,128)(2,1)S(1)}, u32[]{:S(2)}, u32[]{:S(2)}) collective-permute-start(bf16[80,2048]{1,0:T(8,128)(2,1)S(1)} %collective-permute-done.14.refs_4_), channel_id=1, source_target_pairs={{0,2},{1,3},{2,0},{3,1},{4,6},{5,7},{6,4},{7,5},{8,10},{9,11},{10,... | collective-permute-start | bytes 983048 | tf_op jit(solution)/shard_map/ppermute | solution.py:51
  131.4 15.5 %collective-permute-start.15 = (bf16[80,2048]{1,0:T(8,128)(2,1)S(1)}, bf16[80,2048]{1,0:T(8,128)(2,1)S(1)}, u32[]{:S(2)}, u32[]{:S(2)}) collective-permute-start(bf16[80,2048]{1,0:T(8,128)(2,1)S(1)} %collective-permute-done.11.refs_1_), channel_id=1, source_target_pairs={{0,4},{1,5},{2,6},{3,7},{4,0},{5,1},{6,2},{7,3},{8,12},{9,13},{10,... | collective-permute-start | bytes 983048 | tf_op jit(solution)/shard_map/ppermute | solution.py:51
  140.6 3.3 %copy-start.3 = (bf16[640,512]{1,0:T(8,128)(2,1)}, bf16[640,512]{1,0:T(8,128)(2,1)S(1)}, u32[]{:S(2)}) copy-start(bf16[640,512]{1,0:T(8,128)(2,1)S(1)} %broadcast_select_fusion.refs_3_.refs_7_) | copy-start | bytes 1966084
  146.9 18.0 %copy-start.5 = (f32[256,128]{1,0:T(8,128)S(1)}, f32[256,128]{1,0:T(8,128)}, u32[]{:S(2)}) copy-start(f32[256,128]{1,0:T(8,128)} %pad_maximum_fusion.7.refs_5_) | copy-start | bytes 393220
  151.2 13.8 %collective-permute-start.39 = (f32[448,128]{1,0:T(8,128)S(1)}, f32[448,128]{1,0:T(8,128)S(1)}, u32[]{:S(2)}, u32[]{:S(2)}) collective-permute-start(f32[448,128]{1,0:T(8,128)S(1)} %get-tuple-element.45.refs_1_), channel_id=1, source_target_pairs={{0,1},{1,0},{2,3},{3,2},{4,5},{5,4},{6,7},{7,6},{8,9},{9,8},{10,11... | collective-permute-start | bytes 688136 | tf_op jit(solution)/shard_map/ppermute | solution.py:51
  169.6 1.6 collective-permute-start.40
  171.2 9.6 %copy-start.6 = (f32[256,128]{1,0:T(8,128)S(1)}, f32[256,128]{1,0:T(8,128)}, u32[]{:S(2)}) copy-start(f32[256,128]{1,0:T(8,128)} %pad_maximum_fusion.7.refs_5_) | copy-start | bytes 393220
  178.6 1.6 collective-permute-start.41
  180.2 0.7 copy-start.14
  180.2 8.4 %copy-start.1 = (bf16[128,7680]{1,0:T(8,128)(2,1)S(1)}, bf16[128,7680]{1,0:T(8,128)(2,1)}, u32[]{:S(2)}) copy-start(bf16[128,7680]{1,0:T(8,128)(2,1)} %param.17) | copy-start | bytes 5898244
  186.4 1.5 collective-permute-start.42

commit v4 on v3

--- a/solution.py
+++ b/solution.py
@@ -149,135 +149,104 @@
     return gather_any(unit, device)[2][0]
 
 
-def absorb_body(spots, step, has_sum, last, places_ref, hidden_ref, *refs):
+def absorb_body(spots, step, has_sum, rest_count, places_ref, hidden_ref, *refs):
     count = len(spots)
     piece_refs, refs = refs[:count], refs[count:]
     if has_sum:
         raw_in_ref, past_in_ref, *refs = refs
-    if last:
-        rest_ref, past_rest_ref, *refs = refs
+    rest_refs, refs = refs[:rest_count], refs[rest_count:]
     plane_out_ref, raw_ref, past_ref, *refs = refs
-    if last:
-        sum_ref, *refs = refs
-    plane_ref, sems, out_sem = refs
+    if rest_count:
+        sum_ref, plane_ref, sems, out_sem, rest_ref, rest_sems = refs
+    else:
+        plane_ref, sems, out_sem = refs
     place = places_ref[places_ref.shape[0] - 2]
     copies = []
     for i, (other, start, size) in enumerate(spots):
         target = plane_ref.at[jnp.bitwise_xor(place, other), pl.ds(start, size), :]
         copies.append(pltpu.make_async_copy(piece_refs[i], target, sems.at[i]))
-    for copy in copies:
+    rest_copies = [
+        pltpu.make_async_copy(ref, rest_ref.at[i], rest_sems.at[i])
+        for i, ref in enumerate(rest_refs)
+    ]
+    for copy in copies + rest_copies:
         copy.start()
+    rows = raw_ref.shape[0]
+
+    def multiply(index, weights):
+        split = weights.shape[1] // 2
+        hidden = hidden_ref[places_ref[index]]
+        query = jnp.dot(hidden[:rows], weights[:, :split], preferred_element_type=jnp.float32)
+        keys = jnp.dot(hidden, weights[:, split:], preferred_element_type=jnp.float32)
+        return query, keys[:rows], keys[rows:]
+
     for copy in copies:
         copy.wait()
     out = pltpu.make_async_copy(plane_ref, plane_out_ref, out_sem)
     out.start()
-    weights = plane_ref[...].reshape(-1, plane_ref.shape[2])
-    hidden = hidden_ref[places_ref[step]]
-    split = weights.shape[1] // 2
-    rows = raw_ref.shape[0]
-    raw = jnp.dot(hidden[:rows], weights, preferred_element_type=jnp.float32)
-    past = jnp.dot(hidden[rows:], weights[:, split:], preferred_element_type=jnp.float32)
+    main = multiply(step, plane_ref[...].reshape(-1, plane_ref.shape[2]))
+    split = main[0].shape[1]
     if has_sum:
-        raw = raw + raw_in_ref[...]
-        past = past + past_in_ref[...]
-    if not last:
-        raw_ref[...] = raw
-        past_ref[...] = past
+        before = raw_in_ref[:, :split], raw_in_ref[:, split:], past_in_ref[...]
+        main = [part + other for part, other in zip(main, before)]
+    if rest_count:
+        rest = None
+        for i, copy in enumerate(rest_copies):
+            copy.wait()
+            parts = multiply(i, rest_ref[i])
+            rest = parts if rest is None else [x + y for x, y in zip(rest, parts)]
+        more = rest[0].shape[1]
     else:
-        rest, past_rest = rest_ref[...], past_rest_ref[...]
-        more = past_rest.shape[1]
-        half = split + more
-        at = 0
-        for target, start, main, other in (
-            (raw_ref, 0, raw[:, :split], rest[:, :more]),
-            (raw_ref, half, raw[:, split:], rest[:, more:]),
-            (past_ref, 0, past, past_rest),
-        ):
-            target[:, start : start + split] = main
-            target[:, start + split : start + half] = other
-            count = main.shape[0]
-            total = jnp.sum(main * main, -1, keepdims=True)
+        rest, more = [None] * 3, 0
+    at = 0
+    targets = (raw_ref, 0), (raw_ref, split + more), (past_ref, 0)
+    for (target, start), part, other in zip(targets, main, rest):
+        target[:, start : start + split] = part
+        if rest_count:
+            target[:, start + split : start + split + more] = other
+            total = jnp.sum(part * part, -1, keepdims=True)
             total = total + jnp.sum(other * other, -1, keepdims=True)
-            sum_ref[at : at + count] = jnp.broadcast_to(total, (count, HEAD_DIM))
-            at += count
+            size = total.shape[0]
+            sum_ref[at : at + size] = jnp.broadcast_to(total, (size, HEAD_DIM))
+            at += size
     out.wait()
 
 
 def absorb(step, places, hidden, pieces, spots, chips, rows, sums, rests):
-    last = bool(rests)
     hbm = pl.BlockSpec(memory_space=pltpu.HBM)
     vmem = pl.BlockSpec(memory_space=pltpu.VMEM)
     width = pieces[0].shape[1]
+    more = rests[0].shape[1] if rests else 0
     chip_rows = hidden.shape[2] // chips
     past_rows = hidden.shape[1] - rows
-    more = rests[1].shape[1] if last else 0
     operands = [places, hidden, *pieces, *sums, *rests]
     specs = [pl.BlockSpec(memory_space=pltpu.SMEM), vmem] + [hbm] * len(pieces)
-    specs += [vmem] * (len(sums) + len(rests))
+    specs += [vmem] * len(sums) + [hbm] * len(rests)
     shapes = [
         pltpu.HBM((chips, chip_rows, width), jnp.bfloat16),
-        jax.ShapeDtypeStruct((rows, width + 2 * more), jnp.float32),
-        jax.ShapeDtypeStruct((past_rows, width // 2 + more), jnp.float32),
+        jax.ShapeDtypeStruct((rows, width + more), jnp.float32),
+        jax.ShapeDtypeStruct((past_rows, (width + more) // 2), jnp.float32),
     ]
     outs = [hbm, vmem, vmem]
-    if last:
+    scratch = [
+        pltpu.VMEM((chips, chip_rows, width), jnp.bfloat16),
+        pltpu.SemaphoreType.DMA((len(pieces),)),
+        pltpu.SemaphoreType.DMA,
+    ]
+    if rests:
         shapes.append(jax.ShapeDtypeStruct((2 * rows + past_rows, HEAD_DIM), jnp.float32))
         outs.append(vmem)
+        scratch.append(pltpu.VMEM((len(rests),) + rests[0].shape, jnp.bfloat16))
+        scratch.append(pltpu.SemaphoreType.DMA((len(rests),)))
     return pl.pallas_call(
-        functools.partial(absorb_body, spots, step, bool(sums), last),
+        functools.partial(absorb_body, spots, step, bool(sums), len(rests)),
         in_specs=specs,
         out_specs=outs,
         out_shape=shapes,
-        scratch_shapes=[
-            pltpu.VMEM((chips, chip_rows, width), jnp.bfloat16),
-            pltpu.SemaphoreType.DMA((len(pieces),)),
-            pltpu.SemaphoreType.DMA,
-        ],
+        scratch_shapes=scratch,
         compiler_params=pltpu.CompilerParams(vmem_limit_bytes=16 << 20),
         name="absorb",
     )(*operands)
-
-
-def absorb_rest_body(places_ref, hidden_ref, *refs):
-    count = len(refs) - 4
-    plane_refs = refs[:count]
-    raw_ref, past_ref, weight_ref, sems = refs[count:]
-    copies = [
-        pltpu.make_async_copy(ref, weight_ref.at[i], sems.at[i]) for i, ref in enumerate(plane_refs)
-    ]
-    for copy in copies:
-        copy.start()
-    rows, split = raw_ref.shape[0], past_ref.shape[1]
-    raw = past = None
-    for i, copy in enumerate(copies):
-        copy.wait()
-        hidden, weights = hidden_ref[places_ref[i]], weight_ref[i]
-        part = jnp.dot(hidden[:rows], weights, preferred_element_type=jnp.float32)
-        raw = part if raw is None else raw + part
-        part = jnp.dot(hidden[rows:], weights[:, split:], preferred_element_type=jnp.float32)
-        past = part if past is None else past + part
-    raw_ref[...] = raw
-    past_ref[...] = past
-
-
-def absorb_rest(places, hidden, planes, rows):
-    hbm = pl.BlockSpec(memory_space=pltpu.HBM)
-    vmem = pl.BlockSpec(memory_space=pltpu.VMEM)
-    count, width = len(planes), planes[0].shape[1]
-    return pl.pallas_call(
-        absorb_rest_body,
-        in_specs=[pl.BlockSpec(memory_space=pltpu.SMEM), vmem] + [hbm] * count,
-        out_shape=[
-            jax.ShapeDtypeStruct((rows, width), jnp.float32),
-            jax.ShapeDtypeStruct((hidden.shape[1] - rows, width // 2), jnp.float32),
-        ],
-        scratch_shapes=[
-            pltpu.VMEM((count,) + planes[0].shape, jnp.bfloat16),
-            pltpu.SemaphoreType.DMA((count,)),
-        ],
-        compiler_params=pltpu.CompilerParams(vmem_limit_bytes=12 << 20),
-        name="absorb_rest",
-    )(places, hidden, *planes)
 
 
 def turn(values, cosine, sine):
@@ -526,10 +495,9 @@
     usable = usable.astype(jnp.float32)
 
     chips = 4 if len(pieces) == 4 else 1
-    more = absorb_rest(places, stack, rests, 2 * rows)
     sums, planes = [], []
     for step, parts in enumerate(pieces):
-        final = more if step + 1 == len(pieces) else []
+        final = rests if step + 1 == len(pieces) else []
         plane, *sums = absorb(step, places, stack, parts, spots[step], chips, 2 * rows, sums, final)
         planes.append(plane)
     raw, past_raw, sums = sums

time: 189 us -> 187 us (0.989)
  waiting for transfers between devices: 69.1 us -> 72.3 us
  starting transfers between devices: 59.7 us -> 56.6 us
  Pallas kernels: 34.5 us -> 31.9 us
    ppermute x43, waiting for transfers between devices: 69.1 us -> 72.3 us  [permute(): lax.ppermute(value, AXIS, [(s, t) for s, t in pairs if t is not None])]
    ppermute x43, starting transfers between devices: 59.7 us -> 56.6 us  [permute(): lax.ppermute(value, AXIS, [(s, t) for s, t in pairs if t is not None])]
    pallas_call x5 -> x4, Pallas kernels: 17 us -> 14.5 us  [absorb(): pl.pallas_call(functools.partial(absorb_body, spots, step, bool(sums), le...]
  transfers between devices with their start and end apart: 43 -> 43, of which waited for: 20 -> 22; matrix products, arithmetic and copies ran while one was open for 12% -> 12% of each run, Pallas kernels for 7% -> 5%
where the time goes in v4:
time: 187 us; the launch traced here: 186 us
  waiting for transfers between devices  72.3 us (39%)
  starting transfers between devices  56.6 us (30%)
  Pallas kernels  31.9 us (17%)
  other arithmetic  13.1 us (7%)
  local copies, waits for them, and re-layouts  11.1 us (6%)
    ppermute x43, waiting for transfers between devices, permute(): lax.ppermute(value, AXIS, [(s, t) for s, t in pairs if t is not None])  72.3 us
    ppermute x43, starting transfers between devices, permute(): lax.ppermute(value, AXIS, [(s, t) for s, t in pairs if t is not None])  56.6 us
    pallas_call x4, Pallas kernels, absorb(): pl.pallas_call(functools.partial(absorb_body, spots, step, bool(sums), le...  14.5 us
    pallas_call x2, Pallas kernels, attend(): pl.pallas_call(functools.partial(attend_body, first, inner), out_shape=sh...  10.1 us
    pallas_call x1, Pallas kernels, project_latent(): pl.pallas_call(project_body, in_specs=[pl.BlockSpec(memory_space=pltpu.SM...  7.33 us
    add x4, local copies, waits for them, and re-layouts, modulate(): result = normed * (1.0 + scale[:, None, :]) + shift[:, None, :]  3.92 us
  transfers between devices with their start and end apart: 43, of which 22 were waited for; matrix products, arithmetic and copies ran while one was open for 12% of the time, Pallas kernels for 5%

profile of v4, /device:TPU:9, one launch (start us, length us, event | category | flops | bytes accessed | tf_op | source)
XLA Modules:
  0.0 186.1 jit_solution(1666034555355337419)
XLA Ops:
  0.0 3.3 %collective-permute-start.3 = (bf16[64,2560]{1,0:T(8,128)(2,1)}, bf16[64,2560]{1,0:T(8,128)(2,1)}, u32[]{:S(2)}, u32[]{:S(2)}) collective-permute-start(bf16[64,2560]{1,0:T(8,128)(2,1)} %param.11), channel_id=1, source_target_pairs={{0,2},{1,3},{2,4},{3,5},{4,6},{5,7},{6,8},{7,9},{8,10},{9,11},{10,... | collective-permute-start | bytes 983048 | tf_op jit(solution)/shard_map/ppermute | solution.py:51
  3.3 1.0 collective-permute-start.5
  4.3 0.9 constant_dynamic-slice_fusion.3
  5.3 1.2 constant_dynamic-slice_fusion.7
  6.5 0.7 pad_maximum_fusion.4
  8.4 1.2 collective-permute-start.30
  9.7 1.2 collective-permute-start.31
  11.3 4.0 %collective-permute-done.30 = bf16[160,512]{1,0:T(8,128)(2,1)S(1)} collective-permute-done((bf16[160,512]{1,0:T(8,128)(2,1)}, bf16[160,512]{1,0:T(8,128)(2,1)S(1)}, u32[]{:S(2)}, u32[]{:S(2)}) %collective-permute-start.30) | collective-permute-done | bytes 163872 | tf_op jit(solution)/shard_map/ppermute | solution.py:51
  15.3 2.2 %collective-permute-start.32 = (bf16[80,512]{1,0:T(8,128)(2,1)S(1)}, bf16[80,512]{1,0:T(8,128)(2,1)S(1)}, u32[]{:S(2)}, u32[]{:S(2)}) collective-permute-start(bf16[80,512]{1,0:T(8,128)(2,1)S(1)} %slice.119), channel_id=1, source_target_pairs={{0,4},{1,5},{2,6},{3,7},{4,0},{5,1},{6,2},{7,3},{8,12},{9,13},{10,... | collective-permute-start | bytes 245768 | tf_op jit(solution)/shard_map/ppermute | solution.py:51
  17.7 1.7 collective-permute-done.32
  19.4 1.5 collective-permute-done.33
  20.9 3.2 %collective-permute-start.36 = (bf16[640,512]{1,0:T(8,128)(2,1)S(1)}, bf16[640,512]{1,0:T(8,128)(2,1)}, u32[]{:S(2)}, u32[]{:S(2)}) collective-permute-start(bf16[640,512]{1,0:T(8,128)(2,1)S(1)} %bitcast.65), channel_id=1, source_target_pairs={{8,16},{9,17},{10,18},{11,19},{12,20},{13,21},{14,22},{15,23},{16,... | collective-permute-start | bytes 1966088 | tf_op jit(solution)/shard_map/ppermute | solution.py:51
  24.3 1.1 broadcast_select_fusion.5
  25.4 0.9 pad_maximum_fusion.2.refs_0_
  28.2 1.5 collective-permute-start.7
  29.7 1.0 broadcast_select_fusion.6
  30.9 0.8 pad_maximum_fusion.7.refs_5_
  31.8 3.0 %collective-permute-start.2 = (s32[1,4]{0,1:T(4,128)S(1)}, s32[1,4]{0,1:T(4,128)S(1)}, u32[]{:S(2)}, u32[]{:S(2)}) collective-permute-start(s32[1,4]{0,1:T(4,128)S(1)} %copy.40), channel_id=1, source_target_pairs={{0,1},{1,0},{2,3},{3,2},{4,5},{5,4},{6,7},{7,6},{8,9},{9,8},{10,11... | collective-permute-start | bytes 56 | tf_op jit(solution)/shard_map/ppermute | solution.py:51
  34.8 0.8 collective-permute-done.2
  37.3 1.6 mul.215
  38.9 1.2 add.249
  40.1 2.7 %add.250 = f32[128,4,640]{2,1,0:T(4,128)} reshape(f32[2,64,2560]{2,1,0:T(8,128)} %add.249) | data formatting | bytes 2621440 | tf_op jit(solution)/shard_map/add | solution.py:45
  43.1 1.1 broadcast_select_fusion.8
  44.6 2.1 %collective-permute-start.6 = (bf16[160,2048]{1,0:T(8,128)(2,1)}, bf16[160,2048]{1,0:T(8,128)(2,1)S(1)}, u32[]{:S(2)}, u32[]{:S(2)}) collective-permute-start(bf16[160,2048]{1,0:T(8,128)(2,1)} %pad_maximum_fusion.2.refs_0_), channel_id=1, source_target_pairs={{8,16},{9,17},{10,18},{11,19},{12,20},{13,21},{14,22},{15,23},{16,... | collective-permute-start | bytes 1966088 | tf_op jit(solution)/shard_map/ppermute | solution.py:51
  48.0 4.5 %collective-permute-done.7.refs_0_ = bf16[160,2048]{1,0:T(8,128)(2,1)} collective-permute-done((bf16[160,2048]{1,0:T(8,128)(2,1)}, bf16[160,2048]{1,0:T(8,128)(2,1)}, u32[]{:S(2)}, u32[]{:S(2)}) %collective-permute-start.7) | collective-permute-done | bytes 655392 | tf_op jit(solution)/shard_map/ppermute | solution.py:51
  52.5 2.1 %collective-permute-start.8 = (bf16[160,2048]{1,0:T(8,128)(2,1)}, bf16[160,2048]{1,0:T(8,128)(2,1)S(1)}, u32[]{:S(2)}, u32[]{:S(2)}) collective-permute-start(bf16[160,2048]{1,0:T(8,128)(2,1)} %collective-permute-done.7.refs_0_), channel_id=1, source_target_pairs={{8,16},{9,17},{10,18},{11,19},{12,20},{13,21},{14,22},{15,23},{16,... | collective-permute-start | bytes 1966088 | tf_op jit(solution)/shard_map/ppermute | solution.py:51
  54.6 8.2 %collective-permute-done.6 = bf16[160,2048]{1,0:T(8,128)(2,1)S(1)} collective-permute-done((bf16[160,2048]{1,0:T(8,128)(2,1)}, bf16[160,2048]{1,0:T(8,128)(2,1)S(1)}, u32[]{:S(2)}, u32[]{:S(2)}) %collective-permute-start.6) | collective-permute-done | bytes 655392 | tf_op jit(solution)/shard_map/ppermute | solution.py:51
  62.8 1.3 collective-permute-start.9
  64.6 1.2 collective-permute-start.22
  65.9 1.1 collective-permute-start.21
  67.0 9.8 %collective-permute-done.8 = bf16[160,2048]{1,0:T(8,128)(2,1)S(1)} collective-permute-done((bf16[160,2048]{1,0:T(8,128)(2,1)}, bf16[160,2048]{1,0:T(8,128)(2,1)S(1)}, u32[]{:S(2)}, u32[]{:S(2)}) %collective-permute-start.8) | collective-permute-done | bytes 655392 | tf_op jit(solution)/shard_map/ppermute | solution.py:51
  76.8 1.3 collective-permute-start.37
  78.2 2.1 %collective-permute-start.35 = (bf16[640,512]{1,0:T(8,128)(2,1)}, bf16[640,512]{1,0:T(8,128)(2,1)S(1)}, u32[]{:S(2)}, u32[]{:S(2)}) collective-permute-start(bf16[640,512]{1,0:T(8,128)(2,1)} %collective-permute-done.34.refs_10_.refs_5_), channel_id=1, source_target_pairs={{8,16},{9,17},{10,18},{11,19},{12,20},{13,21},{14,22},{15,23},{16,... | collective-permute-start | bytes 1966088 | tf_op jit(solution)/shard_map/ppermute | solution.py:51
  80.3 1.4 collective-permute-start.10
  81.9 1.0 slice.118
  83.3 9.9 %collective-permute-done.21.refs_1_ = bf16[160,2048]{1,0:T(8,128)(2,1)S(1)} collective-permute-done((bf16[160,2048]{1,0:T(8,128)(2,1)}, bf16[160,2048]{1,0:T(8,128)(2,1)S(1)}, u32[]{:S(2)}, u32[]{:S(2)}) %collective-permute-start.21) | collective-permute-done | bytes 655392 | tf_op jit(solution)/shard_map/ppermute | solution.py:51
  93.3 1.1 collective-permute-start.27
  95.9 9.8 %collective-permute-done.10 = bf16[160,2048]{1,0:T(8,128)(2,1)S(1)} collective-permute-done((bf16[160,2048]{1,0:T(8,128)(2,1)S(1)}, bf16[160,2048]{1,0:T(8,128)(2,1)S(1)}, u32[]{:S(2)}, u32[]{:S(2)}) %collective-permute-start.10) | collective-permute-done | bytes 655392 | tf_op jit(solution)/shard_map/ppermute | solution.py:51
  105.7 4.3 %collective-permute-start.38 = (bf16[640,512]{1,0:T(8,128)(2,1)S(1)}, bf16[640,512]{1,0:T(8,128)(2,1)S(1)}, u32[]{:S(2)}, u32[]{:S(2)}) collective-permute-start(bf16[640,512]{1,0:T(8,128)(2,1)S(1)} %broadcast_select_fusion.1.refs_11_.refs_6_), channel_id=1, source_target_pairs={{8,0},{9,1},{10,2},{11,3},{12,4},{13,5},{14,6},{15,7},{16,24},{17,... | collective-permute-start | bytes 1966088 | tf_op jit(solution)/shard_map/ppermute | solution.py:51
  110.1 1.9 %collective-permute-done.18.refs_2_ = bf16[160,2048]{1,0:T(8,128)(2,1)S(1)} collective-permute-done((bf16[160,2048]{1,0:T(8,128)(2,1)S(1)}, bf16[160,2048]{1,0:T(8,128)(2,1)S(1)}, u32[]{:S(2)}, u32[]{:S(2)}) %collective-permute-start.18) | collective-permute-done | bytes 655392 | tf_op jit(solution)/shard_map/ppermute | solution.py:51
  112.4 1.3 collective-permute-start.23
  113.7 1.1 collective-permute-start.20
  114.8 4.9 %collective-permute-done.24.refs_4_ = bf16[80,2048]{1,0:T(8,128)(2,1)S(1)} collective-permute-done((bf16[80,2048]{1,0:T(8,128)(2,1)S(1)}, bf16[80,2048]{1,0:T(8,128)(2,1)S(1)}, u32[]{:S(2)}, u32[]{:S(2)}) %collective-permute-start.24) | collective-permute-done | bytes 327712 | tf_op jit(solution)/shard_map/ppermute | solution.py:51
  119.7 1.1 collective-permute-start.14
  122.3 1.2 collective-permute-start.12
  124.4 1.2 collective-permute-start.19
  125.7 3.4 %collective-permute-done.14.refs_4_ = bf16[80,2048]{1,0:T(8,128)(2,1)S(1)} collective-permute-done((bf16[80,2048]{1,0:T(8,128)(2,1)S(1)}, bf16[80,2048]{1,0:T(8,128)(2,1)S(1)}, u32[]{:S(2)}, u32[]{:S(2)}) %collective-permute-start.14) | collective-permute-done | bytes 327712 | tf_op jit(solution)/shard_map/ppermute | solution.py:51
  129.1 2.4 %collective-permute-done.11.refs_1_ = bf16[80,2048]{1,0:T(8,128)(2,1)S(1)} collective-permute-done((bf16[80,2048]{1,0:T(8,128)(2,1)S(1)}, bf16[80,2048]{1,0:T(8,128)(2,1)S(1)}, u32[]{:S(2)}, u32[]{:S(2)}) %collective-permute-start.11) | collective-permute-done | bytes 327712 | tf_op jit(solution)/shard_map/ppermute | solution.py:51
  131.4 1.2 collective-permute-start.15
  132.8 3.4 %absorb.4 = (bf16[4,160,2048]{2,1,0:T(8,128)(2,1)}, f32[128,2048]{1,0:T(8,128)S(1)}, f32[192,1024]{1,0:T(8,128)S(1)}) custom-call(s32[6]{0:T(128)S(1)} %stack.27.places_ref, bf16[4,320,640]{2,1,0:T(8,128)(2,1)S(1)} %maximum_bitcast_fusion.hidden_ref, bf16[160,2048]{1,0:T(8,128)(2,1)} %pad_maximum_fusion.2.refs_0_, ...), custom_call_target="tpu_custom_call" | custom-call | tf_op jit(solution)/shard_map/absorb/pallas_call | solution.py:241
  136.2 3.2 %absorb.5 = (bf16[4,160,2048]{2,1,0:T(8,128)(2,1)}, f32[128,2048]{1,0:T(8,128)S(1)}, f32[192,1024]{1,0:T(8,128)S(1)}) custom-call(s32[6]{0:T(128)S(1)} %stack.27.places_ref, bf16[4,320,640]{2,1,0:T(8,128)(2,1)S(1)} %maximum_bitcast_fusion.hidden_ref, bf16[160,2048]{1,0:T(8,128)(2,1)} %collective-permute-done.7.refs_0_, ...), custom_call_target="tpu_custom_call" | custom-call | tf_op jit(solution)/shard_map/absorb/pallas_call | solution.py:241
  139.4 1.2 broadcast_select_fusion.refs_12_.refs_7_
  140.6 3.0 %absorb.6 = (bf16[4,160,2048]{2,1,0:T(8,128)(2,1)}, f32[128,2048]{1,0:T(8,128)S(1)}, f32[192,1024]{1,0:T(8,128)S(1)}) custom-call(s32[6]{0:T(128)S(1)} %stack.27.places_ref, bf16[4,320,640]{2,1,0:T(8,128)(2,1)S(1)} %maximum_bitcast_fusion.hidden_ref, bf16[160,2048]{1,0:T(8,128)(2,1)S(1)} %broadcast_select_fusion.3.refs_0_, ...), custom_call_target="tpu_custom_call" | custom-call | tf_op jit(solution)/shard_map/absorb/pallas_call | solution.py:241
  143.6 1.9 %collective-permute-done.16.refs_6_ = bf16[80,2048]{1,0:T(8,128)(2,1)S(1)} collective-permute-done((bf16[80,2048]{1,0:T(8,128)(2,1)S(1)}, bf16[80,2048]{1,0:T(8,128)(2,1)S(1)}, u32[]{:S(2)}, u32[]{:S(2)}) %collective-permute-start.16) | collective-permute-done | bytes 327712 | tf_op jit(solution)/shard_map/ppermute | solution.py:51
  145.5 1.3 collective-permute-done.15.refs_5_
  146.8 4.9 %absorb.7 = (bf16[4,160,2048]{2,1,0:T(8,128)(2,1)}, f32[128,2560]{1,0:T(8,128)S(1)}, f32[192,1280]{1,0:T(8,128)S(1)}, f32[448,128]{1,0:T(8,128)S(1)}) custom-call(s32[6]{0:T(128)S(1)} %stack.27.places_ref, bf16[4,320,640]{2,1,0:T(8,128)(2,1)S(1)} %maximum_bitcast_fusion.hidden_ref, bf16[160,2048]{1,0:T(8,128)(2,1)S(1)} %broadcast_select_fusion.2.refs_0_, ...), custom_call_target="tpu_custom_call" | custom-call | tf_op jit(solution)/shard_map/absorb/pallas_call | solution.py:241
  151.7 9.6 %collective-permute-start.39 = (f32[448,128]{1,0:T(8,128)S(1)}, f32[448,128]{1,0:T(8,128)S(1)}, u32[]{:S(2)}, u32[]{:S(2)}) collective-permute-start(f32[448,128]{1,0:T(8,128)S(1)} %get-tuple-element.41.refs_1_), channel_id=1, source_target_pairs={{0,1},{1,0},{2,3},{3,2},{4,5},{5,4},{6,7},{7,6},{8,9},{9,8},{10,11... | collective-permute-start | bytes 688136 | tf_op jit(solution)/shard_map/ppermute | solution.py:51
  161.3 1.1 collective-permute-done.39.refs_2_
  162.4 4.7 %attend.2 = (bf16[128,1280]{1,0:T(8,128)(2,1)S(1)}, bf16[192,1280]{1,0:T(8,128)(2,1)}) custom-call(f32[128,2560]{1,0:T(8,128)S(1)} %get-tuple-element.40.refs_0_, f32[448,128]{1,0:T(8,128)S(1)} %get-tuple-element.41.refs_1_, f32[448,128]{1,0:T(8,128)S(1)} %collective-permute-done.39.refs_2_, f32[1,1280]{1,0:T(1,128)S(1)} %broadcast_in_dim.19.refs_3_, ...), custom_call_target="tpu_custom_call" | custom-call | tf_op jit(solution)/shard_map/attend/pallas_call | solution.py:313
  167.4 1.3 collective-permute-done.40.other_ref
  168.7 7.3 %project.1 = (f32[128,2560]{1,0:T(8,128)}, f32[256,128]{1,0:T(8,128)}, bf16[128,1280]{1,0:T(8,128)(2,1)}) custom-call(s32[6]{0:T(128)S(1)} %stack.27.places_ref, bf16[128,1280]{1,0:T(8,128)(2,1)S(1)} %get-tuple-element.44.own_ref.refs_10_, bf16[128,1280]{1,0:T(8,128)(2,1)S(1)} %collective-permute-done.40.other_ref, f32[5,7680]{1,0:T(8,128)S(1)} %fusion.14.mod_ref, ...), custom_call_target="tpu_custom_call" | custom-call | tf_op jit(solution)/shard_map/project/pallas_call | solution.py:391
  176.5 1.1 collective-permute-done.41.refs_2_
  178.3 5.5 %attend.3 = bf16[128,1280]{1,0:T(8,128)(2,1)S(1)} custom-call(f32[128,2560]{1,0:T(8,128)} %get-tuple-element.49.refs_0_, f32[256,128]{1,0:T(8,128)} %get-tuple-element.50.refs_1_, f32[256,128]{1,0:T(8,128)} %copy-done.14, f32[1,1280]{1,0:T(1,128)S(1)} %broadcast_in_dim.19.refs_3_, f32[1,1280]{1,0:T(1,128)S(1)} %broadcast_in_dim.20.refs_4_, ...), custom_call_target="tpu_custom_call" | custom-call | tf_op jit(solution)/shard_map/attend/pallas_call | solution.py:313
  184.2 1.0 collective-permute-done.42
  (158 shorter events, 16.1 us)
Async XLA Ops:
  0.0 36.4 %copy-start = (bf16[128,7680]{1,0:T(8,128)(2,1)S(1)}, bf16[128,7680]{1,0:T(8,128)(2,1)}, u32[]{:S(2)}) copy-start(bf16[128,7680]{1,0:T(8,128)(2,1)} %param.17) | copy-start | bytes 5898244
  0.0 10.9 %copy-start.15 = (f32[2560]{0:T(1024)S(1)}, f32[2560]{0:T(1024)}, u32[]{:S(2)}) copy-start(f32[2560]{0:T(1024)} %param.18) | copy-start | bytes 30724
  0.0 11.0 %copy-start.16 = (f32[2560]{0:T(1024)S(1)}, f32[2560]{0:T(1024)}, u32[]{:S(2)}) copy-start(f32[2560]{0:T(1024)} %param.19) | copy-start | bytes 30724
  0.0 31.8 %collective-permute-start.3 = (bf16[64,2560]{1,0:T(8,128)(2,1)}, bf16[64,2560]{1,0:T(8,128)(2,1)}, u32[]{:S(2)}, u32[]{:S(2)}) collective-permute-start(bf16[64,2560]{1,0:T(8,128)(2,1)} %param.11), channel_id=1, source_target_pairs={{0,2},{1,3},{2,4},{3,5},{4,6},{5,7},{6,8},{7,9},{8,10},{9,11},{10,... | collective-permute-start | bytes 983048 | tf_op jit(solution)/shard_map/ppermute | solution.py:51
  3.3 24.9 %collective-permute-start.5 = (bf16[64,2560]{1,0:T(8,128)(2,1)}, bf16[64,2560]{1,0:T(8,128)(2,1)}, u32[]{:S(2)}, u32[]{:S(2)}) collective-permute-start(bf16[64,2560]{1,0:T(8,128)(2,1)} %param.11), channel_id=1, source_target_pairs={{0,1},{1,0},{2,3},{3,2},{4,5},{5,4},{6,7},{7,6},{8,9},{9,8},{10,11... | collective-permute-start | bytes 983048 | tf_op jit(solution)/shard_map/ppermute | solution.py:51
  5.2 2.6 %collective-permute-start.29 = (bf16[80,512]{1,0:T(8,128)(2,1)S(1)}, bf16[80,512]{1,0:T(8,128)(2,1)S(1)}, u32[]{:S(2)}, u32[]{:S(2)}) collective-permute-start(bf16[80,512]{1,0:T(8,128)(2,1)S(1)} %pad_maximum_fusion.10), channel_id=1, source_target_pairs={{0,1},{1,0},{2,3},{3,2},{4,5},{5,4},{6,7},{7,6},{8,9},{9,8},{10,11... | collective-permute-start | bytes 245768 | tf_op jit(solution)/shard_map/ppermute | solution.py:51
  7.2 17.0 %collective-permute-start = (bf16[80,2048]{1,0:T(8,128)(2,1)}, bf16[80,2048]{1,0:T(8,128)(2,1)}, u32[]{:S(2)}, u32[]{:S(2)}) collective-permute-start(bf16[80,2048]{1,0:T(8,128)(2,1)} %pad_maximum_fusion.4), channel_id=1, source_target_pairs={{0,1},{1,0},{2,3},{3,2},{4,5},{5,4},{6,7},{7,6},{8,9},{9,8},{10,11... | collective-permute-start | bytes 983048 | tf_op jit(solution)/shard_map/ppermute | solution.py:51
  8.4 6.9 %collective-permute-start.30 = (bf16[160,512]{1,0:T(8,128)(2,1)}, bf16[160,512]{1,0:T(8,128)(2,1)S(1)}, u32[]{:S(2)}, u32[]{:S(2)}) collective-permute-start(bf16[160,512]{1,0:T(8,128)(2,1)} %pad_maximum_fusion.6), channel_id=1, source_target_pairs={{0,2},{1,3},{2,0},{3,1},{4,6},{5,7},{6,4},{7,5},{8,10},{9,11},{10,... | collective-permute-start | bytes 491528 | tf_op jit(solution)/shard_map/ppermute | solution.py:51
  9.7 7.9 %collective-permute-start.31 = (bf16[160,512]{1,0:T(8,128)(2,1)}, bf16[160,512]{1,0:T(8,128)(2,1)S(1)}, u32[]{:S(2)}, u32[]{:S(2)}) collective-permute-start(bf16[160,512]{1,0:T(8,128)(2,1)} %pad_maximum_fusion.6), channel_id=1, source_target_pairs={{0,4},{1,5},{2,6},{3,7},{4,0},{5,1},{6,2},{7,3},{8,12},{9,13},{10,... | collective-permute-start | bytes 491528 | tf_op jit(solution)/shard_map/ppermute | solution.py:51
  11.3 15.0 %copy-start.7 = (s32[32]{0:T(128)S(1)}, s32[32]{0:T(128)}, u32[]{:S(2)}) copy-start(s32[32]{0:T(128)} %param.12) | copy-start | bytes 388
  15.3 4.0 %collective-permute-start.32 = (bf16[80,512]{1,0:T(8,128)(2,1)S(1)}, bf16[80,512]{1,0:T(8,128)(2,1)S(1)}, u32[]{:S(2)}, u32[]{:S(2)}) collective-permute-start(bf16[80,512]{1,0:T(8,128)(2,1)S(1)} %slice.119), channel_id=1, source_target_pairs={{0,4},{1,5},{2,6},{3,7},{4,0},{5,1},{6,2},{7,3},{8,12},{9,13},{10,... | collective-permute-start | bytes 245768 | tf_op jit(solution)/shard_map/ppermute | solution.py:51
  17.5 3.4 %collective-permute-start.33 = (bf16[80,512]{1,0:T(8,128)(2,1)S(1)}, bf16[80,512]{1,0:T(8,128)(2,1)S(1)}, u32[]{:S(2)}, u32[]{:S(2)}) collective-permute-start(bf16[80,512]{1,0:T(8,128)(2,1)S(1)} %slice.120), channel_id=1, source_target_pairs={{0,2},{1,3},{2,0},{3,1},{4,6},{5,7},{6,4},{7,5},{8,10},{9,11},{10,... | collective-permute-start | bytes 245768 | tf_op jit(solution)/shard_map/ppermute | solution.py:51
  20.9 125.8 %copy-start.4 = (bf16[4,160,512]{2,1,0:T(8,128)(2,1)}, bf16[4,160,512]{2,1,0:T(8,128)(2,1)S(1)}, u32[]{:S(2)}) copy-start(bf16[4,160,512]{2,1,0:T(8,128)(2,1)S(1)} %fusion.7) | copy-start | bytes 1966084
  20.9 43.4 %collective-permute-start.36 = (bf16[640,512]{1,0:T(8,128)(2,1)S(1)}, bf16[640,512]{1,0:T(8,128)(2,1)}, u32[]{:S(2)}, u32[]{:S(2)}) collective-permute-start(bf16[640,512]{1,0:T(8,128)(2,1)S(1)} %bitcast.65), channel_id=1, source_target_pairs={{8,16},{9,17},{10,18},{11,19},{12,20},{13,21},{14,22},{15,23},{16,... | collective-permute-start | bytes 1966088 | tf_op jit(solution)/shard_map/ppermute | solution.py:51
  24.1 40.5 %collective-permute-start.34 = (bf16[640,512]{1,0:T(8,128)(2,1)S(1)}, bf16[640,512]{1,0:T(8,128)(2,1)}, u32[]{:S(2)}, u32[]{:S(2)}) collective-permute-start(bf16[640,512]{1,0:T(8,128)(2,1)S(1)} %bitcast.66), channel_id=1, source_target_pairs={{0,8},{1,9},{2,10},{3,11},{4,12},{5,13},{6,14},{7,15},{8,0},{9,1},... | collective-permute-start | bytes 1966088 | tf_op jit(solution)/shard_map/ppermute | solution.py:51
  24.2 6.5 %copy-start.17 = (s32[1,2]{1,0:T(1,128)S(1)}, s32[1,2]{1,0:T(1,128)}, u32[]{:S(2)}) copy-start(s32[1,2]{1,0:T(1,128)} %param.13) | copy-start | bytes 28
  24.2 6.5 %copy-start.18 = (s32[1,2]{1,0:T(1,128)S(1)}, s32[1,2]{1,0:T(1,128)}, u32[]{:S(2)}) copy-start(s32[1,2]{1,0:T(1,128)} %param.14) | copy-start | bytes 28
  27.3 38.6 %collective-permute-start.26 = (bf16[160,2048]{1,0:T(8,128)(2,1)}, bf16[160,2048]{1,0:T(8,128)(2,1)}, u32[]{:S(2)}, u32[]{:S(2)}) collective-permute-start(bf16[160,2048]{1,0:T(8,128)(2,1)} %pad_maximum_fusion.2.refs_0_), channel_id=1, source_target_pairs={{0,4},{1,5},{2,6},{3,7},{4,0},{5,1},{6,2},{7,3},{8,12},{9,13},{10,... | collective-permute-start | bytes 1966088 | tf_op jit(solution)/shard_map/ppermute | solution.py:51
  28.2 24.3 %collective-permute-start.7 = (bf16[160,2048]{1,0:T(8,128)(2,1)}, bf16[160,2048]{1,0:T(8,128)(2,1)}, u32[]{:S(2)}, u32[]{:S(2)}) collective-permute-start(bf16[160,2048]{1,0:T(8,128)(2,1)} %pad_maximum_fusion.2.refs_0_), channel_id=1, source_target_pairs={{0,8},{1,9},{2,10},{3,11},{4,12},{5,13},{6,14},{7,15},{8,0},{9,1},... | collective-permute-start | bytes 1966088 | tf_op jit(solution)/shard_map/ppermute | solution.py:51
  31.8 3.8 %collective-permute-start.2 = (s32[1,4]{0,1:T(4,128)S(1)}, s32[1,4]{0,1:T(4,128)S(1)}, u32[]{:S(2)}, u32[]{:S(2)}) collective-permute-start(s32[1,4]{0,1:T(4,128)S(1)} %copy.40), channel_id=1, source_target_pairs={{0,1},{1,0},{2,3},{3,2},{4,5},{5,4},{6,7},{7,6},{8,9},{9,8},{10,11... | collective-permute-start | bytes 56 | tf_op jit(solution)/shard_map/ppermute | solution.py:51
  35.7 7.2 %collective-permute-start.4 = (bf16[64,2560]{1,0:T(8,128)(2,1)}, bf16[64,2560]{1,0:T(8,128)(2,1)}, u32[]{:S(2)}, u32[]{:S(2)}) collective-permute-start(bf16[64,2560]{1,0:T(8,128)(2,1)} %collective-permute-done.3), channel_id=1, source_target_pairs={{0,1},{1,0},{2,3},{3,2},{4,5},{5,4},{6,7},{7,6},{8,9},{9,8},{10,11... | collective-permute-start | bytes 983048 | tf_op jit(solution)/shard_map/ppermute | solution.py:51
  37.3 2.8 %copy-start.8 = (f32[2,64,2560]{2,1,0:T(8,128)}, f32[2,64,2560]{2,1,0:T(8,128)S(1)}, u32[]{:S(2)}) copy-start(f32[2,64,2560]{2,1,0:T(8,128)S(1)} %mul.214) | copy-start | bytes 3932164
  38.9 4.0 %copy-start.13 = (bf16[64,2560]{1,0:T(8,128)(2,1)S(1)}, bf16[64,2560]{1,0:T(8,128)(2,1)}, u32[]{:S(2)}) copy-start(bf16[64,2560]{1,0:T(8,128)(2,1)} %param.10) | copy-start | bytes 983044
  42.9 1.7 collective-permute-start.1
  44.6 18.2 %collective-permute-start.6 = (bf16[160,2048]{1,0:T(8,128)(2,1)}, bf16[160,2048]{1,0:T(8,128)(2,1)S(1)}, u32[]{:S(2)}, u32[]{:S(2)}) collective-permute-start(bf16[160,2048]{1,0:T(8,128)(2,1)} %pad_maximum_fusion.2.refs_0_), channel_id=1, source_target_pairs={{8,16},{9,17},{10,18},{11,19},{12,20},{13,21},{14,22},{15,23},{16,... | collective-permute-start | bytes 1966088 | tf_op jit(solution)/shard_map/ppermute | solution.py:51
  48.0 33.7 %copy-start.9 = (f32[2,64,2560]{2,1,0:T(8,128)S(1)}, f32[2,64,2560]{2,1,0:T(8,128)}, u32[]{:S(2)}) copy-start(f32[2,64,2560]{2,1,0:T(8,128)} %copy-done.8) | copy-start | bytes 3932164
  48.0 33.8 %copy-start.10 = (f32[2,64,2560]{2,1,0:T(8,128)S(1)}, f32[2,64,2560]{2,1,0:T(8,128)}, u32[]{:S(2)}) copy-start(f32[2,64,2560]{2,1,0:T(8,128)} %add.249) | copy-start | bytes 3932164
  52.5 24.3 %collective-permute-start.8 = (bf16[160,2048]{1,0:T(8,128)(2,1)}, bf16[160,2048]{1,0:T(8,128)(2,1)S(1)}, u32[]{:S(2)}, u32[]{:S(2)}) collective-permute-start(bf16[160,2048]{1,0:T(8,128)(2,1)} %collective-permute-done.7.refs_0_), channel_id=1, source_target_pairs={{8,16},{9,17},{10,18},{11,19},{12,20},{13,21},{14,22},{15,23},{16,... | collective-permute-start | bytes 1966088 | tf_op jit(solution)/shard_map/ppermute | solution.py:51
  62.8 15.4 %collective-permute-start.9 = (bf16[160,2048]{1,0:T(8,128)(2,1)S(1)}, bf16[160,2048]{1,0:T(8,128)(2,1)S(1)}, u32[]{:S(2)}, u32[]{:S(2)}) collective-permute-start(bf16[160,2048]{1,0:T(8,128)(2,1)S(1)} %collective-permute-done.6), channel_id=1, source_target_pairs={{8,0},{9,1},{10,2},{11,3},{12,4},{13,5},{14,6},{15,7},{16,24},{17,... | collective-permute-start | bytes 1966088 | tf_op jit(solution)/shard_map/ppermute | solution.py:51
  64.3 16.0 %collective-permute-start.25 = (bf16[160,2048]{1,0:T(8,128)(2,1)}, bf16[160,2048]{1,0:T(8,128)(2,1)S(1)}, u32[]{:S(2)}, u32[]{:S(2)}) collective-permute-start(bf16[160,2048]{1,0:T(8,128)(2,1)} %pad_maximum_fusion.2.refs_0_), channel_id=1, source_target_pairs={{0,2},{1,3},{2,0},{3,1},{4,6},{5,7},{6,4},{7,5},{8,10},{9,11},{10,... | collective-permute-start | bytes 1966088 | tf_op jit(solution)/shard_map/ppermute | solution.py:51
  64.6 18.3 %collective-permute-start.22 = (bf16[160,2048]{1,0:T(8,128)(2,1)}, bf16[160,2048]{1,0:T(8,128)(2,1)S(1)}, u32[]{:S(2)}, u32[]{:S(2)}) collective-permute-start(bf16[160,2048]{1,0:T(8,128)(2,1)} %collective-permute-done.7.refs_0_), channel_id=1, source_target_pairs={{0,4},{1,5},{2,6},{3,7},{4,0},{5,1},{6,2},{7,3},{8,12},{9,13},{10,... | collective-permute-start | bytes 1966088 | tf_op jit(solution)/shard_map/ppermute | solution.py:51
  65.9 27.4 %collective-permute-start.21 = (bf16[160,2048]{1,0:T(8,128)(2,1)}, bf16[160,2048]{1,0:T(8,128)(2,1)S(1)}, u32[]{:S(2)}, u32[]{:S(2)}) collective-permute-start(bf16[160,2048]{1,0:T(8,128)(2,1)} %collective-permute-done.7.refs_0_), channel_id=1, source_target_pairs={{0,2},{1,3},{2,0},{3,1},{4,6},{5,7},{6,4},{7,5},{8,10},{9,11},{10,... | collective-permute-start | bytes 1966088 | tf_op jit(solution)/shard_map/ppermute | solution.py:51
  76.8 17.6 %collective-permute-start.37 = (bf16[640,512]{1,0:T(8,128)(2,1)}, bf16[640,512]{1,0:T(8,128)(2,1)S(1)}, u32[]{:S(2)}, u32[]{:S(2)}) collective-permute-start(bf16[640,512]{1,0:T(8,128)(2,1)} %collective-permute-done.36), channel_id=1, source_target_pairs={{8,0},{9,1},{10,2},{11,3},{12,4},{13,5},{14,6},{15,7},{16,24},{17,... | collective-permute-start | bytes 1966088 | tf_op jit(solution)/shard_map/ppermute | solution.py:51
  78.2 17.4 %collective-permute-start.35 = (bf16[640,512]{1,0:T(8,128)(2,1)}, bf16[640,512]{1,0:T(8,128)(2,1)S(1)}, u32[]{:S(2)}, u32[]{:S(2)}) collective-permute-start(bf16[640,512]{1,0:T(8,128)(2,1)} %collective-permute-done.34.refs_10_.refs_5_), channel_id=1, source_target_pairs={{8,16},{9,17},{10,18},{11,19},{12,20},{13,21},{14,22},{15,23},{16,... | collective-permute-start | bytes 1966088 | tf_op jit(solution)/shard_map/ppermute | solution.py:51
  80.3 25.4 %collective-permute-start.10 = (bf16[160,2048]{1,0:T(8,128)(2,1)S(1)}, bf16[160,2048]{1,0:T(8,128)(2,1)S(1)}, u32[]{:S(2)}, u32[]{:S(2)}) collective-permute-start(bf16[160,2048]{1,0:T(8,128)(2,1)S(1)} %broadcast_select_fusion.3.refs_0_), channel_id=1, source_target_pairs={{8,0},{9,1},{10,2},{11,3},{12,4},{13,5},{14,6},{15,7},{16,24},{17,... | collective-permute-start | bytes 1966088 | tf_op jit(solution)/shard_map/ppermute | solution.py:51
  83.0 29.4 %collective-permute-start.28 = (bf16[80,2048]{1,0:T(8,128)(2,1)S(1)}, bf16[80,2048]{1,0:T(8,128)(2,1)S(1)}, u32[]{:S(2)}, u32[]{:S(2)}) collective-permute-start(bf16[80,2048]{1,0:T(8,128)(2,1)S(1)} %slice.118), channel_id=1, source_target_pairs={{0,2},{1,3},{2,0},{3,1},{4,6},{5,7},{6,4},{7,5},{8,10},{9,11},{10,... | collective-permute-start | bytes 983048 | tf_op jit(solution)/shard_map/ppermute | solution.py:51
  93.3 20.4 %collective-permute-start.27 = (bf16[80,2048]{1,0:T(8,128)(2,1)S(1)}, bf16[80,2048]{1,0:T(8,128)(2,1)S(1)}, u32[]{:S(2)}, u32[]{:S(2)}) collective-permute-start(bf16[80,2048]{1,0:T(8,128)(2,1)S(1)} %slice.117), channel_id=1, source_target_pairs={{0,4},{1,5},{2,6},{3,7},{4,0},{5,1},{6,2},{7,3},{8,12},{9,13},{10,... | collective-permute-start | bytes 983048 | tf_op jit(solution)/shard_map/ppermute | solution.py:51
  94.4 17.5 %collective-permute-start.18 = (bf16[160,2048]{1,0:T(8,128)(2,1)S(1)}, bf16[160,2048]{1,0:T(8,128)(2,1)S(1)}, u32[]{:S(2)}, u32[]{:S(2)}) collective-permute-start(bf16[160,2048]{1,0:T(8,128)(2,1)S(1)} %broadcast_select_fusion.3.refs_0_), channel_id=1, source_target_pairs={{0,4},{1,5},{2,6},{3,7},{4,0},{5,1},{6,2},{7,3},{8,12},{9,13},{10,... | collective-permute-start | bytes 1966088 | tf_op jit(solution)/shard_map/ppermute | solution.py:51
  95.5 25.3 %collective-permute-start.17 = (bf16[160,2048]{1,0:T(8,128)(2,1)S(1)}, bf16[160,2048]{1,0:T(8,128)(2,1)S(1)}, u32[]{:S(2)}, u32[]{:S(2)}) collective-permute-start(bf16[160,2048]{1,0:T(8,128)(2,1)S(1)} %broadcast_select_fusion.3.refs_0_), channel_id=1, source_target_pairs={{0,2},{1,3},{2,0},{3,1},{4,6},{5,7},{6,4},{7,5},{8,10},{9,11},{10,... | collective-permute-start | bytes 1966088 | tf_op jit(solution)/shard_map/ppermute | solution.py:51
  95.9 50.9 %copy-start.2 = (bf16[640,512]{1,0:T(8,128)(2,1)}, bf16[640,512]{1,0:T(8,128)(2,1)S(1)}, u32[]{:S(2)}) copy-start(bf16[640,512]{1,0:T(8,128)(2,1)S(1)} %broadcast_select_fusion.1.refs_11_.refs_6_) | copy-start | bytes 1966084
  105.7 17.8 %collective-permute-start.38 = (bf16[640,512]{1,0:T(8,128)(2,1)S(1)}, bf16[640,512]{1,0:T(8,128)(2,1)S(1)}, u32[]{:S(2)}, u32[]{:S(2)}) collective-permute-start(bf16[640,512]{1,0:T(8,128)(2,1)S(1)} %broadcast_select_fusion.1.refs_11_.refs_6_), channel_id=1, source_target_pairs={{8,0},{9,1},{10,2},{11,3},{12,4},{13,5},{14,6},{15,7},{16,24},{17,... | collective-permute-start | bytes 1966088 | tf_op jit(solution)/shard_map/ppermute | solution.py:51
  112.0 7.7 %collective-permute-start.24 = (bf16[80,2048]{1,0:T(8,128)(2,1)S(1)}, bf16[80,2048]{1,0:T(8,128)(2,1)S(1)}, u32[]{:S(2)}, u32[]{:S(2)}) collective-permute-start(bf16[80,2048]{1,0:T(8,128)(2,1)S(1)} %slice.116), channel_id=1, source_target_pairs={{0,2},{1,3},{2,0},{3,1},{4,6},{5,7},{6,4},{7,5},{8,10},{9,11},{10,... | collective-permute-start | bytes 983048 | tf_op jit(solution)/shard_map/ppermute | solution.py:51
  112.3 9.4 %copy-start.11 = (f32[128,4,640]{2,1,0:T(4,128)S(1)}, f32[128,4,640]{2,1,0:T(4,128)}, u32[]{:S(2)}) copy-start(f32[128,4,640]{2,1,0:T(4,128)} %mul.215) | copy-start | bytes 3932164
  112.3 9.4 %copy-start.12 = (f32[128,4,640]{2,1,0:T(4,128)S(1)}, f32[128,4,640]{2,1,0:T(4,128)}, u32[]{:S(2)}) copy-start(f32[128,4,640]{2,1,0:T(4,128)} %add.250) | copy-start | bytes 3932164
  112.4 9.9 %collective-permute-start.23 = (bf16[80,2048]{1,0:T(8,128)(2,1)S(1)}, bf16[80,2048]{1,0:T(8,128)(2,1)S(1)}, u32[]{:S(2)}, u32[]{:S(2)}) collective-permute-start(bf16[80,2048]{1,0:T(8,128)(2,1)S(1)} %slice.115), channel_id=1, source_target_pairs={{0,4},{1,5},{2,6},{3,7},{4,0},{5,1},{6,2},{7,3},{8,12},{9,13},{10,... | collective-permute-start | bytes 983048 | tf_op jit(solution)/shard_map/ppermute | solution.py:51
  113.7 10.8 %collective-permute-start.20 = (bf16[80,2048]{1,0:T(8,128)(2,1)S(1)}, bf16[80,2048]{1,0:T(8,128)(2,1)S(1)}, u32[]{:S(2)}, u32[]{:S(2)}) collective-permute-start(bf16[80,2048]{1,0:T(8,128)(2,1)S(1)} %slice.114), channel_id=1, source_target_pairs={{0,2},{1,3},{2,0},{3,1},{4,6},{5,7},{6,4},{7,5},{8,10},{9,11},{10,... | collective-permute-start | bytes 983048 | tf_op jit(solution)/shard_map/ppermute | solution.py:51
  119.7 9.4 %collective-permute-start.14 = (bf16[80,2048]{1,0:T(8,128)(2,1)S(1)}, bf16[80,2048]{1,0:T(8,128)(2,1)S(1)}, u32[]{:S(2)}, u32[]{:S(2)}) collective-permute-start(bf16[80,2048]{1,0:T(8,128)(2,1)S(1)} %get-tuple-element.63), channel_id=1, source_target_pairs={{0,4},{1,5},{2,6},{3,7},{4,0},{5,1},{6,2},{7,3},{8,12},{9,13},{10,... | collective-permute-start | bytes 983048 | tf_op jit(solution)/shard_map/ppermute | solution.py:51
  120.8 10.6 %collective-permute-start.11 = (bf16[80,2048]{1,0:T(8,128)(2,1)S(1)}, bf16[80,2048]{1,0:T(8,128)(2,1)S(1)}, u32[]{:S(2)}, u32[]{:S(2)}) collective-permute-start(bf16[80,2048]{1,0:T(8,128)(2,1)S(1)} %get-tuple-element.64), channel_id=1, source_target_pairs={{0,2},{1,3},{2,0},{3,1},{4,6},{5,7},{6,4},{7,5},{8,10},{9,11},{10,... | collective-permute-start | bytes 983048 | tf_op jit(solution)/shard_map/ppermute | solution.py:51
  122.3 21.3 %collective-permute-start.12 = (bf16[80,2048]{1,0:T(8,128)(2,1)S(1)}, bf16[80,2048]{1,0:T(8,128)(2,1)S(1)}, u32[]{:S(2)}, u32[]{:S(2)}) collective-permute-start(bf16[80,2048]{1,0:T(8,128)(2,1)S(1)} %get-tuple-element.63), channel_id=1, source_target_pairs={{0,2},{1,3},{2,0},{3,1},{4,6},{5,7},{6,4},{7,5},{8,10},{9,11},{10,... | collective-permute-start | bytes 983048 | tf_op jit(solution)/shard_map/ppermute | solution.py:51
  123.5 20.1 %collective-permute-start.13 = (bf16[80,2048]{1,0:T(8,128)(2,1)S(1)}, bf16[80,2048]{1,0:T(8,128)(2,1)S(1)}, u32[]{:S(2)}, u32[]{:S(2)}) collective-permute-start(bf16[80,2048]{1,0:T(8,128)(2,1)S(1)} %get-tuple-element.64), channel_id=1, source_target_pairs={{0,4},{1,5},{2,6},{3,7},{4,0},{5,1},{6,2},{7,3},{8,12},{9,13},{10,... | collective-permute-start | bytes 983048 | tf_op jit(solution)/shard_map/ppermute | solution.py:51
  124.4 16.2 %collective-permute-start.19 = (bf16[80,2048]{1,0:T(8,128)(2,1)S(1)}, bf16[80,2048]{1,0:T(8,128)(2,1)S(1)}, u32[]{:S(2)}, u32[]{:S(2)}) collective-permute-start(bf16[80,2048]{1,0:T(8,128)(2,1)S(1)} %slice.113), channel_id=1, source_target_pairs={{0,4},{1,5},{2,6},{3,7},{4,0},{5,1},{6,2},{7,3},{8,12},{9,13},{10,... | collective-permute-start | bytes 983048 | tf_op jit(solution)/shard_map/ppermute | solution.py:51
  129.1 16.4 %collective-permute-start.16 = (bf16[80,2048]{1,0:T(8,128)(2,1)S(1)}, bf16[80,2048]{1,0:T(8,128)(2,1)S(1)}, u32[]{:S(2)}, u32[]{:S(2)}) collective-permute-start(bf16[80,2048]{1,0:T(8,128)(2,1)S(1)} %collective-permute-done.14.refs_4_), channel_id=1, source_target_pairs={{0,2},{1,3},{2,0},{3,1},{4,6},{5,7},{6,4},{7,5},{8,10},{9,11},{10,... | collective-permute-start | bytes 983048 | tf_op jit(solution)/shard_map/ppermute | solution.py:51
  131.4 15.3 %collective-permute-start.15 = (bf16[80,2048]{1,0:T(8,128)(2,1)S(1)}, bf16[80,2048]{1,0:T(8,128)(2,1)S(1)}, u32[]{:S(2)}, u32[]{:S(2)}) collective-permute-start(bf16[80,2048]{1,0:T(8,128)(2,1)S(1)} %collective-permute-done.11.refs_1_), channel_id=1, source_target_pairs={{0,4},{1,5},{2,6},{3,7},{4,0},{5,1},{6,2},{7,3},{8,12},{9,13},{10,... | collective-permute-start | bytes 983048 | tf_op jit(solution)/shard_map/ppermute | solution.py:51
  140.6 6.2 %copy-start.3 = (bf16[640,512]{1,0:T(8,128)(2,1)}, bf16[640,512]{1,0:T(8,128)(2,1)S(1)}, u32[]{:S(2)}) copy-start(bf16[640,512]{1,0:T(8,128)(2,1)S(1)} %broadcast_select_fusion.refs_12_.refs_7_) | copy-start | bytes 1966084
  146.8 15.6 %copy-start.5 = (f32[256,128]{1,0:T(8,128)S(1)}, f32[256,128]{1,0:T(8,128)}, u32[]{:S(2)}) copy-start(f32[256,128]{1,0:T(8,128)} %pad_maximum_fusion.7.refs_5_) | copy-start | bytes 393220
  151.7 10.7 %collective-permute-start.39 = (f32[448,128]{1,0:T(8,128)S(1)}, f32[448,128]{1,0:T(8,128)S(1)}, u32[]{:S(2)}, u32[]{:S(2)}) collective-permute-start(f32[448,128]{1,0:T(8,128)S(1)} %get-tuple-element.41.refs_1_), channel_id=1, source_target_pairs={{0,1},{1,0},{2,3},{3,2},{4,5},{5,4},{6,7},{7,6},{8,9},{9,8},{10,11... | collective-permute-start | bytes 688136 | tf_op jit(solution)/shard_map/ppermute | solution.py:51
  167.0 1.6 collective-permute-start.40
  168.7 9.6 %copy-start.6 = (f32[256,128]{1,0:T(8,128)S(1)}, f32[256,128]{1,0:T(8,128)}, u32[]{:S(2)}) copy-start(f32[256,128]{1,0:T(8,128)} %pad_maximum_fusion.7.refs_5_) | copy-start | bytes 393220
  176.0 1.6 collective-permute-start.41
  177.6 0.7 copy-start.14
  177.6 8.4 %copy-start.1 = (bf16[128,7680]{1,0:T(8,128)(2,1)S(1)}, bf16[128,7680]{1,0:T(8,128)(2,1)}, u32[]{:S(2)}) copy-start(bf16[128,7680]{1,0:T(8,128)(2,1)} %param.17) | copy-start | bytes 5898244
  183.8 1.5 collective-permute-start.42

commit v5 on v4

--- a/solution.py
+++ b/solution.py
@@ -134,7 +134,7 @@
     two_end = z_outward(across)
     second = jnp.where(middle, two_mid, two_end)
     three_end = z_outward(second)
-    return [plane, pair, second, jnp.where(middle, across, three_end)]
+    return [plane, pair, second, across, three_end]
 
 
 def gather_any(unit, device):
@@ -147,6 +147,21 @@
 
 def gather_rest_any(unit, device):
     return gather_any(unit, device)[2][0]
+
+
+def begin_choice(middle, first, second, target, sem):
+    inner = pltpu.make_async_copy(first, target, sem)
+    outer = pltpu.make_async_copy(second, target, sem)
+
+    @pl.when(middle)
+    def _():
+        inner.start()
+
+    @pl.when(jnp.logical_not(middle))
+    def _():
+        outer.start()
+
+    return inner
 
 
 def absorb_body(spots, step, has_sum, rest_count, places_ref, hidden_ref, *refs):
@@ -165,12 +180,20 @@
     for i, (other, start, size) in enumerate(spots):
         target = plane_ref.at[jnp.bitwise_xor(place, other), pl.ds(start, size), :]
         copies.append(pltpu.make_async_copy(piece_refs[i], target, sems.at[i]))
+    planes = rest_ref.shape[0] if rest_count else 0
+    plain = planes - 1 if rest_count > planes else planes
     rest_copies = [
-        pltpu.make_async_copy(ref, rest_ref.at[i], rest_sems.at[i])
-        for i, ref in enumerate(rest_refs)
+        pltpu.make_async_copy(rest_refs[i], rest_ref.at[i], rest_sems.at[i]) for i in range(plain)
     ]
     for copy in copies + rest_copies:
         copy.start()
+    if plain < planes:
+        middle = (places_ref[0] == 1) | (places_ref[0] == 2)
+        rest_copies.append(
+            begin_choice(
+                middle, rest_refs[plain], rest_refs[planes], rest_ref.at[plain], rest_sems.at[plain]
+            )
+        )
     rows = raw_ref.shape[0]
 
     def multiply(index, weights):
@@ -236,8 +259,8 @@
     if rests:
         shapes.append(jax.ShapeDtypeStruct((2 * rows + past_rows, HEAD_DIM), jnp.float32))
         outs.append(vmem)
-        scratch.append(pltpu.VMEM((len(rests),) + rests[0].shape, jnp.bfloat16))
-        scratch.append(pltpu.SemaphoreType.DMA((len(rests),)))
+        scratch.append(pltpu.VMEM((hidden.shape[0],) + rests[0].shape, jnp.bfloat16))
+        scratch.append(pltpu.SemaphoreType.DMA((hidden.shape[0],)))
     return pl.pallas_call(
         functools.partial(absorb_body, spots, step, bool(sums), len(rests)),
         in_specs=specs,
@@ -319,17 +342,24 @@
 
 
 def project_body(places_ref, own_ref, other_ref, mod_ref, *refs):
-    count = (len(refs) - 7) // 2
-    raw_ref, sum_ref, value_ref, hidden_ref, main_ref, rest_ref, sems = refs[2 * count :]
-    targets = [main_ref.at[i] for i in range(count)] + [rest_ref.at[i] for i in range(count)]
+    raw_ref, sum_ref, value_ref, hidden_ref, main_ref, rest_ref, sems = refs[-7:]
+    count = main_ref.shape[0]
+    plain = count - 1 if len(refs) - 7 > 2 * count else count
     rows, half = own_ref.shape
     parts, _, part_width = hidden_ref.shape
-    copies = [
-        pltpu.make_async_copy(ref, target, sems.at[i])
-        for i, (ref, target) in enumerate(zip(refs, targets))
+    copies = [pltpu.make_async_copy(refs[i], main_ref.at[i], sems.at[i]) for i in range(count)]
+    copies += [
+        pltpu.make_async_copy(refs[count + i], rest_ref.at[i], sems.at[count + i])
+        for i in range(plain)
     ]
     for copy in copies:
         copy.start()
+    if plain < count:
+        middle = (places_ref[0] == 1) | (places_ref[0] == 2)
+        candidates = refs[count + plain], refs[count + plain + 1]
+        copies.append(
+            begin_choice(middle, *candidates, rest_ref.at[plain], sems.at[count + plain])
+        )
     is_low = places_ref[count + 1] == 0
     own, other = own_ref[...].astype(jnp.float32), other_ref[...].astype(jnp.float32)
     low, high = jnp.where(is_low, own, other), jnp.where(is_low, other, own)
@@ -390,7 +420,7 @@
     hbm = pl.BlockSpec(memory_space=pltpu.HBM)
     return pl.pallas_call(
         project_body,
-        in_specs=[pl.BlockSpec(memory_space=pltpu.SMEM)] + [vmem] * 3 + [hbm] * (2 * count),
+        in_specs=[pl.BlockSpec(memory_space=pltpu.SMEM)] + [vmem] * 3 + [hbm] * (count + len(rests)),
         out_shape=[
             pltpu.HBM((rows, 2 * half), jnp.float32),
             pltpu.HBM((2 * rows, HEAD_DIM), jnp.float32),
@@ -512,7 +542,9 @@
     )
     kept = lax.dynamic_slice_in_dim(latent, core * rows, rows, 0)
     sent = lax.dynamic_slice_in_dim(latent, (1 - core) * rows, rows, 0)
-    return in_order(kept, swap_core(sent), 1)
+    other = swap_core(sent)
+    joined = jnp.concatenate([kept, other, kept], axis=1)
+    return lax.dynamic_slice_in_dim(joined, core * half, width, 1)
 
 
 def solution(mesh):

time: 187 us -> 183 us (0.979)
  the two profiles are of different devices: /device:TPU:9 before, /device:TPU:0 now
where the time goes in v5:
time: 183 us; the launch traced here: 182 us
  waiting for transfers between devices  81.2 us (44%)
  starting transfers between devices  43 us (23%)
  Pallas kernels  31.7 us (17%)
  other arithmetic  12.9 us (7%)
  local copies, waits for them, and re-layouts  12 us (7%)
    ppermute x43, waiting for transfers between devices, permute(): lax.ppermute(value, AXIS, [(s, t) for s, t in pairs if t is not None])  81.2 us
    ppermute x43, starting transfers between devices, permute(): lax.ppermute(value, AXIS, [(s, t) for s, t in pairs if t is not None])  43 us
    pallas_call x4, Pallas kernels, absorb(): pl.pallas_call(functools.partial(absorb_body, spots, step, bool(sums), le...  14.2 us
    pallas_call x2, Pallas kernels, attend(): pl.pallas_call(functools.partial(attend_body, first, inner), out_shape=sh...  10.1 us
    pallas_call x1, Pallas kernels, project_latent(): pl.pallas_call(project_body, in_specs=[pl.BlockSpec(memory_space=pltpu.SM...  7.32 us
    add x4, local copies, waits for them, and re-layouts, modulate(): result = normed * (1.0 + scale[:, None, :]) + shift[:, None, :]  3.92 us
  transfers between devices with their start and end apart: 43, of which 18 were waited for; matrix products, arithmetic and copies ran while one was open for 13% of the time, Pallas kernels for 5%

profile of v5, /device:TPU:0, one launch (start us, length us, event | category | flops | bytes accessed | tf_op | source)
XLA Modules:
  0.0 181.9 jit_solution(11521917380719598630)
XLA Ops:
  0.0 5.7 %collective-permute-start.3 = (bf16[64,2560]{1,0:T(8,128)(2,1)}, bf16[64,2560]{1,0:T(8,128)(2,1)}, u32[]{:S(2)}, u32[]{:S(2)}) collective-permute-start(bf16[64,2560]{1,0:T(8,128)(2,1)} %param.11), channel_id=1, source_target_pairs={{0,2},{1,3},{2,4},{3,5},{4,6},{5,7},{6,8},{7,9},{8,10},{9,11},{10,... | collective-permute-start | bytes 983048 | tf_op jit(solution)/shard_map/ppermute | solution.py:51
  5.7 0.9 constant_dynamic-slice_fusion.4
  7.2 1.2 constant_dynamic-slice_fusion.8
  8.4 0.7 pad_maximum_fusion.4
  9.3 0.7 pad_maximum_fusion.5
  9.9 0.9 collective-permute-start.30
  10.8 1.5 collective-permute-start.31
  12.7 5.0 %collective-permute-done.30 = bf16[160,512]{1,0:T(8,128)(2,1)S(1)} collective-permute-done((bf16[160,512]{1,0:T(8,128)(2,1)}, bf16[160,512]{1,0:T(8,128)(2,1)S(1)}, u32[]{:S(2)}, u32[]{:S(2)}) %collective-permute-start.30) | collective-permute-done | bytes 163872 | tf_op jit(solution)/shard_map/ppermute | solution.py:51
  17.7 2.1 %collective-permute-start.33 = (bf16[80,512]{1,0:T(8,128)(2,1)S(1)}, bf16[80,512]{1,0:T(8,128)(2,1)S(1)}, u32[]{:S(2)}, u32[]{:S(2)}) collective-permute-start(bf16[80,512]{1,0:T(8,128)(2,1)S(1)} %slice.120), channel_id=1, source_target_pairs={{0,2},{1,3},{2,0},{3,1},{4,6},{5,7},{6,4},{7,5},{8,10},{9,11},{10,... | collective-permute-start | bytes 245768 | tf_op jit(solution)/shard_map/ppermute | solution.py:51
  19.9 2.2 %collective-permute-done.32 = bf16[80,512]{1,0:T(8,128)(2,1)S(1)} collective-permute-done((bf16[80,512]{1,0:T(8,128)(2,1)S(1)}, bf16[80,512]{1,0:T(8,128)(2,1)S(1)}, u32[]{:S(2)}, u32[]{:S(2)}) %collective-permute-start.32) | collective-permute-done | bytes 81952 | tf_op jit(solution)/shard_map/ppermute | solution.py:51
  22.2 1.5 collective-permute-start.36
  23.7 5.0 %collective-permute-start.34 = (bf16[640,512]{1,0:T(8,128)(2,1)S(1)}, bf16[640,512]{1,0:T(8,128)(2,1)}, u32[]{:S(2)}, u32[]{:S(2)}) collective-permute-start(bf16[640,512]{1,0:T(8,128)(2,1)S(1)} %bitcast.66), channel_id=1, source_target_pairs={{0,8},{1,9},{2,10},{3,11},{4,12},{5,13},{6,14},{7,15},{8,0},{9,1},... | collective-permute-start | bytes 1966088 | tf_op jit(solution)/shard_map/ppermute | solution.py:51
  28.7 1.1 broadcast_select_fusion.4
  29.9 0.9 pad_maximum_fusion.2.refs_0_
  32.5 0.8 pad_maximum_fusion.6.refs_5_
  34.0 1.0 broadcast_select_fusion.5
  35.0 0.7 collective-permute-start.26
  37.0 1.5 mul.216
  38.5 1.2 add.252
  39.7 2.7 %add.253 = f32[128,4,640]{2,1,0:T(4,128)} reshape(f32[2,64,2560]{2,1,0:T(8,128)} %add.252) | data formatting | bytes 2621440 | tf_op jit(solution)/shard_map/add | solution.py:45
  42.7 1.1 broadcast_select_fusion.9
  44.5 0.7 collective-permute-start.6
  45.2 1.0 broadcast_select_fusion.7
  46.9 12.3 %collective-permute-done.7.refs_0_ = bf16[160,2048]{1,0:T(8,128)(2,1)S(1)} collective-permute-done((bf16[160,2048]{1,0:T(8,128)(2,1)}, bf16[160,2048]{1,0:T(8,128)(2,1)S(1)}, u32[]{:S(2)}, u32[]{:S(2)}) %collective-permute-start.7) | collective-permute-done | bytes 655392 | tf_op jit(solution)/shard_map/ppermute | solution.py:51
  59.2 0.7 collective-permute-start.8
  59.9 1.3 collective-permute-start.9
  62.0 1.5 collective-permute-start.22
  63.5 1.4 collective-permute-start.21
  64.9 1.0 copy_bitcast_fusion
  66.0 1.4 collective-permute-start.37
  67.4 13.7 %collective-permute-done.9 = bf16[160,2048]{1,0:T(8,128)(2,1)S(1)} collective-permute-done((bf16[160,2048]{1,0:T(8,128)(2,1)S(1)}, bf16[160,2048]{1,0:T(8,128)(2,1)S(1)}, u32[]{:S(2)}, u32[]{:S(2)}) %collective-permute-start.9) | collective-permute-done | bytes 655392 | tf_op jit(solution)/shard_map/ppermute | solution.py:51
  81.1 0.7 collective-permute-start.35
  81.9 1.5 collective-permute-start.18
  83.4 0.6 collective-permute-start.17
  84.0 9.3 %collective-permute-done.21.refs_1_ = bf16[160,2048]{1,0:T(8,128)(2,1)S(1)} collective-permute-done((bf16[160,2048]{1,0:T(8,128)(2,1)S(1)}, bf16[160,2048]{1,0:T(8,128)(2,1)S(1)}, u32[]{:S(2)}, u32[]{:S(2)}) %collective-permute-start.21) | collective-permute-done | bytes 655392 | tf_op jit(solution)/shard_map/ppermute | solution.py:51
  93.3 1.3 collective-permute-start.10
  95.3 1.0 slice.118
  97.0 1.5 collective-permute-start.27
  98.6 1.5 collective-permute-start.38
  100.1 7.3 %collective-permute-done.17.refs_1_ = bf16[160,2048]{1,0:T(8,128)(2,1)S(1)} collective-permute-done((bf16[160,2048]{1,0:T(8,128)(2,1)S(1)}, bf16[160,2048]{1,0:T(8,128)(2,1)S(1)}, u32[]{:S(2)}, u32[]{:S(2)}) %collective-permute-start.17) | collective-permute-done | bytes 655392 | tf_op jit(solution)/shard_map/ppermute | solution.py:51
  107.9 8.5 %collective-permute-done.10 = bf16[160,2048]{1,0:T(8,128)(2,1)S(1)} collective-permute-done((bf16[160,2048]{1,0:T(8,128)(2,1)S(1)}, bf16[160,2048]{1,0:T(8,128)(2,1)S(1)}, u32[]{:S(2)}, u32[]{:S(2)}) %collective-permute-start.10) | collective-permute-done | bytes 655392 | tf_op jit(solution)/shard_map/ppermute | solution.py:51
  116.5 1.4 collective-permute-start.23
  118.0 0.7 collective-permute-start.20
  119.2 2.2 %collective-permute-done.24.refs_4_ = bf16[80,2048]{1,0:T(8,128)(2,1)S(1)} collective-permute-done((bf16[80,2048]{1,0:T(8,128)(2,1)S(1)}, bf16[80,2048]{1,0:T(8,128)(2,1)S(1)}, u32[]{:S(2)}, u32[]{:S(2)}) %collective-permute-start.24) | collective-permute-done | bytes 327712 | tf_op jit(solution)/shard_map/ppermute | solution.py:51
  121.4 1.4 collective-permute-start.14
  122.8 4.2 %collective-permute-done.23.refs_3_ = bf16[80,2048]{1,0:T(8,128)(2,1)S(1)} collective-permute-done((bf16[80,2048]{1,0:T(8,128)(2,1)S(1)}, bf16[80,2048]{1,0:T(8,128)(2,1)S(1)}, u32[]{:S(2)}, u32[]{:S(2)}) %collective-permute-start.23) | collective-permute-done | bytes 327712 | tf_op jit(solution)/shard_map/ppermute | solution.py:51
  128.7 1.1 collective-permute-start.12
  129.7 4.2 %collective-permute-done.19.refs_3_ = bf16[80,2048]{1,0:T(8,128)(2,1)S(1)} collective-permute-done((bf16[80,2048]{1,0:T(8,128)(2,1)S(1)}, bf16[80,2048]{1,0:T(8,128)(2,1)S(1)}, u32[]{:S(2)}, u32[]{:S(2)}) %collective-permute-start.19) | collective-permute-done | bytes 327712 | tf_op jit(solution)/shard_map/ppermute | solution.py:51
  134.0 1.1 collective-permute-start.13
  135.0 6.0 %collective-permute-done.14.refs_4_ = bf16[80,2048]{1,0:T(8,128)(2,1)S(1)} collective-permute-done((bf16[80,2048]{1,0:T(8,128)(2,1)S(1)}, bf16[80,2048]{1,0:T(8,128)(2,1)S(1)}, u32[]{:S(2)}, u32[]{:S(2)}) %collective-permute-start.14) | collective-permute-done | bytes 327712 | tf_op jit(solution)/shard_map/ppermute | solution.py:51
  141.0 1.1 collective-permute-start.15
  142.2 3.4 %absorb.4 = (bf16[4,160,2048]{2,1,0:T(8,128)(2,1)}, f32[128,2048]{1,0:T(8,128)S(1)}, f32[192,1024]{1,0:T(8,128)S(1)}) custom-call(s32[6]{0:T(128)S(1)} %stack.27.places_ref, bf16[4,320,640]{2,1,0:T(8,128)(2,1)S(1)} %maximum_bitcast_fusion.hidden_ref, bf16[160,2048]{1,0:T(8,128)(2,1)} %pad_maximum_fusion.2.refs_0_, ...), custom_call_target="tpu_custom_call" | custom-call | tf_op jit(solution)/shard_map/absorb/pallas_call | solution.py:264
  145.6 2.9 %absorb.5 = (bf16[4,160,2048]{2,1,0:T(8,128)(2,1)}, f32[128,2048]{1,0:T(8,128)S(1)}, f32[192,1024]{1,0:T(8,128)S(1)}) custom-call(s32[6]{0:T(128)S(1)} %stack.27.places_ref, bf16[4,320,640]{2,1,0:T(8,128)(2,1)S(1)} %maximum_bitcast_fusion.hidden_ref, bf16[160,2048]{1,0:T(8,128)(2,1)S(1)} %collective-permute-done.7.refs_0_, ...), custom_call_target="tpu_custom_call" | custom-call | tf_op jit(solution)/shard_map/absorb/pallas_call | solution.py:264
  148.6 3.0 %absorb.6 = (bf16[4,160,2048]{2,1,0:T(8,128)(2,1)}, f32[128,2048]{1,0:T(8,128)S(1)}, f32[192,1024]{1,0:T(8,128)S(1)}) custom-call(s32[6]{0:T(128)S(1)} %stack.27.places_ref, bf16[4,320,640]{2,1,0:T(8,128)(2,1)S(1)} %maximum_bitcast_fusion.hidden_ref, bf16[160,2048]{1,0:T(8,128)(2,1)S(1)} %broadcast_select_fusion.2.refs_0_, ...), custom_call_target="tpu_custom_call" | custom-call | tf_op jit(solution)/shard_map/absorb/pallas_call | solution.py:264
  151.6 4.9 %absorb.7 = (bf16[4,160,2048]{2,1,0:T(8,128)(2,1)}, f32[128,2560]{1,0:T(8,128)S(1)}, f32[192,1280]{1,0:T(8,128)S(1)}, f32[448,128]{1,0:T(8,128)S(1)}) custom-call(s32[6]{0:T(128)S(1)} %stack.27.places_ref, bf16[4,320,640]{2,1,0:T(8,128)(2,1)S(1)} %maximum_bitcast_fusion.hidden_ref, bf16[160,2048]{1,0:T(8,128)(2,1)S(1)} %broadcast_select_fusion.1.refs_0_, ...), custom_call_target="tpu_custom_call" | custom-call | tf_op jit(solution)/shard_map/absorb/pallas_call | solution.py:264
  156.7 1.4 collective-permute-done.39.refs_2_
  158.2 4.6 %attend.2 = (bf16[128,1280]{1,0:T(8,128)(2,1)S(1)}, bf16[192,1280]{1,0:T(8,128)(2,1)}) custom-call(f32[128,2560]{1,0:T(8,128)S(1)} %get-tuple-element.40.refs_0_, f32[448,128]{1,0:T(8,128)S(1)} %get-tuple-element.41.refs_1_, f32[448,128]{1,0:T(8,128)S(1)} %collective-permute-done.39.refs_2_, f32[1,1280]{1,0:T(1,128)S(1)} %broadcast_in_dim.19.refs_3_, ...), custom_call_target="tpu_custom_call" | custom-call | tf_op jit(solution)/shard_map/attend/pallas_call | solution.py:336
  162.9 1.5 collective-permute-done.40.other_ref
  164.4 7.3 %project.1 = (f32[128,2560]{1,0:T(8,128)}, f32[256,128]{1,0:T(8,128)}, bf16[128,1280]{1,0:T(8,128)(2,1)}) custom-call(s32[6]{0:T(128)S(1)} %stack.27.places_ref, bf16[128,1280]{1,0:T(8,128)(2,1)S(1)} %get-tuple-element.44.own_ref.refs_10_, bf16[128,1280]{1,0:T(8,128)(2,1)S(1)} %collective-permute-done.40.other_ref, f32[5,7680]{1,0:T(8,128)S(1)} %fusion.16.mod_ref, ...), custom_call_target="tpu_custom_call" | custom-call | tf_op jit(solution)/shard_map/project/pallas_call | solution.py:421
  172.0 1.3 collective-permute-done.41.refs_2_
  173.4 0.6 copy-done.14
  174.0 5.5 %attend.3 = bf16[128,1280]{1,0:T(8,128)(2,1)S(1)} custom-call(f32[128,2560]{1,0:T(8,128)} %get-tuple-element.49.refs_0_, f32[256,128]{1,0:T(8,128)} %get-tuple-element.50.refs_1_, f32[256,128]{1,0:T(8,128)} %copy-done.14, f32[1,1280]{1,0:T(1,128)S(1)} %broadcast_in_dim.19.refs_3_, f32[1,1280]{1,0:T(1,128)S(1)} %broadcast_in_dim.20.refs_4_, ...), custom_call_target="tpu_custom_call" | custom-call | tf_op jit(solution)/shard_map/attend/pallas_call | solution.py:336
  179.8 1.2 collective-permute-done.42
  181.0 0.9 fusion.7
  (156 shorter events, 12.5 us)
Async XLA Ops:
  0.0 36.1 %copy-start = (bf16[128,7680]{1,0:T(8,128)(2,1)S(1)}, bf16[128,7680]{1,0:T(8,128)(2,1)}, u32[]{:S(2)}) copy-start(bf16[128,7680]{1,0:T(8,128)(2,1)} %param.17) | copy-start | bytes 5898244
  0.0 12.3 %copy-start.15 = (f32[2560]{0:T(1024)S(1)}, f32[2560]{0:T(1024)}, u32[]{:S(2)}) copy-start(f32[2560]{0:T(1024)} %param.18) | copy-start | bytes 30724
  0.0 12.4 %copy-start.16 = (f32[2560]{0:T(1024)S(1)}, f32[2560]{0:T(1024)}, u32[]{:S(2)}) copy-start(f32[2560]{0:T(1024)} %param.19) | copy-start | bytes 30724
  0.0 42.5 %collective-permute-start.3 = (bf16[64,2560]{1,0:T(8,128)(2,1)}, bf16[64,2560]{1,0:T(8,128)(2,1)}, u32[]{:S(2)}, u32[]{:S(2)}) collective-permute-start(bf16[64,2560]{1,0:T(8,128)(2,1)} %param.11), channel_id=1, source_target_pairs={{0,2},{1,3},{2,4},{3,5},{4,6},{5,7},{6,8},{7,9},{8,10},{9,11},{10,... | collective-permute-start | bytes 983048 | tf_op jit(solution)/shard_map/ppermute | solution.py:51
  5.7 27.6 %collective-permute-start.5 = (bf16[64,2560]{1,0:T(8,128)(2,1)}, bf16[64,2560]{1,0:T(8,128)(2,1)}, u32[]{:S(2)}, u32[]{:S(2)}) collective-permute-start(bf16[64,2560]{1,0:T(8,128)(2,1)} %param.11), channel_id=1, source_target_pairs={{0,1},{1,0},{2,3},{3,2},{4,5},{5,4},{6,7},{7,6},{8,9},{9,8},{10,11... | collective-permute-start | bytes 983048 | tf_op jit(solution)/shard_map/ppermute | solution.py:51
  6.6 2.6 %collective-permute-start.29 = (bf16[80,512]{1,0:T(8,128)(2,1)S(1)}, bf16[80,512]{1,0:T(8,128)(2,1)S(1)}, u32[]{:S(2)}, u32[]{:S(2)}) collective-permute-start(bf16[80,512]{1,0:T(8,128)(2,1)S(1)} %pad_maximum_fusion.9), channel_id=1, source_target_pairs={{0,1},{1,0},{2,3},{3,2},{4,5},{5,4},{6,7},{7,6},{8,9},{9,8},{10,11... | collective-permute-start | bytes 245768 | tf_op jit(solution)/shard_map/ppermute | solution.py:51
  9.1 19.6 %collective-permute-start = (bf16[80,2048]{1,0:T(8,128)(2,1)}, bf16[80,2048]{1,0:T(8,128)(2,1)}, u32[]{:S(2)}, u32[]{:S(2)}) collective-permute-start(bf16[80,2048]{1,0:T(8,128)(2,1)} %pad_maximum_fusion.4), channel_id=1, source_target_pairs={{0,1},{1,0},{2,3},{3,2},{4,5},{5,4},{6,7},{7,6},{8,9},{9,8},{10,11... | collective-permute-start | bytes 983048 | tf_op jit(solution)/shard_map/ppermute | solution.py:51
  9.9 7.7 %collective-permute-start.30 = (bf16[160,512]{1,0:T(8,128)(2,1)}, bf16[160,512]{1,0:T(8,128)(2,1)S(1)}, u32[]{:S(2)}, u32[]{:S(2)}) collective-permute-start(bf16[160,512]{1,0:T(8,128)(2,1)} %pad_maximum_fusion.5), channel_id=1, source_target_pairs={{0,2},{1,3},{2,0},{3,1},{4,6},{5,7},{6,4},{7,5},{8,10},{9,11},{10,... | collective-permute-start | bytes 491528 | tf_op jit(solution)/shard_map/ppermute | solution.py:51
  10.8 6.9 %collective-permute-start.31 = (bf16[160,512]{1,0:T(8,128)(2,1)}, bf16[160,512]{1,0:T(8,128)(2,1)S(1)}, u32[]{:S(2)}, u32[]{:S(2)}) collective-permute-start(bf16[160,512]{1,0:T(8,128)(2,1)} %pad_maximum_fusion.5), channel_id=1, source_target_pairs={{0,4},{1,5},{2,6},{3,7},{4,0},{5,1},{6,2},{7,3},{8,12},{9,13},{10,... | collective-permute-start | bytes 491528 | tf_op jit(solution)/shard_map/ppermute | solution.py:51
  12.7 18.1 %copy-start.7 = (s32[32]{0:T(128)S(1)}, s32[32]{0:T(128)}, u32[]{:S(2)}) copy-start(s32[32]{0:T(128)} %param.12) | copy-start | bytes 388
  17.7 4.4 %collective-permute-start.32 = (bf16[80,512]{1,0:T(8,128)(2,1)S(1)}, bf16[80,512]{1,0:T(8,128)(2,1)S(1)}, u32[]{:S(2)}, u32[]{:S(2)}) collective-permute-start(bf16[80,512]{1,0:T(8,128)(2,1)S(1)} %slice.119), channel_id=1, source_target_pairs={{0,4},{1,5},{2,6},{3,7},{4,0},{5,1},{6,2},{7,3},{8,12},{9,13},{10,... | collective-permute-start | bytes 245768 | tf_op jit(solution)/shard_map/ppermute | solution.py:51
  17.7 4.5 %collective-permute-start.33 = (bf16[80,512]{1,0:T(8,128)(2,1)S(1)}, bf16[80,512]{1,0:T(8,128)(2,1)S(1)}, u32[]{:S(2)}, u32[]{:S(2)}) collective-permute-start(bf16[80,512]{1,0:T(8,128)(2,1)S(1)} %slice.120), channel_id=1, source_target_pairs={{0,2},{1,3},{2,0},{3,1},{4,6},{5,7},{6,4},{7,5},{8,10},{9,11},{10,... | collective-permute-start | bytes 245768 | tf_op jit(solution)/shard_map/ppermute | solution.py:51
  19.8 11.8 %copy-start.17 = (s32[1,2]{1,0:T(1,128)S(1)}, s32[1,2]{1,0:T(1,128)}, u32[]{:S(2)}) copy-start(s32[1,2]{1,0:T(1,128)} %param.13) | copy-start | bytes 28
  19.8 11.8 %copy-start.18 = (s32[1,2]{1,0:T(1,128)S(1)}, s32[1,2]{1,0:T(1,128)}, u32[]{:S(2)}) copy-start(s32[1,2]{1,0:T(1,128)} %param.14) | copy-start | bytes 28
  22.2 129.4 %copy-start.3 = (bf16[4,160,512]{2,1,0:T(8,128)(2,1)}, bf16[4,160,512]{2,1,0:T(8,128)(2,1)S(1)}, u32[]{:S(2)}) copy-start(bf16[4,160,512]{2,1,0:T(8,128)(2,1)S(1)} %fusion.9) | copy-start | bytes 1966084
  22.2 39.2 %collective-permute-start.36 = (bf16[640,512]{1,0:T(8,128)(2,1)S(1)}, bf16[640,512]{1,0:T(8,128)(2,1)}, u32[]{:S(2)}, u32[]{:S(2)}) collective-permute-start(bf16[640,512]{1,0:T(8,128)(2,1)S(1)} %bitcast.65), channel_id=1, source_target_pairs={{8,16},{9,17},{10,18},{11,19},{12,20},{13,21},{14,22},{15,23},{16,... | collective-permute-start | bytes 1966088 | tf_op jit(solution)/shard_map/ppermute | solution.py:51
  23.7 38.3 %collective-permute-start.34 = (bf16[640,512]{1,0:T(8,128)(2,1)S(1)}, bf16[640,512]{1,0:T(8,128)(2,1)}, u32[]{:S(2)}, u32[]{:S(2)}) collective-permute-start(bf16[640,512]{1,0:T(8,128)(2,1)S(1)} %bitcast.66), channel_id=1, source_target_pairs={{0,8},{1,9},{2,10},{3,11},{4,12},{5,13},{6,14},{7,15},{8,0},{9,1},... | collective-permute-start | bytes 1966088 | tf_op jit(solution)/shard_map/ppermute | solution.py:51
  32.0 3.0 %collective-permute-start.2 = (s32[1,4]{0,1:T(4,128)S(1)}, s32[1,4]{0,1:T(4,128)S(1)}, u32[]{:S(2)}, u32[]{:S(2)}) collective-permute-start(s32[1,4]{0,1:T(4,128)S(1)} %copy.40), channel_id=1, source_target_pairs={{0,1},{1,0},{2,3},{3,2},{4,5},{5,4},{6,7},{7,6},{8,9},{9,8},{10,11... | collective-permute-start | bytes 56 | tf_op jit(solution)/shard_map/ppermute | solution.py:51
  33.4 9.2 %collective-permute-start.1 = (bf16[64,2560]{1,0:T(8,128)(2,1)}, bf16[64,2560]{1,0:T(8,128)(2,1)}, u32[]{:S(2)}, u32[]{:S(2)}) collective-permute-start(bf16[64,2560]{1,0:T(8,128)(2,1)} %param.10), channel_id=1, source_target_pairs={{0,1},{1,0},{2,3},{3,2},{4,5},{5,4},{6,7},{7,6},{8,9},{9,8},{10,11... | collective-permute-start | bytes 983048 | tf_op jit(solution)/shard_map/ppermute | solution.py:51
  35.0 11.5 %copy-start.11 = (bf16[64,2560]{1,0:T(8,128)(2,1)}, bf16[64,2560]{1,0:T(8,128)(2,1)S(1)}, u32[]{:S(2)}) copy-start(bf16[64,2560]{1,0:T(8,128)(2,1)S(1)} %broadcast_select_fusion.5) | copy-start | bytes 983044
  35.0 28.5 %collective-permute-start.26 = (bf16[160,2048]{1,0:T(8,128)(2,1)}, bf16[160,2048]{1,0:T(8,128)(2,1)}, u32[]{:S(2)}, u32[]{:S(2)}) collective-permute-start(bf16[160,2048]{1,0:T(8,128)(2,1)} %pad_maximum_fusion.2.refs_0_), channel_id=1, source_target_pairs={{0,4},{1,5},{2,6},{3,7},{4,0},{5,1},{6,2},{7,3},{8,12},{9,13},{10,... | collective-permute-start | bytes 1966088 | tf_op jit(solution)/shard_map/ppermute | solution.py:51
  37.0 2.8 %copy-start.8 = (f32[2,64,2560]{2,1,0:T(8,128)}, f32[2,64,2560]{2,1,0:T(8,128)S(1)}, u32[]{:S(2)}) copy-start(f32[2,64,2560]{2,1,0:T(8,128)S(1)} %mul.215) | copy-start | bytes 3932164
  42.5 16.7 %collective-permute-start.7 = (bf16[160,2048]{1,0:T(8,128)(2,1)}, bf16[160,2048]{1,0:T(8,128)(2,1)S(1)}, u32[]{:S(2)}, u32[]{:S(2)}) collective-permute-start(bf16[160,2048]{1,0:T(8,128)(2,1)} %pad_maximum_fusion.2.refs_0_), channel_id=1, source_target_pairs={{0,8},{1,9},{2,10},{3,11},{4,12},{5,13},{6,14},{7,15},{8,0},{9,1},... | collective-permute-start | bytes 1966088 | tf_op jit(solution)/shard_map/ppermute | solution.py:51
  42.6 1.9 %collective-permute-start.4 = (bf16[64,2560]{1,0:T(8,128)(2,1)}, bf16[64,2560]{1,0:T(8,128)(2,1)S(1)}, u32[]{:S(2)}, u32[]{:S(2)}) collective-permute-start(bf16[64,2560]{1,0:T(8,128)(2,1)} %collective-permute-done.3), channel_id=1, source_target_pairs={{0,1},{1,0},{2,3},{3,2},{4,5},{5,4},{6,7},{7,6},{8,9},{9,8},{10,11... | collective-permute-start | bytes 983048 | tf_op jit(solution)/shard_map/ppermute | solution.py:51
  44.5 15.4 %collective-permute-start.6 = (bf16[160,2048]{1,0:T(8,128)(2,1)}, bf16[160,2048]{1,0:T(8,128)(2,1)S(1)}, u32[]{:S(2)}, u32[]{:S(2)}) collective-permute-start(bf16[160,2048]{1,0:T(8,128)(2,1)} %pad_maximum_fusion.2.refs_0_), channel_id=1, source_target_pairs={{8,16},{9,17},{10,18},{11,19},{12,20},{13,21},{14,22},{15,23},{16,... | collective-permute-start | bytes 1966088 | tf_op jit(solution)/shard_map/ppermute | solution.py:51
  59.2 6.8 %collective-permute-start.8 = (bf16[160,2048]{1,0:T(8,128)(2,1)S(1)}, bf16[160,2048]{1,0:T(8,128)(2,1)S(1)}, u32[]{:S(2)}, u32[]{:S(2)}) collective-permute-start(bf16[160,2048]{1,0:T(8,128)(2,1)S(1)} %collective-permute-done.7.refs_0_), channel_id=1, source_target_pairs={{8,16},{9,17},{10,18},{11,19},{12,20},{13,21},{14,22},{15,23},{16,... | collective-permute-start | bytes 1966088 | tf_op jit(solution)/shard_map/ppermute | solution.py:51
  59.9 21.2 %collective-permute-start.9 = (bf16[160,2048]{1,0:T(8,128)(2,1)S(1)}, bf16[160,2048]{1,0:T(8,128)(2,1)S(1)}, u32[]{:S(2)}, u32[]{:S(2)}) collective-permute-start(bf16[160,2048]{1,0:T(8,128)(2,1)S(1)} %collective-permute-done.6), channel_id=1, source_target_pairs={{8,0},{9,1},{10,2},{11,3},{12,4},{13,5},{14,6},{15,7},{16,24},{17,... | collective-permute-start | bytes 1966088 | tf_op jit(solution)/shard_map/ppermute | solution.py:51
  61.4 20.5 %collective-permute-start.25 = (bf16[160,2048]{1,0:T(8,128)(2,1)}, bf16[160,2048]{1,0:T(8,128)(2,1)S(1)}, u32[]{:S(2)}, u32[]{:S(2)}) collective-permute-start(bf16[160,2048]{1,0:T(8,128)(2,1)} %pad_maximum_fusion.2.refs_0_), channel_id=1, source_target_pairs={{0,2},{1,3},{2,0},{3,1},{4,6},{5,7},{6,4},{7,5},{8,10},{9,11},{10,... | collective-permute-start | bytes 1966088 | tf_op jit(solution)/shard_map/ppermute | solution.py:51
  62.0 21.4 %collective-permute-start.22 = (bf16[160,2048]{1,0:T(8,128)(2,1)S(1)}, bf16[160,2048]{1,0:T(8,128)(2,1)S(1)}, u32[]{:S(2)}, u32[]{:S(2)}) collective-permute-start(bf16[160,2048]{1,0:T(8,128)(2,1)S(1)} %collective-permute-done.7.refs_0_), channel_id=1, source_target_pairs={{0,4},{1,5},{2,6},{3,7},{4,0},{5,1},{6,2},{7,3},{8,12},{9,13},{10,... | collective-permute-start | bytes 1966088 | tf_op jit(solution)/shard_map/ppermute | solution.py:51
  63.5 29.8 %collective-permute-start.21 = (bf16[160,2048]{1,0:T(8,128)(2,1)S(1)}, bf16[160,2048]{1,0:T(8,128)(2,1)S(1)}, u32[]{:S(2)}, u32[]{:S(2)}) collective-permute-start(bf16[160,2048]{1,0:T(8,128)(2,1)S(1)} %collective-permute-done.7.refs_0_), channel_id=1, source_target_pairs={{0,2},{1,3},{2,0},{3,1},{4,6},{5,7},{6,4},{7,5},{8,10},{9,11},{10,... | collective-permute-start | bytes 1966088 | tf_op jit(solution)/shard_map/ppermute | solution.py:51
  65.9 28.8 %copy-start.12 = (f32[128,4,640]{2,1,0:T(4,128)S(1)}, f32[128,4,640]{2,1,0:T(4,128)}, u32[]{:S(2)}) copy-start(f32[128,4,640]{2,1,0:T(4,128)} %mul.216) | copy-start | bytes 3932164
  66.0 28.8 %copy-start.13 = (f32[128,4,640]{2,1,0:T(4,128)S(1)}, f32[128,4,640]{2,1,0:T(4,128)}, u32[]{:S(2)}) copy-start(f32[128,4,640]{2,1,0:T(4,128)} %add.253) | copy-start | bytes 3932164
  66.0 30.4 %collective-permute-start.37 = (bf16[640,512]{1,0:T(8,128)(2,1)}, bf16[640,512]{1,0:T(8,128)(2,1)S(1)}, u32[]{:S(2)}, u32[]{:S(2)}) collective-permute-start(bf16[640,512]{1,0:T(8,128)(2,1)} %collective-permute-done.36.refs_12_.refs_7_), channel_id=1, source_target_pairs={{8,0},{9,1},{10,2},{11,3},{12,4},{13,5},{14,6},{15,7},{16,24},{17,... | collective-permute-start | bytes 1966088 | tf_op jit(solution)/shard_map/ppermute | solution.py:51
  81.1 15.9 %collective-permute-start.35 = (bf16[640,512]{1,0:T(8,128)(2,1)}, bf16[640,512]{1,0:T(8,128)(2,1)S(1)}, u32[]{:S(2)}, u32[]{:S(2)}) collective-permute-start(bf16[640,512]{1,0:T(8,128)(2,1)} %collective-permute-done.34.refs_10_.refs_5_), channel_id=1, source_target_pairs={{8,16},{9,17},{10,18},{11,19},{12,20},{13,21},{14,22},{15,23},{16,... | collective-permute-start | bytes 1966088 | tf_op jit(solution)/shard_map/ppermute | solution.py:51
  81.9 16.7 %collective-permute-start.18 = (bf16[160,2048]{1,0:T(8,128)(2,1)S(1)}, bf16[160,2048]{1,0:T(8,128)(2,1)S(1)}, u32[]{:S(2)}, u32[]{:S(2)}) collective-permute-start(bf16[160,2048]{1,0:T(8,128)(2,1)S(1)} %broadcast_select_fusion.2.refs_0_), channel_id=1, source_target_pairs={{0,4},{1,5},{2,6},{3,7},{4,0},{5,1},{6,2},{7,3},{8,12},{9,13},{10,... | collective-permute-start | bytes 1966088 | tf_op jit(solution)/shard_map/ppermute | solution.py:51
  83.4 24.0 %collective-permute-start.17 = (bf16[160,2048]{1,0:T(8,128)(2,1)S(1)}, bf16[160,2048]{1,0:T(8,128)(2,1)S(1)}, u32[]{:S(2)}, u32[]{:S(2)}) collective-permute-start(bf16[160,2048]{1,0:T(8,128)(2,1)S(1)} %broadcast_select_fusion.2.refs_0_), channel_id=1, source_target_pairs={{0,2},{1,3},{2,0},{3,1},{4,6},{5,7},{6,4},{7,5},{8,10},{9,11},{10,... | collective-permute-start | bytes 1966088 | tf_op jit(solution)/shard_map/ppermute | solution.py:51
  93.3 23.1 %collective-permute-start.10 = (bf16[160,2048]{1,0:T(8,128)(2,1)S(1)}, bf16[160,2048]{1,0:T(8,128)(2,1)S(1)}, u32[]{:S(2)}, u32[]{:S(2)}) collective-permute-start(bf16[160,2048]{1,0:T(8,128)(2,1)S(1)} %broadcast_select_fusion.2.refs_0_), channel_id=1, source_target_pairs={{8,0},{9,1},{10,2},{11,3},{12,4},{13,5},{14,6},{15,7},{16,24},{17,... | collective-permute-start | bytes 1966088 | tf_op jit(solution)/shard_map/ppermute | solution.py:51
  96.4 21.6 %collective-permute-start.28 = (bf16[80,2048]{1,0:T(8,128)(2,1)S(1)}, bf16[80,2048]{1,0:T(8,128)(2,1)S(1)}, u32[]{:S(2)}, u32[]{:S(2)}) collective-permute-start(bf16[80,2048]{1,0:T(8,128)(2,1)S(1)} %slice.118), channel_id=1, source_target_pairs={{0,2},{1,3},{2,0},{3,1},{4,6},{5,7},{6,4},{7,5},{8,10},{9,11},{10,... | collective-permute-start | bytes 983048 | tf_op jit(solution)/shard_map/ppermute | solution.py:51
  97.0 21.7 %collective-permute-start.27 = (bf16[80,2048]{1,0:T(8,128)(2,1)S(1)}, bf16[80,2048]{1,0:T(8,128)(2,1)S(1)}, u32[]{:S(2)}, u32[]{:S(2)}) collective-permute-start(bf16[80,2048]{1,0:T(8,128)(2,1)S(1)} %slice.117), channel_id=1, source_target_pairs={{0,4},{1,5},{2,6},{3,7},{4,0},{5,1},{6,2},{7,3},{8,12},{9,13},{10,... | collective-permute-start | bytes 983048 | tf_op jit(solution)/shard_map/ppermute | solution.py:51
  98.6 53.0 %copy-start.2 = (bf16[640,512]{1,0:T(8,128)(2,1)}, bf16[640,512]{1,0:T(8,128)(2,1)S(1)}, u32[]{:S(2)}) copy-start(bf16[640,512]{1,0:T(8,128)(2,1)S(1)} %broadcast_select_fusion.refs_11_.refs_6_) | copy-start | bytes 1966084
  98.6 52.9 %collective-permute-start.38 = (bf16[640,512]{1,0:T(8,128)(2,1)S(1)}, bf16[640,512]{1,0:T(8,128)(2,1)S(1)}, u32[]{:S(2)}, u32[]{:S(2)}) collective-permute-start(bf16[640,512]{1,0:T(8,128)(2,1)S(1)} %broadcast_select_fusion.refs_11_.refs_6_), channel_id=1, source_target_pairs={{8,0},{9,1},{10,2},{11,3},{12,4},{13,5},{14,6},{15,7},{16,24},{17,... | collective-permute-start | bytes 1966088 | tf_op jit(solution)/shard_map/ppermute | solution.py:51
  107.4 14.0 %collective-permute-start.24 = (bf16[80,2048]{1,0:T(8,128)(2,1)S(1)}, bf16[80,2048]{1,0:T(8,128)(2,1)S(1)}, u32[]{:S(2)}, u32[]{:S(2)}) collective-permute-start(bf16[80,2048]{1,0:T(8,128)(2,1)S(1)} %slice.116), channel_id=1, source_target_pairs={{0,2},{1,3},{2,0},{3,1},{4,6},{5,7},{6,4},{7,5},{8,10},{9,11},{10,... | collective-permute-start | bytes 983048 | tf_op jit(solution)/shard_map/ppermute | solution.py:51
  116.5 10.5 %collective-permute-start.23 = (bf16[80,2048]{1,0:T(8,128)(2,1)S(1)}, bf16[80,2048]{1,0:T(8,128)(2,1)S(1)}, u32[]{:S(2)}, u32[]{:S(2)}) collective-permute-start(bf16[80,2048]{1,0:T(8,128)(2,1)S(1)} %slice.115), channel_id=1, source_target_pairs={{0,4},{1,5},{2,6},{3,7},{4,0},{5,1},{6,2},{7,3},{8,12},{9,13},{10,... | collective-permute-start | bytes 983048 | tf_op jit(solution)/shard_map/ppermute | solution.py:51
  118.0 10.6 %collective-permute-start.20 = (bf16[80,2048]{1,0:T(8,128)(2,1)S(1)}, bf16[80,2048]{1,0:T(8,128)(2,1)S(1)}, u32[]{:S(2)}, u32[]{:S(2)}) collective-permute-start(bf16[80,2048]{1,0:T(8,128)(2,1)S(1)} %slice.114), channel_id=1, source_target_pairs={{0,2},{1,3},{2,0},{3,1},{4,6},{5,7},{6,4},{7,5},{8,10},{9,11},{10,... | collective-permute-start | bytes 983048 | tf_op jit(solution)/shard_map/ppermute | solution.py:51
  118.7 15.2 %collective-permute-start.19 = (bf16[80,2048]{1,0:T(8,128)(2,1)S(1)}, bf16[80,2048]{1,0:T(8,128)(2,1)S(1)}, u32[]{:S(2)}, u32[]{:S(2)}) collective-permute-start(bf16[80,2048]{1,0:T(8,128)(2,1)S(1)} %slice.113), channel_id=1, source_target_pairs={{0,4},{1,5},{2,6},{3,7},{4,0},{5,1},{6,2},{7,3},{8,12},{9,13},{10,... | collective-permute-start | bytes 983048 | tf_op jit(solution)/shard_map/ppermute | solution.py:51
  121.4 19.6 %collective-permute-start.14 = (bf16[80,2048]{1,0:T(8,128)(2,1)S(1)}, bf16[80,2048]{1,0:T(8,128)(2,1)S(1)}, u32[]{:S(2)}, u32[]{:S(2)}) collective-permute-start(bf16[80,2048]{1,0:T(8,128)(2,1)S(1)} %get-tuple-element.63), channel_id=1, source_target_pairs={{0,4},{1,5},{2,6},{3,7},{4,0},{5,1},{6,2},{7,3},{8,12},{9,13},{10,... | collective-permute-start | bytes 983048 | tf_op jit(solution)/shard_map/ppermute | solution.py:51
  127.0 14.0 %collective-permute-start.11 = (bf16[80,2048]{1,0:T(8,128)(2,1)S(1)}, bf16[80,2048]{1,0:T(8,128)(2,1)S(1)}, u32[]{:S(2)}, u32[]{:S(2)}) collective-permute-start(bf16[80,2048]{1,0:T(8,128)(2,1)S(1)} %get-tuple-element.64), channel_id=1, source_target_pairs={{0,2},{1,3},{2,0},{3,1},{4,6},{5,7},{6,4},{7,5},{8,10},{9,11},{10,... | collective-permute-start | bytes 983048 | tf_op jit(solution)/shard_map/ppermute | solution.py:51
  128.0 14.1 %copy-start.9 = (f32[2,64,2560]{2,1,0:T(8,128)S(1)}, f32[2,64,2560]{2,1,0:T(8,128)}, u32[]{:S(2)}) copy-start(f32[2,64,2560]{2,1,0:T(8,128)} %copy-done.8) | copy-start | bytes 3932164
  128.0 14.1 %copy-start.10 = (f32[2,64,2560]{2,1,0:T(8,128)S(1)}, f32[2,64,2560]{2,1,0:T(8,128)}, u32[]{:S(2)}) copy-start(f32[2,64,2560]{2,1,0:T(8,128)} %add.252) | copy-start | bytes 3932164
  128.7 22.9 %collective-permute-start.12 = (bf16[80,2048]{1,0:T(8,128)(2,1)S(1)}, bf16[80,2048]{1,0:T(8,128)(2,1)S(1)}, u32[]{:S(2)}, u32[]{:S(2)}) collective-permute-start(bf16[80,2048]{1,0:T(8,128)(2,1)S(1)} %get-tuple-element.63), channel_id=1, source_target_pairs={{0,2},{1,3},{2,0},{3,1},{4,6},{5,7},{6,4},{7,5},{8,10},{9,11},{10,... | collective-permute-start | bytes 983048 | tf_op jit(solution)/shard_map/ppermute | solution.py:51
  134.0 17.6 %collective-permute-start.13 = (bf16[80,2048]{1,0:T(8,128)(2,1)S(1)}, bf16[80,2048]{1,0:T(8,128)(2,1)S(1)}, u32[]{:S(2)}, u32[]{:S(2)}) collective-permute-start(bf16[80,2048]{1,0:T(8,128)(2,1)S(1)} %get-tuple-element.64), channel_id=1, source_target_pairs={{0,4},{1,5},{2,6},{3,7},{4,0},{5,1},{6,2},{7,3},{8,12},{9,13},{10,... | collective-permute-start | bytes 983048 | tf_op jit(solution)/shard_map/ppermute | solution.py:51
  141.0 10.6 %collective-permute-start.16 = (bf16[80,2048]{1,0:T(8,128)(2,1)S(1)}, bf16[80,2048]{1,0:T(8,128)(2,1)S(1)}, u32[]{:S(2)}, u32[]{:S(2)}) collective-permute-start(bf16[80,2048]{1,0:T(8,128)(2,1)S(1)} %collective-permute-done.14.refs_4_), channel_id=1, source_target_pairs={{0,2},{1,3},{2,0},{3,1},{4,6},{5,7},{6,4},{7,5},{8,10},{9,11},{10,... | collective-permute-start | bytes 983048 | tf_op jit(solution)/shard_map/ppermute | solution.py:51
  141.0 10.6 %collective-permute-start.15 = (bf16[80,2048]{1,0:T(8,128)(2,1)S(1)}, bf16[80,2048]{1,0:T(8,128)(2,1)S(1)}, u32[]{:S(2)}, u32[]{:S(2)}) collective-permute-start(bf16[80,2048]{1,0:T(8,128)(2,1)S(1)} %collective-permute-done.11.refs_1_), channel_id=1, source_target_pairs={{0,4},{1,5},{2,6},{3,7},{4,0},{5,1},{6,2},{7,3},{8,12},{9,13},{10,... | collective-permute-start | bytes 983048 | tf_op jit(solution)/shard_map/ppermute | solution.py:51
  151.6 5.0 %copy-start.4 = (bf16[640,512]{1,0:T(8,128)(2,1)}, bf16[640,512]{1,0:T(8,128)(2,1)S(1)}, u32[]{:S(2)}) copy-start(bf16[640,512]{1,0:T(8,128)(2,1)S(1)} %collective-permute-done.38.refs_13_.refs_8_) | copy-start | bytes 1966084
  151.6 6.5 %copy-start.5 = (f32[256,128]{1,0:T(8,128)S(1)}, f32[256,128]{1,0:T(8,128)}, u32[]{:S(2)}) copy-start(f32[256,128]{1,0:T(8,128)} %pad_maximum_fusion.6.refs_5_) | copy-start | bytes 393220
  156.6 1.6 collective-permute-start.39
  162.8 1.6 collective-permute-start.40
  164.4 9.6 %copy-start.6 = (f32[256,128]{1,0:T(8,128)S(1)}, f32[256,128]{1,0:T(8,128)}, u32[]{:S(2)}) copy-start(f32[256,128]{1,0:T(8,128)} %pad_maximum_fusion.6.refs_5_) | copy-start | bytes 393220
  171.8 1.6 collective-permute-start.41
  173.4 0.7 copy-start.14
  173.4 8.6 %copy-start.1 = (bf16[128,7680]{1,0:T(8,128)(2,1)S(1)}, bf16[128,7680]{1,0:T(8,128)(2,1)}, u32[]{:S(2)}) copy-start(bf16[128,7680]{1,0:T(8,128)(2,1)} %param.17) | copy-start | bytes 5898244
  179.6 1.5 collective-permute-start.42
